TPU v7x, 32 devices: a whole 2x2x4 slice. The times are simulated.
32 devices in a mesh: rows: 8 (over z, y), heads: 4 (over x, core).
Axes of the slice: x: 2, y: 2, z: 4, core: 2. Of those that a mesh axis runs over, the one named last changes fastest.
Arguments:
- token_ids: int32 [32, 256], P('rows'), may hold values from 0 to 50303
- lengths: int32 [32], P('rows'), may hold values from 40 to 256
- label_ids: int32 [32, 4], P('rows'), may hold values from 0 to 50303
- targets: float32 [32, 4], P('rows'), may hold values from -14 to -8
- step_count: int32 [1], replicated, may hold values from 2 to 20
- soap_owners: int32 [8], P('rows'), may hold values from 0 to 1
- soap_basis: float32 [4, 12, 64, 64], P(None, 'heads'), may hold values from -0.75 to 0.75
- table_anchor: bfloat16 [50304, 768], P(('heads', 'rows')), may hold values from -0.625 to 0.625
- table_delta: float32 [50304, 768], P(('heads', 'rows')), may hold values from -0.3125 to 0.3125
- table_first: float32 [50304, 768], P(('heads', 'rows')), may hold values from -0.00024414062 to 0.00024414062
- table_second: float32 [50304, 768], P(('heads', 'rows')), may hold values from 2.1874195e-11 to 8.749678e-11
- qkv_anchor: bfloat16 [3, 768, 768], P(None, 'rows', 'heads'), may hold values from -0.3125 to 0.3125
- qkv_delta: float32 [3, 768, 768], P(None, 'rows', 'heads'), may hold values from -0.21875 to 0.21875
- qkv_first: float32 [3, 768, 768], P(None, 'rows', 'heads'), may hold values from -0.00024414062 to 0.00024414062
- qkv_second: float32 [3, 768, 768], P(None, 'rows', 'heads'), may hold values from 2.1874195e-11 to 8.749678e-11
- out_anchor: bfloat16 [768, 768], P('heads', 'rows'), may hold values from -0.875 to 0.875
- out_delta: float32 [768, 768], P('heads', 'rows'), may hold values from -0.625 to 0.625
- out_first: float32 [768, 768], P('heads', 'rows'), may hold values from -0.00024414062 to 0.00024414062
- out_second: float32 [768, 768], P('heads', 'rows'), may hold values from 2.1874195e-11 to 8.749678e-11
- up_anchor: bfloat16 [768, 3072], P('rows', 'heads'), may hold values from -0.21875 to 0.21875
- up_delta: float32 [768, 3072], P('rows', 'heads'), may hold values from -0.15625 to 0.15625
- up_first: float32 [768, 3072], P('rows', 'heads'), may hold values from -0.00024414062 to 0.00024414062
- up_second: float32 [768, 3072], P('rows', 'heads'), may hold values from 2.1874195e-11 to 8.749678e-11
- down_anchor: bfloat16 [3072, 768], P('heads', 'rows'), may hold values from -0.21875 to 0.21875
- down_delta: float32 [3072, 768], P('heads', 'rows'), may hold values from -0.15625 to 0.15625
- down_first: float32 [3072, 768], P('heads', 'rows'), may hold values from -0.00024414062 to 0.00024414062
- down_second: float32 [3072, 768], P('heads', 'rows'), may hold values from 2.1874195e-11 to 8.749678e-11
- gain_anchor: float32 [3, 768], replicated, may hold values from 0.5 to 1.5
- gain_delta: float32 [3, 768], replicated, may hold values from -1.5 to 1.5
- gain_first: float32 [3, 768], replicated, may hold values from -0.0012207031 to 0.0012207031
- gain_second: float32 [3, 768], replicated, may hold values from 5.468549e-10 to 2.1874196e-09
- bias_anchor: float32 [3, 768], replicated, may hold values from -4 to 4
- bias_delta: float32 [3, 768], replicated, may hold values from -1.5 to 1.5
- bias_first: float32 [3, 768], replicated, may hold values from -0.0012207031 to 0.0012207031
- bias_second: float32 [3, 768], replicated, may hold values from 5.468549e-10 to 2.1874196e-09
Outputs:
- loss_value: float32 [], replicated
- new_table: float32 [50304, 768], P(('heads', 'rows'))
- new_table_first: float32 [50304, 768], P(('heads', 'rows'))
- new_table_second: float32 [50304, 768], P(('heads', 'rows'))
- new_qkv: float32 [3, 768, 768], P(None, 'rows', 'heads')
- new_qkv_first: float32 [3, 768, 768], P(None, 'rows', 'heads')
- new_qkv_second: float32 [3, 768, 768], P(None, 'rows', 'heads')
- new_out: float32 [768, 768], P('heads', 'rows')
- new_out_first: float32 [768, 768], P('heads', 'rows')
- new_out_second: float32 [768, 768], P('heads', 'rows')
- new_up: float32 [768, 3072], P('rows', 'heads')
- new_up_first: float32 [768, 3072], P('rows', 'heads')
- new_up_second: float32 [768, 3072], P('rows', 'heads')
- new_down: float32 [3072, 768], P('heads', 'rows')
- new_down_first: float32 [3072, 768], P('heads', 'rows')
- new_down_second: float32 [3072, 768], P('heads', 'rows')
- new_gain: float32 [3, 768], replicated
- new_gain_first: float32 [3, 768], replicated
- new_gain_second: float32 [3, 768], replicated
- new_bias: float32 [3, 768], replicated
- new_bias_first: float32 [3, 768], replicated
- new_bias_second: float32 [3, 768], replicated
All inputs are finite; a program needn't handle non-finite values.
Results may differ from a plain program's by a relative error of at most 0.02.
Values may be sent and summed in bfloat16 or wider, within the bound.
No kernel may reach another device: no remote copies, remote signals or barrier semaphores. Data moves between devices by JAX's collectives and lax.ppermute only.
A program may use at most 256 MiB of HBM per device.

v0:
```python
import jax
import jax.numpy as jnp
from jax import lax
from jax.sharding import PartitionSpec as P

D = 768
HDIM = 64
SEQ = 256
NLW = 4
CGIT = 8


EPS_NORM = 1e-05
BETA_ONE = 0.9
BETA_TWO = 0.999
ADAM_EPS = 1e-08
LEARN_RATE = 0.03
DECAY_RATE = 0.01
CLIP_NORM = 1.0
CG_SHIFT = 0.002
MASKED = -1e30
HALF_ROOT = 0.7071067811865476
INV_ROOT_TAU = 0.3989422804014327
HIGH = lax.Precision.HIGHEST


def shortened(array):

    def short(part):
        return part.astype(jnp.bfloat16) if part.dtype == jnp.float32 else part

    return jax.tree.map(short, array)


def merged(array, axis, combine):
    everything = jax.tree.map(lambda part: lax.all_gather(part, axis), array)
    initial = jax.tree.map(lambda part: part[0], everything)

    def lap(k, so_far):
        return combine(so_far, jax.tree.map(lambda part: part[k], everything))

    return lax.fori_loop(1, lax.axis_size(axis), lap, initial)


def product(left, right):
    return jnp.dot(left, right, preferred_element_type=jnp.float32)


def heads_einsum(form, left, right):
    return jnp.einsum(form, left, right, preferred_element_type=jnp.float32)


def gelu_slope(values):
    return (
        0.5 * (1.0 + lax.erf(values * HALF_ROOT))
        + values * jnp.exp(-0.5 * values * values) * INV_ROOT_TAU
    )


def norm_pair(values, dots, gain, bias, gain_dot, bias_dot):
    center = values - jnp.mean(values, axis=-1, keepdims=True)
    inverse = lax.rsqrt(jnp.mean(center * center, axis=-1, keepdims=True) + EPS_NORM)
    normed = center * inverse
    normed_dot = inverse * (
        dots
        - jnp.mean(dots, axis=-1, keepdims=True)
        - normed * jnp.mean(normed * dots, axis=-1, keepdims=True)
    )
    return (normed * gain + bias, normed_dot * gain + normed * gain_dot + bias_dot, normed, inverse)


def norm_backward(grad_out, normed, inverse, gain):
    scaled = grad_out * gain
    grad_in = inverse * (
        scaled
        - jnp.mean(scaled, axis=-1, keepdims=True)
        - normed * jnp.mean(scaled * normed, axis=-1, keepdims=True)
    )
    return (grad_in, jnp.sum(grad_out * normed, axis=0), jnp.sum(grad_out, axis=0))


def gather_tokens(values):
    return jax.tree.map(
        lambda part, own: part.astype(own.dtype),
        lax.all_gather(shortened(values), "heads", axis=0, tiled=True),
        values,
    )


def scatter_tokens(values):
    return jax.tree.map(
        lambda part: part.astype(jnp.float32),
        lax.psum_scatter(shortened(values), "heads", scatter_dimension=0, tiled=True),
    )


def attention_scores(queries, key_rows, live_keys):
    scores = heads_einsum("gqhd,gkhd->ghqk", queries, key_rows) * HDIM ** (-0.5)
    return jnp.where(live_keys[:, None, None, :], scores, MASKED)


def combine_stats(left_stats, right_stats):
    peak_val = jnp.maximum(left_stats[0], right_stats[0])
    left_scale = jnp.exp(left_stats[0] - peak_val)
    right_scale = jnp.exp(right_stats[0] - peak_val)
    return (
        peak_val,
        left_stats[1] * left_scale + right_stats[1] * right_scale,
        left_stats[2] * left_scale + right_stats[2] * right_scale,
        left_stats[3] + right_stats[3],
        left_stats[4] + right_stats[4],
    )


def layer_forward(
    start_x, start_dot, live_keys, weights, steps_low, gain, bias, gain_dot, bias_dot, prompts
):
    qkv_full, out_full, up_full, down_full = weights
    qkv_step, out_step, up_step, down_step = steps_low
    local_heads = qkv_full.shape[2] // HDIM
    attn_in, attn_dot_in = gather_tokens(
        (start_x.astype(jnp.bfloat16), start_dot.astype(jnp.bfloat16))
    )
    projected = heads_einsum("td,cde->cte", attn_in, qkv_full).astype(jnp.bfloat16)
    projected_dot = (
        heads_einsum("td,cde->cte", attn_dot_in, qkv_full)
        + heads_einsum("td,cde->cte", attn_in, qkv_step)
    ).astype(jnp.bfloat16)
    projected = projected.reshape(3, prompts, SEQ, local_heads, HDIM)
    projected_dot = projected_dot.reshape(3, prompts, SEQ, local_heads, HDIM)
    scores = attention_scores(projected[0], projected[1], live_keys)
    peak_val = jnp.max(scores, axis=-1, keepdims=True)
    exponent = jnp.exp(scores - peak_val)
    totals = jnp.sum(exponent, axis=-1, keepdims=True)
    probs = exponent / totals
    probs_low = probs.astype(jnp.bfloat16)
    log_total = peak_val + jnp.log(totals)
    score_dot = (
        heads_einsum("gqhd,gkhd->ghqk", projected_dot[0], projected[1])
        + heads_einsum("gqhd,gkhd->ghqk", projected[0], projected_dot[1])
    ) * HDIM ** (-0.5)
    prob_dot = (probs * (score_dot - jnp.sum(probs * score_dot, axis=-1, keepdims=True))).astype(
        jnp.bfloat16
    )
    attended = heads_einsum("ghqk,gkhd->gqhd", probs_low, projected[2]).astype(jnp.bfloat16)
    attended_dot = (
        heads_einsum("ghqk,gkhd->gqhd", prob_dot, projected[2])
        + heads_einsum("ghqk,gkhd->gqhd", probs_low, projected_dot[2])
    ).astype(jnp.bfloat16)
    attended = attended.reshape(prompts * SEQ, local_heads * HDIM)
    attended_dot = attended_dot.reshape(prompts * SEQ, local_heads * HDIM)
    attn_out, attn_dot = scatter_tokens(
        (product(attended, out_full), product(attended_dot, out_full) + product(attended, out_step))
    )
    hidden, hidden_dot, normed_one, inverse_one = norm_pair(
        start_x + attn_out, start_dot + attn_dot, gain[1], bias[1], gain_dot[1], bias_dot[1]
    )
    ffn_input, ffn_dot_in = gather_tokens(
        (hidden.astype(jnp.bfloat16), hidden_dot.astype(jnp.bfloat16))
    )
    pre_gelu = product(ffn_input, up_full)
    pre_dot = product(ffn_dot_in, up_full) + product(ffn_input, up_step)
    activated = jax.nn.gelu(pre_gelu, approximate=False).astype(jnp.bfloat16)
    act_dot = (gelu_slope(pre_gelu) * pre_dot).astype(jnp.bfloat16)
    ffn_out, ffn_dot = scatter_tokens(
        (product(activated, down_full), product(act_dot, down_full) + product(activated, down_step))
    )
    final_out, final_dot, normed_two, inverse_two = norm_pair(
        hidden + ffn_out, hidden_dot + ffn_dot, gain[2], bias[2], gain_dot[2], bias_dot[2]
    )
    saved = (
        attn_in,
        projected,
        log_total,
        attended,
        normed_one,
        inverse_one,
        ffn_input,
        pre_gelu,
        activated,
        normed_two,
        inverse_two,
    )
    return (final_out, final_dot, saved)


def layer_backward(grad_final, saved, live_keys, weights, gain, prompts):
    qkv_full, out_full, up_full, down_full = weights
    (
        attn_in,
        projected,
        log_total,
        attended,
        normed_one,
        inverse_one,
        ffn_input,
        pre_gelu,
        activated,
        normed_two,
        inverse_two,
    ) = saved
    local_heads = qkv_full.shape[2] // HDIM
    grad_two, gain_two, bias_two = norm_backward(grad_final, normed_two, inverse_two, gain[2])
    grad_ffn = gather_tokens(grad_two.astype(jnp.bfloat16))
    grad_down = heads_einsum("tf,td->fd", activated, grad_ffn)
    grad_act = heads_einsum("td,fd->tf", grad_ffn, down_full)
    grad_pre = (gelu_slope(pre_gelu) * grad_act).astype(jnp.bfloat16)
    grad_up = heads_einsum("td,tf->df", ffn_input, grad_pre)
    grad_hidden = grad_two + scatter_tokens(heads_einsum("tf,df->td", grad_pre, up_full))
    grad_one, gain_one, bias_one = norm_backward(grad_hidden, normed_one, inverse_one, gain[1])
    grad_attn = gather_tokens(grad_one.astype(jnp.bfloat16))
    grad_out = heads_einsum("te,td->ed", attended, grad_attn)
    grad_att = heads_einsum("td,ed->te", grad_attn, out_full).astype(jnp.bfloat16)
    grad_att = grad_att.reshape(prompts, SEQ, local_heads, HDIM)
    scores = attention_scores(projected[0], projected[1], live_keys)
    probs_full = jnp.exp(scores - log_total)
    grad_prob = heads_einsum("gqhd,gkhd->ghqk", grad_att, projected[2])
    grad_value = heads_einsum("ghqk,gqhd->gkhd", probs_full.astype(jnp.bfloat16), grad_att)
    delta_sum = jnp.sum(probs_full * grad_prob, axis=-1, keepdims=True)
    grad_score = (probs_full * (grad_prob - delta_sum)).astype(jnp.bfloat16)
    grad_query = heads_einsum("ghqk,gkhd->gqhd", grad_score, projected[1]) * HDIM ** (-0.5)
    grad_key = heads_einsum("ghqk,gqhd->gkhd", grad_score, projected[0]) * HDIM ** (-0.5)
    grad_rows = (
        jnp.stack([grad_query, grad_key, grad_value])
        .reshape(3, prompts * SEQ, local_heads * HDIM)
        .astype(jnp.bfloat16)
    )
    grad_qkv = heads_einsum("td,cte->cde", attn_in, grad_rows)
    grad_in = scatter_tokens(heads_einsum("cte,cde->td", grad_rows, qkv_full))
    return (
        grad_one + grad_in,
        (grad_qkv, grad_out, grad_up, grad_down),
        (gain_one, gain_two),
        (bias_one, bias_two),
    )


def kernel_apply(features, vector, summed):
    return jnp.dot(features, summed, precision=HIGH) / D + CG_SHIFT * vector


def residual_norm(residual):
    return lax.psum(jnp.sum(residual * residual, axis=0), "rows")


def adam_moments(gradient, moment_one, moment_two, bias_one, bias_two):
    new_one = BETA_ONE * moment_one + (1.0 - BETA_ONE) * gradient
    new_two = BETA_TWO * moment_two + (1.0 - BETA_TWO) * gradient * gradient
    return (new_one / bias_one / (jnp.sqrt(new_two / bias_two) + ADAM_EPS), new_one, new_two)


def adam_update(master, gradient, moment_one, moment_two, clip_scale, bias_one, bias_two):
    direction, new_one, new_two = adam_moments(
        clip_scale * gradient, moment_one, moment_two, bias_one, bias_two
    )
    return (master - LEARN_RATE * (direction + DECAY_RATE * master), new_one, new_two)


def soap_columns(master, gradient, moment_one, moment_two, basis, clip_scale, bias_one, bias_two):
    height = gradient.shape[0]
    groups = basis.shape[0]
    split = (clip_scale * gradient).reshape(height, groups, HDIM)
    turned = jnp.einsum("iha,hab->ihb", split, basis, precision=HIGH).reshape(height, groups * HDIM)
    direction, new_one, new_two = adam_moments(turned, moment_one, moment_two, bias_one, bias_two)
    back = jnp.einsum(
        "ihb,hab->iha", direction.reshape(height, groups, HDIM), basis, precision=HIGH
    ).reshape(height, groups * HDIM)
    return (master - LEARN_RATE * (back + DECAY_RATE * master), new_one, new_two)


def per_device(
    token_ids,
    lengths,
    label_ids,
    targets,
    step_count,
    soap_owners,
    soap_basis,
    table_anchor,
    table_delta,
    table_first,
    table_second,
    qkv_anchor,
    qkv_delta,
    qkv_first,
    qkv_second,
    out_anchor,
    out_delta,
    out_first,
    out_second,
    up_anchor,
    up_delta,
    up_first,
    up_second,
    down_anchor,
    down_delta,
    down_first,
    down_second,
    gain_anchor,
    gain_delta,
    gain_first,
    gain_second,
    bias_anchor,
    bias_delta,
    bias_first,
    bias_second,
):
    head_index = lax.axis_index("heads")
    prompts = token_ids.shape[0]
    own_count = prompts // lax.axis_size("heads")
    full_table, table_step = (
        lax.all_gather(table_anchor, "rows", axis=0, tiled=True),
        lax.all_gather(table_delta.astype(jnp.bfloat16), "rows", axis=0, tiled=True),
    )
    vocab_part = full_table.shape[0]
    gathered = (
        lax.all_gather(qkv_anchor, "rows", axis=1, tiled=True),
        lax.all_gather(out_anchor, "rows", axis=1, tiled=True),
        lax.all_gather(up_anchor, "rows", axis=0, tiled=True),
        lax.all_gather(down_anchor, "rows", axis=1, tiled=True),
        lax.all_gather(qkv_delta.astype(jnp.bfloat16), "rows", axis=1, tiled=True),
        lax.all_gather(out_delta.astype(jnp.bfloat16), "rows", axis=1, tiled=True),
        lax.all_gather(up_delta.astype(jnp.bfloat16), "rows", axis=0, tiled=True),
        lax.all_gather(down_delta.astype(jnp.bfloat16), "rows", axis=1, tiled=True),
    )
    weights = gathered[:4]
    steps_low = gathered[4:]
    flat_ids = token_ids.reshape(-1)
    local_ids = flat_ids - head_index * vocab_part
    inside = (local_ids >= 0) & (local_ids < vocab_part)
    clipped_ids = jnp.clip(local_ids, 0, vocab_part - 1)
    base_rows = jnp.where(
        inside[:, None], jnp.take(full_table, clipped_ids, axis=0).astype(jnp.float32), 0.0
    )
    step_rows = jnp.where(
        inside[:, None], jnp.take(table_step, clipped_ids, axis=0).astype(jnp.float32), 0.0
    )
    embedded, embedded_dot = scatter_tokens((base_rows, step_rows))
    start_x, start_dot, normed_zero, inverse_zero = norm_pair(
        embedded, embedded_dot, gain_anchor[0], bias_anchor[0], gain_delta[0], bias_delta[0]
    )
    live_keys = lax.broadcasted_iota(jnp.int32, (prompts, SEQ), 1) < lengths[:, None]
    final_out, final_dot, saved = layer_forward(
        start_x,
        start_dot,
        live_keys,
        weights,
        steps_low,
        gain_anchor,
        bias_anchor,
        gain_delta,
        bias_delta,
        prompts,
    )
    own_lengths = lax.dynamic_slice_in_dim(lengths, head_index * own_count, own_count, 0)
    live_own = lax.broadcasted_iota(jnp.int32, (own_count, SEQ), 1) < own_lengths[:, None]
    length_own = own_lengths.astype(jnp.float32)[:, None]
    feat_own = (
        jnp.sum(jnp.where(live_own[:, :, None], final_out.reshape(own_count, SEQ, D), 0.0), axis=1)
        / length_own
    ).astype(jnp.bfloat16)
    feat_dot_own = (
        jnp.sum(jnp.where(live_own[:, :, None], final_dot.reshape(own_count, SEQ, D), 0.0), axis=1)
        / length_own
    ).astype(jnp.bfloat16)
    feat_all, feat_dot_all = gather_tokens((feat_own, feat_dot_own))
    logits = heads_einsum("gd,vd->gv", feat_all, full_table)
    logit_dot = heads_einsum("gd,vd->gv", feat_dot_all, full_table) + heads_einsum(
        "gd,vd->gv", feat_all, table_step
    )
    label_local = label_ids - head_index * vocab_part
    label_owned = (label_local >= 0) & (label_local < vocab_part)
    label_clip = jnp.clip(label_local, 0, vocab_part - 1)
    label_logit = jnp.where(label_owned, jnp.take_along_axis(logits, label_clip, axis=1), 0.0)
    label_dot = jnp.where(label_owned, jnp.take_along_axis(logit_dot, label_clip, axis=1), 0.0)
    peak_local = jnp.max(logits, axis=1)
    exponent = jnp.exp(logits - peak_local[:, None])
    stats = (
        peak_local,
        jnp.sum(exponent, axis=1),
        jnp.sum(exponent * logit_dot, axis=1),
        label_logit,
        label_dot,
    )
    peak_all, sum_all, weighted_all, label_all, label_dot_all = merged(
        stats, "heads", combine_stats
    )
    log_norm = peak_all + jnp.log(sum_all)
    linear = label_all - log_norm[:, None] + label_dot_all - (weighted_all / sum_all)[:, None]
    differ = linear - targets
    own_differ = lax.dynamic_slice_in_dim(differ, head_index * own_count, own_count, 0)
    loss_part = jnp.sum(own_differ * own_differ) / NLW
    feat_float = feat_all.astype(jnp.float32)
    feature_total = lax.psum(jnp.sum(feat_float, axis=0), "rows")
    features = feat_float - feature_total / (feat_float.shape[0] * lax.axis_size("rows"))
    solution = jnp.zeros_like(differ)
    residual = differ
    direction = differ
    norm_now = residual_norm(residual)
    for step in range(CGIT):
        summed, direction_sq = lax.psum(
            (
                jnp.dot(features.T, direction, precision=HIGH),
                jnp.sum(direction * direction, axis=0),
            ),
            "rows",
        )
        image = kernel_apply(features, direction, summed)
        alpha = norm_now / (jnp.sum(summed * summed, axis=0) / D + CG_SHIFT * direction_sq)
        solution = solution + alpha * direction
        residual = residual - alpha * image
        if step + 1 < CGIT:
            norm_next = residual_norm(residual)
            direction = residual + norm_next / norm_now * direction
            norm_now = norm_next
    coefficient = 2.0 * solution / NLW
    vocab_iota = lax.broadcasted_iota(jnp.int32, logits.shape, 1)
    grad_logits = -jnp.sum(coefficient, axis=1, keepdims=True) * jnp.exp(logits - log_norm[:, None])
    for word in range(NLW):
        grad_logits = grad_logits + jnp.where(
            vocab_iota == label_local[:, word : word + 1], coefficient[:, word : word + 1], 0.0
        )
    grad_logits = grad_logits.astype(jnp.bfloat16)
    grad_feat = scatter_tokens(product(grad_logits, full_table))
    grad_final = jnp.where(live_own[:, :, None], (grad_feat / length_own)[:, None, :], 0.0).reshape(
        own_count * SEQ, D
    )
    grad_start, weight_grads, gain_grads, bias_grads = layer_backward(
        grad_final, saved, live_keys, weights, gain_anchor, prompts
    )
    grad_embed, gain_zero, bias_zero = norm_backward(
        grad_start, normed_zero, inverse_zero, gain_anchor[0]
    )
    grad_embed_all = gather_tokens(grad_embed.astype(jnp.bfloat16))
    head_term = heads_einsum("gv,gd->vd", grad_logits, feat_all)
    lookup_grad = jnp.where(inside[:, None], grad_embed_all.astype(jnp.float32), 0.0)
    table_term = head_term.at[clipped_ids].add(lookup_grad)
    table_grad = lax.psum_scatter(
        table_term.astype(jnp.bfloat16), "rows", scatter_dimension=0, tiled=True
    ).astype(jnp.float32)
    owned = (
        lax.psum_scatter(
            weight_grads[0].astype(jnp.bfloat16), "rows", scatter_dimension=1, tiled=True
        ).astype(jnp.float32),
        lax.psum_scatter(
            weight_grads[1].astype(jnp.bfloat16), "rows", scatter_dimension=1, tiled=True
        ).astype(jnp.float32),
        lax.psum_scatter(
            weight_grads[2].astype(jnp.bfloat16), "rows", scatter_dimension=0, tiled=True
        ).astype(jnp.float32),
        lax.psum_scatter(
            weight_grads[3].astype(jnp.bfloat16), "rows", scatter_dimension=1, tiled=True
        ).astype(jnp.float32),
    )
    gain_part = jnp.stack([gain_zero, gain_grads[0], gain_grads[1]])
    bias_part = jnp.stack([bias_zero, bias_grads[0], bias_grads[1]])
    owned_squares = jnp.sum(table_grad * table_grad) + sum(
        (jnp.sum(gradient * gradient) for gradient in owned)
    )
    gain_grad, bias_grad, loss_value, squares = lax.psum(
        (gain_part, bias_part, loss_part, owned_squares), ("rows", "heads")
    )
    squares = squares + jnp.sum(gain_grad * gain_grad) + jnp.sum(bias_grad * bias_grad)
    clip_scale = jnp.minimum(1.0, CLIP_NORM / jnp.sqrt(squares))
    count = step_count[0].astype(jnp.float32)
    bias_one = 1.0 - jnp.power(BETA_ONE, count)
    bias_two = 1.0 - jnp.power(BETA_TWO, count)
    deltas = (table_delta, qkv_delta, out_delta, up_delta, down_delta, gain_delta, bias_delta)
    grads = (table_grad, owned[0], owned[1], owned[2], owned[3], gain_grad, bias_grad)
    firsts = (table_first, qkv_first, out_first, up_first, down_first, gain_first, bias_first)
    seconds = (
        table_second,
        qkv_second,
        out_second,
        up_second,
        down_second,
        gain_second,
        bias_second,
    )
    results = [
        adam_update(
            deltas[index],
            grads[index],
            firsts[index],
            seconds[index],
            clip_scale,
            bias_one,
            bias_two,
        )
        for index in range(7)
    ]
    own_flag = soap_owners[0] == 1
    qkv_parts = [
        soap_columns(
            qkv_delta[index],
            owned[0][index],
            qkv_first[index],
            qkv_second[index],
            soap_basis[index],
            clip_scale,
            bias_one,
            bias_two,
        )
        for index in range(3)
    ]
    qkv_soap = tuple((jnp.stack([part[member] for part in qkv_parts]) for member in range(3)))
    results[1] = tuple(
        (jnp.where(own_flag, qkv_soap[member], results[1][member]) for member in range(3))
    )
    out_soap = soap_columns(
        out_delta.T,
        owned[1].T,
        out_first.T,
        out_second.T,
        soap_basis[3],
        clip_scale,
        bias_one,
        bias_two,
    )
    results[2] = tuple(
        (jnp.where(own_flag, out_soap[member].T, results[2][member]) for member in range(3))
    )
    flat = [loss_value]
    for triple in results:
        flat.extend(triple)
    return (
        flat[0],
        flat[1],
        flat[2],
        flat[3],
        flat[4],
        flat[5],
        flat[6],
        flat[7],
        flat[8],
        flat[9],
        flat[10],
        flat[11],
        flat[12],
        flat[13],
        flat[14],
        flat[15],
        flat[16],
        flat[17],
        flat[18],
        flat[19],
        flat[20],
        flat[21],
    )


def solution(mesh):
    placed = (
        P("rows", None),
        P("rows"),
        P("rows", None),
        P("rows", None),
        P(),
        P("rows"),
        P(None, "heads", None, None),
        P(("heads", "rows"), None),
        P(("heads", "rows"), None),
        P(("heads", "rows"), None),
        P(("heads", "rows"), None),
        P(None, "rows", "heads"),
        P(None, "rows", "heads"),
        P(None, "rows", "heads"),
        P(None, "rows", "heads"),
        P("heads", "rows"),
        P("heads", "rows"),
        P("heads", "rows"),
        P("heads", "rows"),
        P("rows", "heads"),
        P("rows", "heads"),
        P("rows", "heads"),
        P("rows", "heads"),
        P("heads", "rows"),
        P("heads", "rows"),
        P("heads", "rows"),
        P("heads", "rows"),
        P(),
        P(),
        P(),
        P(),
        P(),
        P(),
        P(),
        P(),
    )
    return jax.shard_map(
        per_device,
        mesh=mesh,
        in_specs=placed,
        out_specs=(
            P(),
            P(("heads", "rows"), None),
            P(("heads", "rows"), None),
            P(("heads", "rows"), None),
            P(None, "rows", "heads"),
            P(None, "rows", "heads"),
            P(None, "rows", "heads"),
            P("heads", "rows"),
            P("heads", "rows"),
            P("heads", "rows"),
            P("rows", "heads"),
            P("rows", "heads"),
            P("rows", "heads"),
            P("heads", "rows"),
            P("heads", "rows"),
            P("heads", "rows"),
            P(),
            P(),
            P(),
            P(),
            P(),
            P(),
        ),
        check_vma=False,
    )
```

profile of v0, /device:TPU:0, one launch (start us, length us, event | category | flops | bytes accessed | tf_op | source)
XLA Modules:
  0.0 2795.1 jit_solution(15720885713043264310)
XLA Ops:
  12.8 371.1 %all-gather.49.cloned.1.call-done = bf16[8,1572,768]{2,1,0:T(8,128)(2,1)} async-done(((bf16[1,1572,768]{2,1,0:T(8,128)(2,1)}), bf16[8,1572,768]{2,1,0:T(8,128)(2,1)}) %all-gather.49.cloned.1.call-update) | async-done | bytes 19316752 | tf_op jit(solution)/shard_map/all_gather | solution.py:312
  419.4 338.2 %all-gather.51.cloned.1.call-done = bf16[8,1572,768]{2,1,0:T(8,128)(2,1)} async-done(((bf16[1,1572,768]{2,1,0:T(8,128)(2,1)}), bf16[8,1572,768]{2,1,0:T(8,128)(2,1)}) %all-gather.51.cloned.1.call-update) | async-done | bytes 19316752 | tf_op jit(solution)/shard_map/all_gather | solution.py:313
  828.3 37.3 %all_gather.89 = bf16[3,768,192]{2,0,1:T(4,128)(2,1)S(1)} all-gather(bf16[3,96,192]{2,0,1:T(4,128)(2,1)S(1)} %copy.222), channel_id=1, replica_groups=mesh['rows'=8,'heads'=4] {'rows'}, dimensions={1}, use_global_device_ids=true | all-gather | bytes 995328 | tf_op jit(solution)/shard_map/all_gather | solution.py:317
  866.6 33.2 %all_gather.90 = bf16[192,768]{0,1:T(8,128)(2,1)} all-gather(bf16[192,96]{0,1:T(8,128)(2,1)S(1)} %copy.229), channel_id=1, replica_groups=mesh['rows'=8,'heads'=4] {'rows'}, dimensions={1}, use_global_device_ids=true | all-gather | bytes 331776 | tf_op jit(solution)/shard_map/all_gather | solution.py:318
  977.0 42.9 %all_gather.101 = bf16[3,768,192]{2,0,1:T(4,128)(2,1)} all-gather(bf16[3,96,192]{2,0,1:T(4,128)(2,1)S(1)} %copy.231), channel_id=1, replica_groups=mesh['rows'=8,'heads'=4] {'rows'}, dimensions={1}, use_global_device_ids=true | all-gather | bytes 995328 | tf_op jit(solution)/shard_map/all_gather | solution.py:321
  1023.4 33.1 %all_gather.102 = bf16[192,768]{0,1:T(8,128)(2,1)} all-gather(bf16[192,96]{0,1:T(8,128)(2,1)S(1)} %copy.242), channel_id=1, replica_groups=mesh['rows'=8,'heads'=4] {'rows'}, dimensions={1}, use_global_device_ids=true | all-gather | bytes 331776 | tf_op jit(solution)/shard_map/all_gather | solution.py:322
  1141.9 29.5 %reduce-scatter.27.cloned.1.call-done = bf16[256,768]{1,0:T(8,128)(2,1)} async-done(((bf16[1024,768]{1,0:T(8,128)(2,1)}), bf16[256,768]{1,0:T(8,128)(2,1)}) %reduce-scatter.27.cloned.1.call-update) | async-done | bytes 393232 | tf_op jit(solution)/shard_map/reduce_scatter | solution.py:93
  1201.5 39.0 %all-gather.39.cloned.1.call-done = bf16[768,768]{1,0:T(8,128)(2,1)} async-done(((bf16[96,768]{1,0:T(8,128)(2,1)}), bf16[768,768]{1,0:T(8,128)(2,1)}) %all-gather.39.cloned.1.call-update) | async-done | bytes 1179664 | tf_op jit(solution)/shard_map/all_gather | solution.py:323
  1249.1 33.8 %all-gather.41.cloned.1.call-done = bf16[768,768]{0,1:T(8,128)(2,1)} async-done(((bf16[768,96]{0,1:T(8,128)(2,1)}), bf16[768,768]{0,1:T(8,128)(2,1)}) %all-gather.41.cloned.1.call-update) | async-done | bytes 1179664 | tf_op jit(solution)/shard_map/all_gather | solution.py:324
  1414.9 33.0 %all-reduce.14 = (f32[768,4]{0,1:T(4,128)S(1)}, f32[4]{0:T(128)S(1)}) all-reduce(f32[768,4]{0,1:T(4,128)S(1)} %fusion.237, f32[4]{0:T(128)S(1)} %get-tuple-element.504), channel_id=1, replica_groups=mesh['rows'=8,'heads'=4] {'rows'}, use_global_device_ids=true, to_apply=%region_34.37 | all-reduce | flops 3076 | bytes 24608 | tf_op jit(solution)/shard_map/psum | solution.py:401
  1467.3 34.8 %all-reduce.13 = (f32[768,4]{0,1:T(4,128)S(1)}, f32[4]{0:T(128)S(1)}) all-reduce(f32[768,4]{0,1:T(4,128)S(1)} %fusion.236, f32[4]{0:T(128)S(1)} %get-tuple-element.502), channel_id=1, replica_groups=mesh['rows'=8,'heads'=4] {'rows'}, use_global_device_ids=true, to_apply=%region_38.41 | all-reduce | flops 3076 | bytes 24608 | tf_op jit(solution)/shard_map/psum | solution.py:401
  1521.4 34.9 %all-reduce.12 = (f32[768,4]{0,1:T(4,128)S(1)}, f32[4]{0:T(128)S(1)}) all-reduce(f32[768,4]{0,1:T(4,128)S(1)} %fusion.235, f32[4]{0:T(128)S(1)} %get-tuple-element.500), channel_id=1, replica_groups=mesh['rows'=8,'heads'=4] {'rows'}, use_global_device_ids=true, to_apply=%region_44.47 | all-reduce | flops 3076 | bytes 24608 | tf_op jit(solution)/shard_map/psum | solution.py:401
  1575.6 34.8 %all-reduce.11 = (f32[768,4]{0,1:T(4,128)S(1)}, f32[4]{0:T(128)S(1)}) all-reduce(f32[768,4]{0,1:T(4,128)S(1)} %fusion.234, f32[4]{0:T(128)S(1)} %get-tuple-element.498), channel_id=1, replica_groups=mesh['rows'=8,'heads'=4] {'rows'}, use_global_device_ids=true, to_apply=%region_50.53 | all-reduce | flops 3076 | bytes 24608 | tf_op jit(solution)/shard_map/psum | solution.py:401
  1629.7 34.9 %all-reduce.10 = (f32[768,4]{0,1:T(4,128)S(1)}, f32[4]{0:T(128)S(1)}) all-reduce(f32[768,4]{0,1:T(4,128)S(1)} %fusion.233, f32[4]{0:T(128)S(1)} %get-tuple-element.496), channel_id=1, replica_groups=mesh['rows'=8,'heads'=4] {'rows'}, use_global_device_ids=true, to_apply=%region_56.59 | all-reduce | flops 3076 | bytes 24608 | tf_op jit(solution)/shard_map/psum | solution.py:401
  1683.9 34.8 %all-reduce.9 = (f32[768,4]{0,1:T(4,128)S(1)}, f32[4]{0:T(128)S(1)}) all-reduce(f32[768,4]{0,1:T(4,128)S(1)} %fusion.232, f32[4]{0:T(128)S(1)} %get-tuple-element.494), channel_id=1, replica_groups=mesh['rows'=8,'heads'=4] {'rows'}, use_global_device_ids=true, to_apply=%region_62.65 | all-reduce | flops 3076 | bytes 24608 | tf_op jit(solution)/shard_map/psum | solution.py:401
  1738.1 34.8 %all-reduce.8 = (f32[768,4]{0,1:T(4,128)S(1)}, f32[4]{0:T(128)S(1)}) all-reduce(f32[768,4]{0,1:T(4,128)S(1)} %fusion.231, f32[4]{0:T(128)S(1)} %get-tuple-element.492), channel_id=1, replica_groups=mesh['rows'=8,'heads'=4] {'rows'}, use_global_device_ids=true, to_apply=%region_68.71 | all-reduce | flops 3076 | bytes 24608 | tf_op jit(solution)/shard_map/psum | solution.py:401
  1793.3 35.4 %all-reduce.7 = (f32[4]{0:T(128)S(1)}, f32[768,4]{0,1:T(4,128)S(1)}) all-reduce(f32[4]{0:T(128)S(1)} %multiply_reduce_fusion.22, f32[768,4]{0,1:T(4,128)S(1)} %fusion.230), channel_id=1, replica_groups=mesh['rows'=8,'heads'=4] {'rows'}, use_global_device_ids=true, to_apply=%region_77.80 | all-reduce | flops 3076 | bytes 24608 | tf_op jit(solution)/shard_map/psum | solution.py:401
  1992.8 43.8 %reduce-scatter.35.cloned.1.call-done = bf16[96,768]{1,0:T(8,128)(2,1)} async-done(((bf16[768,768]{1,0:T(8,128)(2,1)}), bf16[96,768]{1,0:T(8,128)(2,1)}) %reduce-scatter.35.cloned.1.call-update) | async-done | bytes 147472 | tf_op jit(solution)/shard_map/reduce_scatter | solution.py:448
  2038.3 66.2 %reduce-scatter.37.cloned.1.call-done = bf16[768,96]{0,1:T(8,128)(2,1)} async-done(((bf16[768,768]{0,1:T(8,128)(2,1)}), bf16[768,96]{0,1:T(8,128)(2,1)}) %reduce-scatter.37.cloned.1.call-update) | async-done | bytes 147472 | tf_op jit(solution)/shard_map/reduce_scatter | solution.py:451
  2106.1 62.9 %reduce-scatter.41.cloned.1.call-done = bf16[96,192]{1,0:T(8,128)(2,1)} async-done(((bf16[768,192]{1,0:T(8,128)(2,1)}), bf16[96,192]{1,0:T(8,128)(2,1)}) %reduce-scatter.41.cloned.1.call-update) | async-done | bytes 36880
  2170.5 65.4 %reduce-scatter.39.cloned.1.call-done = bf16[96,576]{1,0:T(8,128)(2,1)} async-done(((bf16[768,576]{1,0:T(8,128)(2,1)}), bf16[96,576]{1,0:T(8,128)(2,1)}) %reduce-scatter.39.cloned.1.call-update) | async-done | bytes 110608
  2256.7 33.0 %scatter_custom_fusion = f32[12576,768]{1,0:T(8,128)} fusion(f32[12576,768]{1,0:T(8,128)} %fusion.258, s32[1024]{0:T(1024)S(1)} %bitcast.501, bf16[1024,768]{1,0:T(8,128)(2,1)} %all-gather.47.cloned.1.call-done, f32[]{:T(128)} %constant.87.clone.1, pred[1024]{0:T(1024)(128)(4,1)S(1)} %copy-done.85), kind=kCustom, calls=%fused_computation.39 | custom fusion | flops 2359296 | bytes 40207872 | tf_op jit(solution)/shard_map/scatter-add | solution.py:437
  2310.4 375.7 %fusion = bf16[1576,768]{1,0:T(8,128)(2,1)S(1)} fusion(bf16[12576,768]{1,0:T(8,128)(2,1)} %convert_element_type.278), kind=kCustom, calls=%all-reduce-scatter | all-reduce-scatter fusion | flops 9682945 | bytes 21737984
  2703.0 47.2 %all-reduce.6 = (f32[]{:T(128)}, f32[]{:T(128)}, f32[3,768]{1,0:T(4,128)}, f32[3,768]{1,0:T(4,128)}) all-reduce(f32[]{:T(128)S(6)} %div.370, f32[]{:T(128)S(6)} %add.717, f32[3,768]{1,0:T(4,128)} %pad_maximum_fusion, f32[3,768]{1,0:T(4,128)} %pad_maximum_fusion.1), channel_id=1, replica_groups=mesh['rows'=8,'heads'=4] {'rows','heads'}, use_global_device_ids=true, to_apply=%region_29.32 | all-reduce | flops 4610 | bytes 36880 | tf_op jit(solution)/shard_map/psum | solution.py:460
  (547 shorter events, 839.9 us)
Async XLA Ops:
  7.2 376.7 %all-gather.49.cloned.1.call-start = ((), (), s32[]{:S(2)}) async-start(), calls=%async_computation.33 | async-start | bytes 21786624 | tf_op jit(solution)/shard_map/all_gather | solution.py:312
  7.9 749.7 %all-gather.51.cloned.1.call-start = ((), (), s32[]{:S(2)}) async-start(), calls=%async_computation.34 | async-start | bytes 21786624 | tf_op jit(solution)/shard_map/all_gather | solution.py:313
  12.0 811.6 %reduce-scatter.19.cloned.1.call-start = ((), (), s32[]{:S(2)}) async-start(), calls=%async_computation.12 | async-start | bytes 1966080 | tf_op jit(solution)/shard_map/reduce_scatter | solution.py:93
  795.6 104.9 %all-gather.27.cloned.1.call-start = ((), (), s32[]{:S(2)}) async-start(), calls=%async_computation.13 | async-start | bytes 1966080 | tf_op jit(solution)/shard_map/all_gather | solution.py:85
  828.1 111.0 %reduce-scatter.21.cloned.1.call-start = ((), (), s32[]{:S(2)}) async-start(), calls=%async_computation.14 | async-start | bytes 1966080 | tf_op jit(solution)/shard_map/reduce_scatter | solution.py:93
  911.6 58.6 %reduce-scatter.25.cloned.1.call-start = ((), (), s32[]{:S(2)}) async-start(), calls=%async_computation.19 | async-start | bytes 1966080 | tf_op jit(solution)/shard_map/reduce_scatter | solution.py:93
  912.1 149.0 %all-gather.31.cloned.1.call-start = ((), (), s32[]{:S(2)}) async-start(), calls=%async_computation.16 | async-start | bytes 1327104 | tf_op jit(solution)/shard_map/all_gather | solution.py:319
  912.9 148.3 %all-gather.29.cloned.1.call-start = ((), (), s32[]{:S(2)}) async-start(), calls=%async_computation.15 | async-start | bytes 1966080 | tf_op jit(solution)/shard_map/all_gather | solution.py:85
  975.1 114.4 %all-gather.33.cloned.1.call-start = ((), (), s32[]{:S(2)}) async-start(), calls=%async_computation.17 | async-start | bytes 1327104 | tf_op jit(solution)/shard_map/all_gather | solution.py:320
  975.9 133.4 %all-gather.35.cloned.1.call-start = ((), (), s32[]{:S(2)}) async-start(), calls=%async_computation.20 | async-start | bytes 1966080 | tf_op jit(solution)/shard_map/all_gather | solution.py:85
  1060.7 79.7 %reduce-scatter.23.cloned.1.call-start = ((), (), s32[]{:S(2)}) async-start(), calls=%async_computation.18 | async-start | bytes 1966080 | tf_op jit(solution)/shard_map/reduce_scatter | solution.py:93
  1093.8 77.6 %reduce-scatter.27.cloned.1.call-start = ((), (), s32[]{:S(2)}) async-start(), calls=%async_computation.21 | async-start | bytes 1966080 | tf_op jit(solution)/shard_map/reduce_scatter | solution.py:93
  1128.1 68.6 %all-gather.37.cloned.1.call-start = ((), (), s32[]{:S(2)}) async-start(), calls=%async_computation.22 | async-start | bytes 1966080 | tf_op jit(solution)/shard_map/all_gather | solution.py:85
  1176.9 63.6 %all-gather.39.cloned.1.call-start = ((), (), s32[]{:S(2)}) async-start(), calls=%async_computation.23 | async-start | bytes 1327104 | tf_op jit(solution)/shard_map/all_gather | solution.py:323
  1178.6 104.3 %all-gather.41.cloned.1.call-start = ((), (), s32[]{:S(2)}) async-start(), calls=%async_computation.24 | async-start | bytes 1327104 | tf_op jit(solution)/shard_map/all_gather | solution.py:324
  1179.4 135.7 %reduce-scatter.29.cloned.1.call-start = ((), (), s32[]{:S(2)}) async-start(), calls=%async_computation.25 | async-start | bytes 1966080 | tf_op jit(solution)/shard_map/reduce_scatter | solution.py:93
  1288.2 577.3 %all-gather.43.cloned.1.call-start = ((), (), s32[]{:S(2)}) async-start(), calls=%async_computation.26 | async-start | bytes 1966080 | tf_op jit(solution)/shard_map/all_gather | solution.py:85
  1848.2 53.9 %reduce-scatter.31.cloned.1.call-start = ((), (), s32[]{:S(2)}) async-start(), calls=%async_computation.27 | async-start | bytes 1966080 | tf_op jit(solution)/shard_map/reduce_scatter | solution.py:93
  1905.6 62.9 %reduce-scatter.33.cloned.1.call-start = ((), (), s32[]{:S(2)}) async-start(), calls=%async_computation.29 | async-start | bytes 1966080 | tf_op jit(solution)/shard_map/reduce_scatter | solution.py:93
  1940.4 96.3 %reduce-scatter.35.cloned.1.call-start = ((), (), s32[]{:S(2)}) async-start(), calls=%async_computation.31 | async-start | bytes 1327104 | tf_op jit(solution)/shard_map/reduce_scatter | solution.py:448
  1944.4 160.1 %reduce-scatter.37.cloned.1.call-start = ((), (), s32[]{:S(2)}) async-start(), calls=%async_computation.32 | async-start | bytes 1327104 | tf_op jit(solution)/shard_map/reduce_scatter | solution.py:451
  1949.1 219.8 %reduce-scatter.41.cloned.1.call-start = ((), (), s32[]{:S(2)}) async-start(), calls=%async_computation.36 | async-start | bytes 442368
  1950.6 285.3 %reduce-scatter.39.cloned.1.call-start = ((), (), s32[]{:S(2)}) async-start(), calls=%async_computation.35 | async-start | bytes 1105920
  1959.5 297.2 %all-gather.47.cloned.1.call-start = ((), (), s32[]{:S(2)}) async-start(), calls=%async_computation.30 | async-start | bytes 1966080 | tf_op jit(solution)/shard_map/all_gather | solution.py:85
  (99 other events, 3614.7 us)
Sparse Core Ops, SparseCore 0:
  9.5 374.3 all-gather.48
  386.0 371.5 all-gather.50
  795.7 27.9 reduce-scatter.18
  828.2 19.6 all-gather.26
  911.7 27.3 reduce-scatter.20
  942.1 28.0 reduce-scatter.24
  972.3 53.4 all-gather.30
  1028.0 18.1 all-gather.28
  1048.4 41.1 all-gather.32
  1090.9 18.3 all-gather.34
  1112.4 27.9 reduce-scatter.22
  1143.4 27.9 reduce-scatter.26
  1177.0 19.6 all-gather.36
  1199.3 41.1 all-gather.38
  1243.1 39.7 all-gather.40
  1288.3 26.6 reduce-scatter.28
  1874.1 27.9 reduce-scatter.30
  1905.8 19.6 all-gather.44
  1940.5 28.0 reduce-scatter.32
  1972.0 64.6 reduce-scatter.34
  2040.6 63.7 reduce-scatter.36
  2107.7 61.2 reduce-scatter.40
  2172.8 63.1 reduce-scatter.38
  2238.0 18.6 all-gather.46
  (1 shorter events, 17.1 us)
where the time goes:
time: 2810 us; the launch traced here: 2800 us
  waiting for transfers between devices  1300 us (46%)
  blocking collectives  1020 us (36%)
  matrix products  166 us (6%)
  other arithmetic  139 us (5%)
  local copies, waits for them, and re-layouts  135 us (5%)
    unnamed x3, blocking collectives  387 us
    all_gather x1, waiting for transfers between devices, per_device(): lax.all_gather(table_anchor, 'rows', axis=0, tiled=True)  371 us
    all_gather x1, waiting for transfers between devices, per_device(): lax.all_gather(table_delta.astype(jnp.bfloat16), 'rows', axis=0, tiled=True)  338 us
    psum x8, blocking collectives, per_device(): lax.psum((jnp.dot(features.T, direction, precision=HIGH), jnp.sum(directi...  277 us
    reduce_scatter x8, waiting for transfers between devices, scatter_tokens(): lax.psum_scatter(shortened(values), 'heads', scatter_dimension=0, tiled=T...  177 us
    unnamed x28, waiting for transfers between devices  132 us
    psum x7, blocking collectives, residual_norm(): return lax.psum(jnp.sum(residual * residual, axis=0), 'rows')  120 us
    dot_general x22, matrix products, heads_einsum(): return jnp.einsum(form, left, right, preferred_element_type=jnp.float32)  88.5 us
  transfers between devices with their start and end apart: 26, of which 23 were waited for; matrix products, arithmetic and copies ran while one was open for 6% of the time, Pallas kernels for 0%

commit v1 on v0

v1 whole, which is shorter than its diff:
```python
import jax
import jax.numpy as jnp
from jax import lax
from jax.experimental import pallas as pl
from jax.sharding import PartitionSpec as P

D = 768
HDIM = 64
SEQ = 256
NLW = 4
CGIT = 8
STATS = 16

EPS_NORM = 1e-05
BETA_ONE = 0.9
BETA_TWO = 0.999
ADAM_EPS = 1e-08
LEARN_RATE = 0.03
DECAY_RATE = 0.01
CLIP_NORM = 1.0
CG_SHIFT = 0.002
MASKED = -1e30
HALF_ROOT = 0.7071067811865476
INV_ROOT_TAU = 0.3989422804014327
HIGH = lax.Precision.HIGHEST
ALL = ("heads", "rows")
LOW = jnp.bfloat16


def einsum(form, left, right):
    return jnp.einsum(form, left, right, preferred_element_type=jnp.float32)


def gelu_slope(values):
    return (
        0.5 * (1.0 + lax.erf(values * HALF_ROOT))
        + values * jnp.exp(-0.5 * values * values) * INV_ROOT_TAU
    )


def norm_pair(values, dots, gain, bias, gain_dot, bias_dot):
    center = values - jnp.mean(values, axis=-1, keepdims=True)
    inverse = lax.rsqrt(jnp.mean(center * center, axis=-1, keepdims=True) + EPS_NORM)
    normed = center * inverse
    normed_dot = inverse * (
        dots
        - jnp.mean(dots, axis=-1, keepdims=True)
        - normed * jnp.mean(normed * dots, axis=-1, keepdims=True)
    )
    return (normed * gain + bias, normed_dot * gain + normed * gain_dot + bias_dot, normed, inverse)


def norm_backward(grad_out, normed, inverse, gain):
    scaled = grad_out * gain
    grad_in = inverse * (
        scaled
        - jnp.mean(scaled, axis=-1, keepdims=True)
        - normed * jnp.mean(scaled * normed, axis=-1, keepdims=True)
    )
    return (grad_in, jnp.sum(grad_out * normed, axis=0), jnp.sum(grad_out, axis=0))


def partners(axis):
    size = lax.axis_size(axis)
    bit = 1
    while bit < size:
        yield bit, [(index, index ^ bit) for index in range(size)]
        bit *= 2


def spread(block):
    for axis in reversed(ALL):
        here = lax.axis_index(axis)
        for bit, pairs in partners(axis):
            other = lax.ppermute(block, axis, pairs)
            block = jnp.where(
                (here & bit) > 0,
                jnp.concatenate([other, block]),
                jnp.concatenate([block, other]),
            )
    return block


def total(values, combine=jnp.add):
    for axis in reversed(ALL):
        for _, pairs in partners(axis):
            values = jax.tree.map(
                lambda part: combine(part, lax.ppermute(part, axis, pairs)), values
            )
    return values


def solve_kernel(stats_ref, feat_ref, targets_ref, coef_ref, norm_ref, loss_ref):
    count = feat_ref.shape[0]

    def stat(index):
        return stats_ref[:, index * count : (index + 1) * count]

    peaks = stat(0)
    peak = jnp.max(peaks, axis=0, keepdims=True)
    scale = jnp.exp(peaks - peak)
    mass = jnp.sum(stat(1) * scale, axis=0, keepdims=True)
    weighted = jnp.sum(stat(2) * scale, axis=0, keepdims=True)
    log_norm = peak + jnp.log(mass)
    shift = log_norm + weighted / mass
    picked = [
        jnp.sum(stat(3 + word) + stat(3 + NLW + word), axis=0, keepdims=True)
        for word in range(NLW)
    ]
    differ = jnp.concatenate(picked, axis=0) - shift - targets_ref[...]
    feat = feat_ref[...].astype(jnp.float32)
    center = feat - jnp.mean(feat, axis=0, keepdims=True)
    kernel = (
        lax.dot_general(
            center,
            center,
            (((1,), (1,)), ((), ())),
            precision=HIGH,
            preferred_element_type=jnp.float32,
        )
        / D
    )
    answer = jnp.zeros_like(differ)
    residual = differ
    direction = differ
    norm_now = jnp.sum(residual * residual, axis=1, keepdims=True)
    for step in range(CGIT):
        image = (
            jnp.dot(direction, kernel, precision=HIGH, preferred_element_type=jnp.float32)
            + CG_SHIFT * direction
        )
        alpha = norm_now / jnp.sum(direction * image, axis=1, keepdims=True)
        answer = answer + alpha * direction
        residual = residual - alpha * image
        if step + 1 < CGIT:
            norm_next = jnp.sum(residual * residual, axis=1, keepdims=True)
            direction = residual + norm_next / norm_now * direction
            norm_now = norm_next
    coef_ref[...] = 2.0 * answer / NLW
    norm_ref[...] = log_norm
    squares = jnp.sum(differ * differ, axis=1, keepdims=True)
    loss_ref[...] = jnp.sum(squares, axis=0, keepdims=True) / NLW


def solve(stats, feat, targets):
    count = feat.shape[0]
    return pl.pallas_call(
        solve_kernel,
        out_shape=(
            jax.ShapeDtypeStruct((NLW, count), jnp.float32),
            jax.ShapeDtypeStruct((1, count), jnp.float32),
            jax.ShapeDtypeStruct((1, 1), jnp.float32),
        ),
    )(stats, feat, targets)


def adam_moments(gradient, moment_one, moment_two, bias_one, bias_two):
    new_one = BETA_ONE * moment_one + (1.0 - BETA_ONE) * gradient
    new_two = BETA_TWO * moment_two + (1.0 - BETA_TWO) * gradient * gradient
    return (new_one / bias_one / (jnp.sqrt(new_two / bias_two) + ADAM_EPS), new_one, new_two)


def adam_update(master, gradient, moment_one, moment_two, clip_scale, bias_one, bias_two):
    direction, new_one, new_two = adam_moments(
        clip_scale * gradient, moment_one, moment_two, bias_one, bias_two
    )
    return (master - LEARN_RATE * (direction + DECAY_RATE * master), new_one, new_two)


def turned_update(owner, master, gradient, first, second, basis, clip_scale, bias_one, bias_two):
    count, height, width = gradient.shape

    def grouped(array):
        return array.reshape(count, height, width // HDIM, HDIM)

    plain = clip_scale * gradient
    turned = jnp.einsum("ciha,chab->cihb", grouped(plain), basis, precision=HIGH)
    used = jnp.where(owner, turned.reshape(gradient.shape), plain)
    direction, new_one, new_two = adam_moments(used, first, second, bias_one, bias_two)
    back = jnp.einsum("cihb,chab->ciha", grouped(direction), basis, precision=HIGH)
    direction = jnp.where(owner, back.reshape(gradient.shape), direction)
    return (master - LEARN_RATE * (direction + DECAY_RATE * master), new_one, new_two)


def per_device(
    token_ids,
    lengths,
    label_ids,
    targets,
    step_count,
    soap_owners,
    soap_basis,
    table_anchor,
    table_delta,
    table_first,
    table_second,
    qkv_anchor,
    qkv_delta,
    qkv_first,
    qkv_second,
    out_anchor,
    out_delta,
    out_first,
    out_second,
    up_anchor,
    up_delta,
    up_first,
    up_second,
    down_anchor,
    down_delta,
    down_first,
    down_second,
    gain_anchor,
    gain_delta,
    gain_first,
    gain_second,
    bias_anchor,
    bias_delta,
    bias_first,
    bias_second,
):
    n_heads = lax.axis_size("heads")
    n_rows = lax.axis_size("rows")
    count = n_heads * n_rows
    head_index = lax.axis_index("heads")
    me = head_index * n_rows + lax.axis_index("rows")
    vocab = table_anchor.shape[0]
    group_wide = qkv_anchor.shape[2]
    local_heads = group_wide // HDIM

    def side_by_side(qkv, out):
        return jnp.concatenate([qkv[0], qkv[1], qkv[2], out.T], axis=1)

    def gathered(anchor, delta):
        block = jnp.concatenate([anchor, delta.astype(LOW)], axis=1)
        full = lax.all_gather(block, ALL, axis=0, tiled=True)
        return full.reshape(n_heads, D, block.shape[1])

    attn_all = gathered(side_by_side(qkv_anchor, out_anchor), side_by_side(qkv_delta, out_delta))
    up_all = gathered(up_anchor, up_delta)
    down_all = gathered(down_anchor.T, down_delta.T)

    room = 8 * -(-(2 * SEQ // count + 8) // 8)
    slots = count * room
    ids = lax.dynamic_index_in_dim(token_ids, head_index, 0, keepdims=False)
    owner = ids // vocab
    local = ids - owner * vocab
    place = lax.iota(jnp.int32, SEQ)
    same = ids[:, None] == ids[None, :]
    earliest = jnp.min(jnp.where(same, place[None, :], SEQ), axis=1)
    leads = earliest == place
    rank = jnp.sum(
        (leads[None, :] & (owner[:, None] == owner[None, :]) & (place[None, :] < earliest[:, None])),
        axis=1,
        dtype=jnp.int32,
    )
    longest = jnp.max(rank) + 1
    rounds = -(-total(longest.reshape(1, 1), jnp.maximum)[0, 0] // room)
    both = jnp.concatenate([table_anchor, table_delta.astype(LOW)], axis=1)

    def slot_of(turn):
        within = rank - turn * room
        return jnp.where((within >= 0) & (within < room), owner * room + within, -1)

    def asked(turn):
        taken = jnp.where(leads, slot_of(turn), -1)
        hit = lax.iota(jnp.int32, slots)[:, None] == taken[None, :]
        wanted = jnp.sum(jnp.where(hit, local[None, :] + 1, 0), axis=1) - 1
        wanted = lax.all_to_all(wanted.reshape(count, room), ALL, 0, 0, tiled=True)
        return wanted.reshape(slots)

    def chosen(wanted):
        return (wanted[:, None] == lax.broadcasted_iota(jnp.int32, (slots, vocab), 1)).astype(LOW)

    def token_slots(turn):
        return (
            slot_of(turn)[:, None] == lax.broadcasted_iota(jnp.int32, (SEQ, slots), 1)
        ).astype(LOW)

    def fetch(turn, wanted):
        rows = einsum("sv,vd->sd", chosen(wanted), both).astype(LOW)
        rows = lax.all_to_all(rows.reshape(count, room, 2 * D), ALL, 0, 0, tiled=True)
        return einsum("ts,sd->td", token_slots(turn), rows.reshape(slots, 2 * D))

    def give(turn, wanted, grads):
        sums = einsum("ts,td->sd", token_slots(turn), grads).astype(LOW)
        sums = lax.all_to_all(sums.reshape(count, room, D), ALL, 0, 0, tiled=True)
        return einsum("sv,sd->vd", chosen(wanted), sums.reshape(slots, D))

    def more(start, step):
        def rest(value):
            return lax.fori_loop(1, rounds, lambda turn, so_far: so_far + step(turn), value)

        return lax.cond(rounds > 1, rest, lambda value: value, start)

    wanted_first = asked(0)
    embedded_both = more(fetch(0, wanted_first), lambda turn: fetch(turn, asked(turn)))
    start_x, start_dot, normed_zero, inverse_zero = norm_pair(
        embedded_both[:, :D],
        embedded_both[:, D:],
        gain_anchor[0],
        bias_anchor[0],
        gain_delta[0],
        bias_delta[0],
    )

    own_length = lax.dynamic_index_in_dim(lengths, head_index, 0, keepdims=False)
    live = lax.iota(jnp.int32, SEQ) < own_length
    length_float = own_length.astype(jnp.float32)

    notes = jnp.concatenate([label_ids.astype(jnp.float32), targets], axis=1)
    notes = jnp.swapaxes(lax.all_gather(notes, "rows"), 0, 1).reshape(count, 2 * NLW)
    labels = notes[:, :NLW].astype(jnp.int32) - me * vocab
    targets_all = notes[:, NLW:].T

    attn_in = start_x.astype(LOW)
    attn_dot_in = start_dot.astype(LOW)
    three = 3 * group_wide
    wide = attn_all.shape[2] // 2
    through = einsum("td,hde->the", attn_in, attn_all)
    projected = through[:, :, :three].astype(LOW)
    projected_dot = (
        through[:, :, wide : wide + three]
        + einsum("td,hde->the", attn_dot_in, attn_all[:, :, :three])
    ).astype(LOW)

    def split_heads(array):
        array = array.reshape(SEQ, n_heads, 3, local_heads, HDIM)
        return [array[:, :, index].reshape(SEQ, n_heads * local_heads, HDIM) for index in range(3)]

    query, key, value = split_heads(projected)
    query_dot, key_dot, value_dot = split_heads(projected_dot)
    scores = einsum("qhd,khd->hqk", query, key) * HDIM ** (-0.5)
    scores = jnp.where(live[None, None, :], scores, MASKED)
    exponent = jnp.exp(scores - jnp.max(scores, axis=-1, keepdims=True))
    probs = exponent / jnp.sum(exponent, axis=-1, keepdims=True)
    probs_low = probs.astype(LOW)
    score_dot = (
        einsum("qhd,khd->hqk", query_dot, key) + einsum("qhd,khd->hqk", query, key_dot)
    ) * HDIM ** (-0.5)
    prob_dot = (probs * (score_dot - jnp.sum(probs * score_dot, axis=-1, keepdims=True))).astype(LOW)
    attended = einsum("hqk,khd->qhd", probs_low, value).astype(LOW)
    attended_dot = (
        einsum("hqk,khd->qhd", prob_dot, value) + einsum("hqk,khd->qhd", probs_low, value_dot)
    ).astype(LOW)
    attended = attended.reshape(SEQ, n_heads, group_wide)
    attended_dot = attended_dot.reshape(SEQ, n_heads, group_wide)
    out_full = attn_all[:, :, three:wide]
    out_step = attn_all[:, :, wide + three :]
    attn_out = einsum("the,hde->td", attended, out_full)
    attn_dot = einsum("the,hde->td", attended_dot, out_full) + einsum(
        "the,hde->td", attended, out_step
    )
    hidden, hidden_dot, normed_one, inverse_one = norm_pair(
        start_x + attn_out,
        start_dot + attn_dot,
        gain_anchor[1],
        bias_anchor[1],
        gain_delta[1],
        bias_delta[1],
    )
    ffn_input = hidden.astype(LOW)
    half = up_all.shape[2] // 2
    up_full = up_all[:, :, :half]
    down_full = down_all[:, :, :half]
    through = einsum("td,hde->the", ffn_input, up_all)
    pre_gelu = through[:, :, :half]
    pre_dot = through[:, :, half:] + einsum("td,hde->the", hidden_dot.astype(LOW), up_full)
    activated = jax.nn.gelu(pre_gelu, approximate=False).astype(LOW)
    slope = gelu_slope(pre_gelu)
    act_dot = (slope * pre_dot).astype(LOW)
    ffn_out = einsum("the,hde->td", activated, down_full)
    ffn_dot = einsum("the,hde->td", act_dot, down_full) + einsum(
        "the,hde->td", activated, down_all[:, :, half:]
    )
    final_out, final_dot, normed_two, inverse_two = norm_pair(
        hidden + ffn_out,
        hidden_dot + ffn_dot,
        gain_anchor[2],
        bias_anchor[2],
        gain_delta[2],
        bias_delta[2],
    )

    def pooled(values):
        return (jnp.sum(jnp.where(live[:, None], values, 0.0), axis=0) / length_float).astype(LOW)

    feats = spread(jnp.concatenate([pooled(final_dot), pooled(final_out)])[None])
    feat_all = feats[:, D:]
    logits = einsum("gd,vd->gv", feat_all, table_anchor)
    logit_dot = einsum("gd,vd->gv", feats, both)
    vocab_iota = lax.broadcasted_iota(jnp.int32, logits.shape, 1)
    marks = [vocab_iota == labels[:, word : word + 1] for word in range(NLW)]
    peak_local = jnp.max(logits, axis=1)
    exponent = jnp.exp(logits - peak_local[:, None])
    stats = [peak_local, jnp.sum(exponent, axis=1), jnp.sum(exponent * logit_dot, axis=1)]
    stats += [jnp.sum(jnp.where(mark, logits, 0.0), axis=1) for mark in marks]
    stats += [jnp.sum(jnp.where(mark, logit_dot, 0.0), axis=1) for mark in marks]
    stats += [jnp.zeros_like(peak_local)] * (STATS - len(stats))
    stats = spread(jnp.stack(stats).reshape(1, STATS * count))
    coefficient, log_norm, loss_value = solve(stats, feat_all, targets_all)
    coefficient = coefficient.T
    grad_logits = -jnp.sum(coefficient, axis=1, keepdims=True) * jnp.exp(logits - log_norm.T)
    for word, mark in enumerate(marks):
        grad_logits = grad_logits + jnp.where(mark, coefficient[:, word : word + 1], 0.0)
    grad_logits = grad_logits.astype(LOW)
    grad_feat = einsum("gv,vd->gd", grad_logits, table_anchor)
    grad_feat = jnp.sum(lax.all_to_all(grad_feat, ALL, 0, 0, tiled=True), axis=0)

    grad_final = jnp.where(live[:, None], (grad_feat / length_float)[None, :], 0.0)
    grad_two, gain_two, bias_two_grad = norm_backward(
        grad_final, normed_two, inverse_two, gain_anchor[2]
    )

    def owned(gradient):
        low = gradient.astype(LOW).reshape(n_heads * D, -1)
        return lax.psum_scatter(low, ALL, scatter_dimension=0, tiled=True).astype(jnp.float32)

    grad_ffn = grad_two.astype(LOW)
    grad_down = owned(einsum("td,the->hde", grad_ffn, activated))
    grad_act = einsum("td,hde->the", grad_ffn, down_full)
    grad_pre = (slope * grad_act).astype(LOW)
    grad_up = owned(einsum("td,the->hde", ffn_input, grad_pre))
    grad_hidden = grad_two + einsum("the,hde->td", grad_pre, up_full)
    grad_one, gain_one, bias_one_grad = norm_backward(
        grad_hidden, normed_one, inverse_one, gain_anchor[1]
    )
    grad_attn = grad_one.astype(LOW)
    grad_out = einsum("td,the->hde", grad_attn, attended).astype(LOW)
    grad_att = einsum("td,hde->the", grad_attn, out_full).astype(LOW)
    grad_att = grad_att.reshape(SEQ, n_heads * local_heads, HDIM)
    grad_prob = einsum("qhd,khd->hqk", grad_att, value)
    grad_value = einsum("hqk,qhd->khd", probs_low, grad_att)
    delta_sum = jnp.sum(probs * grad_prob, axis=-1, keepdims=True)
    grad_score = (probs * (grad_prob - delta_sum)).astype(LOW)
    grad_query = einsum("hqk,khd->qhd", grad_score, key) * HDIM ** (-0.5)
    grad_key = einsum("hqk,qhd->khd", grad_score, query) * HDIM ** (-0.5)
    grad_rows = jnp.concatenate(
        [
            part.astype(LOW).reshape(SEQ, n_heads, group_wide)
            for part in (grad_query, grad_key, grad_value)
        ],
        axis=2,
    )
    grad_qkv = einsum("td,the->hde", attn_in, grad_rows).astype(LOW)
    grad_attn_all = owned(jnp.concatenate([grad_qkv, grad_out], axis=2))
    grad_start = grad_one + einsum("the,hde->td", grad_rows, attn_all[:, :, :three])
    grad_embed, gain_zero, bias_zero = norm_backward(
        grad_start, normed_zero, inverse_zero, gain_anchor[0]
    )
    grad_embed = grad_embed.astype(LOW)
    table_term = einsum("gv,gd->vd", grad_logits, feat_all) + give(0, wanted_first, grad_embed)
    table_grad = more(table_term, lambda turn: give(turn, asked(turn), grad_embed))

    gain_grad, bias_grad = total(
        (
            jnp.stack([gain_zero, gain_one, gain_two]),
            jnp.stack([bias_zero, bias_one_grad, bias_two_grad]),
        )
    )
    squares = sum(jnp.sum(part * part) for part in (table_grad, grad_attn_all, grad_up, grad_down))
    squares = total(squares.reshape(1, 1))[0, 0]
    squares = squares + jnp.sum(gain_grad * gain_grad) + jnp.sum(bias_grad * bias_grad)
    clip_scale = jnp.minimum(1.0, CLIP_NORM / jnp.sqrt(squares))
    steps_done = step_count[0].astype(jnp.float32)
    bias_one = 1.0 - jnp.power(BETA_ONE, steps_done)
    bias_two = 1.0 - jnp.power(BETA_TWO, steps_done)
    rates = (clip_scale, bias_one, bias_two)

    def with_out(qkv, out):
        return jnp.concatenate([qkv, out.T[None]], axis=0)

    height = qkv_delta.shape[1]
    turned = turned_update(
        soap_owners[0] == 1,
        with_out(qkv_delta, out_delta),
        jnp.swapaxes(grad_attn_all.reshape(height, 4, group_wide), 0, 1),
        with_out(qkv_first, out_first),
        with_out(qkv_second, out_second),
        soap_basis,
        *rates,
    )
    return (
        loss_value[0, 0],
        *adam_update(table_delta, table_grad, table_first, table_second, *rates),
        *(part[:3] for part in turned),
        *(part[3].T for part in turned),
        *adam_update(up_delta, grad_up, up_first, up_second, *rates),
        *adam_update(down_delta, grad_down.T, down_first, down_second, *rates),
        *adam_update(gain_delta, gain_grad, gain_first, gain_second, *rates),
        *adam_update(bias_delta, bias_grad, bias_first, bias_second, *rates),
    )


def solution(mesh):
    group = P("rows", None)
    table = P(("heads", "rows"), None)
    qkv = P(None, "rows", "heads")
    tall = P("heads", "rows")
    wide = P("rows", "heads")
    placed = (
        group,
        P("rows"),
        group,
        group,
        P(),
        P("rows"),
        P(None, "heads", None, None),
        *(table,) * 4,
        *(qkv,) * 4,
        *(tall,) * 4,
        *(wide,) * 4,
        *(tall,) * 4,
        *(P(),) * 8,
    )
    return jax.shard_map(
        per_device,
        mesh=mesh,
        in_specs=placed,
        out_specs=(
            P(),
            *(table,) * 3,
            *(qkv,) * 3,
            *(tall,) * 3,
            *(wide,) * 3,
            *(tall,) * 3,
            *(P(),) * 6,
        ),
        check_vma=False,
    )
```

time: 2810 us -> 831 us (0.30)
  blocking collectives: 1020 us -> 26.1 us
  waiting for transfers between devices: 1300 us -> 433 us
  starting transfers between devices: 3.28 us -> 115 us
  local copies, waits for them, and re-layouts: 135 us -> 39.8 us
  other arithmetic: 139 us -> 64.7 us
  matrix products: 166 us -> 107 us
    all_gather x13 -> x3, waiting for transfers between devices: 885 us -> 103 us  [gathered(): full = lax.all_gather(block, ALL, axis=0, tiled=True)]
    psum x17 -> x0, blocking collectives: 466 us -> none  [the longest x8 277 us: per_device(): lax.psum((jnp.dot(features.T, direction, precision=HIGH), jnp.sum(directi...]
    unnamed x3 -> x0, blocking collectives: 387 us -> none
    all_gather x8 -> x1, blocking collectives: 167 us -> 26.1 us  [per_device(): lax.all_gather(notes, 'rows')]
    unnamed x28 -> x6, waiting for transfers between devices: 132 us -> 0.1 us
    ppermute x0 -> x30, starting transfers between devices: none -> 96.9 us  [the longest x20 88.5 us: total(): lax.ppermute(part, axis, pairs)]
    ppermute x0 -> x30, waiting for transfers between devices: none -> 78.6 us  [the longest x20 56.6 us: total(): lax.ppermute(part, axis, pairs)]
    unnamed x230 -> x271, local copies, waits for them, and re-layouts: 80.4 us -> 16.9 us
  transfers between devices with their start and end apart: 26 -> 40, of which waited for: 23 -> 31; matrix products, arithmetic and copies ran while one was open for 6% -> 14% of each run, Pallas kernels for 0% -> 0%
where the time goes in v1:
time: 831 us; the launch traced here: 822 us
  waiting for transfers between devices  433 us (52%)
  starting transfers between devices  115 us (14%)
  matrix products  107 us (13%)
  other arithmetic  64.7 us (8%)
  local copies, waits for them, and re-layouts  39.8 us (5%)
  between operations  29.5 us (4%)
  blocking collectives  26.1 us (3%)
    reduce_scatter x3, waiting for transfers between devices, owned(): lax.psum_scatter(low, ALL, scatter_dimension=0, tiled=True)  246 us
    all_gather x3, waiting for transfers between devices, gathered(): full = lax.all_gather(block, ALL, axis=0, tiled=True)  103 us
    dot_general x33, matrix products, einsum(): return jnp.einsum(form, left, right, preferred_element_type=jnp.float32)  103 us
    ppermute x20, starting transfers between devices, total(): lax.ppermute(part, axis, pairs)  88.5 us
    ppermute x20, waiting for transfers between devices, total(): lax.ppermute(part, axis, pairs)  56.6 us
    all_gather x1, blocking collectives, per_device(): lax.all_gather(notes, 'rows')  26.1 us
    ppermute x10, waiting for transfers between devices, spread(): other = lax.ppermute(block, axis, pairs)  22.1 us
    unnamed x271, local copies, waits for them, and re-layouts  16.9 us
  transfers between devices with their start and end apart: 40, of which 31 were waited for; matrix products, arithmetic and copies ran while one was open for 14% of the time, Pallas kernels for 0%

profile of v1, /device:TPU:0, one launch (start us, length us, event | category | flops | bytes accessed | tf_op | source)
XLA Modules:
  0.0 822.3 jit_solution(10085218036904204716)
XLA Ops:
  17.7 7.3 all-to-all-start.4
  34.2 8.2 %fusion.28 = bf16[768,1536]{1,0:T(8,128)(2,1)} fusion(bf16[1572,1536]{1,0:T(8,128)(2,1)} %pad_maximum_fusion, s32[768]{0:T(1024)S(1)} %eq.255), kind=kOutput, calls=%fused_computation.57 | convolution fusion | flops 3711200256 | bytes 7191552 | tf_op jit(solution)/shard_map/sv,vd->sd/dot_general | solution.py:31
  56.8 48.7 %collective-permute-start.1 = (s32[1,1]{1,0:T(1,128)}, s32[1,1]{1,0:T(1,128)}, u32[]{:S(2)}, u32[]{:S(2)}) collective-permute-start(s32[1,1]{1,0:T(1,128)} %max.15), channel_id=1, source_target_pairs={{0,8},{4,12},{8,0},{12,4},{16,24},{20,28},{24,16},{28,20},{1,9},{5... | collective-permute-start | bytes 20 | tf_op jit(solution)/shard_map/ppermute | solution.py:88
  106.1 5.9 collective-permute-start.2
  112.0 21.9 %collective-permute-done.2 = s32[1,1]{1,0:T(1,128)} collective-permute-done((s32[1,1]{1,0:T(1,128)}, s32[1,1]{1,0:T(1,128)}, u32[]{:S(2)}, u32[]{:S(2)}) %collective-permute-start.2) | collective-permute-done | bytes 36 | tf_op jit(solution)/shard_map/ppermute | solution.py:88
  147.2 5.8 fusion.157
  180.1 35.9 %all-gather.8.cloned.1.call-done = bf16[3072,1536]{1,0:T(8,128)(2,1)} async-done(((bf16[96,1536]{1,0:T(8,128)(2,1)}), bf16[3072,1536]{1,0:T(8,128)(2,1)}) %all-gather.8.cloned.1.call-update) | async-done | bytes 9437200 | tf_op jit(solution)/shard_map/all_gather | solution.py:236
  216.0 5.7 fusion.160
  224.3 7.6 fusion.31
  231.9 67.6 %all-gather.10.cloned.1.call-done = bf16[3072,1536]{1,0:T(8,128)(2,1)} async-done(((bf16[96,1536]{1,0:T(8,128)(2,1)}), bf16[3072,1536]{1,0:T(8,128)(2,1)}) %all-gather.10.cloned.1.call-update) | async-done | bytes 9437200 | tf_op jit(solution)/shard_map/all_gather | solution.py:236
  305.1 9.5 %fusion.69 = f32[256,768]{1,0:T(8,128)} fusion(bf16[4,768,1536]{2,1,0:T(8,128)(2,1)} %bitcast.383, f32[256,4,1536]{2,0,1:T(8,128)} %copy-done.3, bf16[4,768,1536]{2,1,0:T(8,128)(2,1)} %bitcast.322, f32[256,768]{1,0:T(8,128)S(1)} %copy-done.127, f32[768]{0:T(1024)S(1)} %get-tuple-element.436, f32[768]{0:T(1024)S(1)} %get-tuple-element.557, ...), kind=kOutput, calls=%fused_computation.117 | convolution fusion | flops 2426732544 | bytes 18101248 | tf_op jit(solution)/shard_map/the,hde->td/dot_general | solution.py:31
  314.7 5.6 fusion.183
  330.3 26.1 %all-gather.1 = f32[8,4,8]{2,1,0:T(4,128)S(1)} all-gather(f32[1,4,8]{2,1,0:T(4,128)S(1)} %maximum_bitcast_fusion), channel_id=2, replica_groups=mesh['rows'=8,'heads'=4] {'rows'}, dimensions={0}, use_global_device_ids=true | all-gather | bytes 1152 | tf_op jit(solution)/shard_map/all_gather | solution.py:312
  385.2 6.8 shard_map.498
  411.9 5.3 multiply_reduce_fusion.3
  428.8 6.6 copy.213
  441.4 5.4 convolution_convert_fusion.1
  460.7 5.2 collective-permute-done.25
  471.4 6.9 collective-permute-done.26
  483.2 10.6 %collective-permute-done.27 = f32[3,768]{1,0:T(4,128)S(1)} collective-permute-done((f32[3,768]{1,0:T(4,128)S(1)}, f32[3,768]{1,0:T(4,128)S(1)}, u32[]{:S(2)}, u32[]{:S(2)}) %collective-permute-start.27) | collective-permute-done | bytes 9248 | tf_op jit(solution)/shard_map/ppermute | solution.py:88
  515.1 27.3 %reduce-scatter.4.cloned.1.call-done = bf16[96,768]{1,0:T(8,128)(2,1)} async-done(((bf16[3072,768]{1,0:T(8,128)(2,1)}), bf16[96,768]{1,0:T(8,128)(2,1)}) %reduce-scatter.4.cloned.1.call-update) | async-done | bytes 147472 | tf_op jit(solution)/shard_map/reduce_scatter | solution.py:417
  545.3 109.5 %reduce-scatter.6.cloned.1.call-done = bf16[96,768]{1,0:T(8,128)(2,1)} async-done(((bf16[3072,768]{1,0:T(8,128)(2,1)}), bf16[96,768]{1,0:T(8,128)(2,1)}) %reduce-scatter.6.cloned.1.call-update) | async-done | bytes 147472 | tf_op jit(solution)/shard_map/reduce_scatter | solution.py:417
  657.0 109.5 %reduce-scatter.8.cloned.1.call-done = bf16[96,768]{1,0:T(8,128)(2,1)} async-done(((bf16[3072,768]{1,0:T(8,128)(2,1)}), bf16[96,768]{1,0:T(8,128)(2,1)}) %reduce-scatter.8.cloned.1.call-update) | async-done | bytes 147472 | tf_op jit(solution)/shard_map/reduce_scatter | solution.py:417
  798.1 13.5 %multiply_subtract_fusion = (f32[1572,768]{1,0:T(8,128)}, f32[1572,768]{1,0:T(8,128)}, f32[1572,768]{1,0:T(8,128)}) fusion(f32[1572,768]{1,0:T(8,128)} %param.51, f32[]{:T(128)} %bitcast.109, f32[]{:T(128)} %bitcast.108, f32[1572,768]{1,0:T(8,128)} %get-tuple-element.736, f32[]{:T(128)S(6)} %min.3, f32[1572,768]{1,0:T(8,128)} %param.53, f32[1572,768]{1,0:T(8,128)} %param.52), kind=kLoop, calls=%fused_computation.33 | loop fusion | flops 19316736 | bytes 33804300 | tf_op jit(solution)/shard_map/sub | solution.py:167
  (510 shorter events, 230.5 us)
Async XLA Ops:
  7.2 140.0 %all-gather.6.cloned.1.call-start = ((), (), s32[]{:S(2)}) async-start(), calls=%async_computation.11 | async-start | bytes 9732096 | tf_op jit(solution)/shard_map/all_gather | solution.py:236
  12.0 203.9 %all-gather.8.cloned.1.call-start = ((), (), s32[]{:S(2)}) async-start(), calls=%async_computation.12 | async-start | bytes 9732096 | tf_op jit(solution)/shard_map/all_gather | solution.py:236
  14.7 284.7 %all-gather.10.cloned.1.call-start = ((), (), s32[]{:S(2)}) async-start(), calls=%async_computation.13 | async-start | bytes 9732096 | tf_op jit(solution)/shard_map/all_gather | solution.py:236
  17.7 14.6 %all-to-all-start.4 = ((s32[32,1,24]{2,1,0:T(1,128)}), s32[32,1,24]{2,1,0:T(1,128)S(1)}, u32[]{:S(2)}, u32[]{:S(2)}) async-start(s32[32,1,24]{2,1,0:T(1,128)} %bitcast.16), calls=%async_computation.4 | async-start | bytes 32768 | tf_op jit(solution)/shard_map/all_to_all | solution.py:269
  42.4 98.4 %all-to-all-start.5 = ((bf16[32,24,1536]{2,1,0:T(8,128)(2,1)}), bf16[32,24,1536]{2,1,0:T(8,128)(2,1)S(1)}, u32[]{:S(2)}, u32[]{:S(2)}) async-start(bf16[32,24,1536]{2,1,0:T(8,128)(2,1)} %bitcast.333), calls=%async_computation.5 | async-start | bytes 4718592 | tf_op jit(solution)/shard_map/all_to_all | solution.py:282
  48.0 8.2 collective-permute-start
  56.8 48.7 %collective-permute-start.1 = (s32[1,1]{1,0:T(1,128)}, s32[1,1]{1,0:T(1,128)}, u32[]{:S(2)}, u32[]{:S(2)}) collective-permute-start(s32[1,1]{1,0:T(1,128)} %max.15), channel_id=1, source_target_pairs={{0,8},{4,12},{8,0},{12,4},{16,24},{20,28},{24,16},{28,20},{1,9},{5... | collective-permute-start | bytes 20 | tf_op jit(solution)/shard_map/ppermute | solution.py:88
  106.1 27.8 %collective-permute-start.2 = (s32[1,1]{1,0:T(1,128)}, s32[1,1]{1,0:T(1,128)}, u32[]{:S(2)}, u32[]{:S(2)}) collective-permute-start(s32[1,1]{1,0:T(1,128)} %max.16), channel_id=1, source_target_pairs={{0,16},{4,20},{8,24},{12,28},{16,0},{20,4},{24,8},{28,12},{1,17},{... | collective-permute-start | bytes 20 | tf_op jit(solution)/shard_map/ppermute | solution.py:88
  328.4 28.2 %collective-permute-start.7 = (bf16[4,1536]{1,0:T(4,128)(2,1)S(1)}, bf16[4,1536]{1,0:T(4,128)(2,1)S(1)}, u32[]{:S(2)}, u32[]{:S(2)}) collective-permute-start(bf16[4,1536]{1,0:T(4,128)(2,1)S(1)} %maximum_select_fusion.6), channel_id=1, source_target_pairs={{0,16},{4,20},{8,24},{12,28},{16,0},{20,4},{24,8},{28,12},{1,17},{... | collective-permute-start | bytes 36872 | tf_op jit(solution)/shard_map/ppermute | solution.py:75
  374.8 4.6 collective-permute-start.12
  395.6 10.3 %all-to-all-start.6 = ((f32[32,1,768]{2,1,0:T(1,128)}), f32[32,1,768]{2,1,0:T(1,128)S(1)}, u32[]{:S(2)}, u32[]{:S(2)}) async-start(f32[32,1,768]{2,1,0:T(1,128)} %copy.207), calls=%async_computation.6 | async-start | bytes 196608 | tf_op jit(solution)/shard_map/all_to_all | solution.py:408
  398.4 144.0 %reduce-scatter.4.cloned.1.call-start = ((), (), s32[]{:S(2)}) async-start(), calls=%async_computation.14 | async-start | bytes 4866048 | tf_op jit(solution)/shard_map/reduce_scatter | solution.py:417
  435.4 219.3 %reduce-scatter.6.cloned.1.call-start = ((), (), s32[]{:S(2)}) async-start(), calls=%async_computation.15 | async-start | bytes 4866048 | tf_op jit(solution)/shard_map/reduce_scatter | solution.py:417
  440.7 325.8 %reduce-scatter.8.cloned.1.call-start = ((), (), s32[]{:S(2)}) async-start(), calls=%async_computation.16 | async-start | bytes 4866048 | tf_op jit(solution)/shard_map/reduce_scatter | solution.py:417
  455.7 48.9 %all-to-all-start.7 = ((bf16[32,24,768]{2,1,0:T(8,128)(2,1)}), bf16[32,24,768]{2,1,0:T(8,128)(2,1)S(1)}, u32[]{:S(2)}, u32[]{:S(2)}) async-start(bf16[32,24,768]{2,1,0:T(8,128)(2,1)} %bitcast.94), calls=%async_computation.7 | async-start | bytes 2359296 | tf_op jit(solution)/shard_map/all_to_all | solution.py:287
  458.5 7.5 collective-permute-start.25
  460.3 10.9 %collective-permute-start.20 = (f32[3,768]{1,0:T(4,128)S(1)}, f32[3,768]{1,0:T(4,128)S(1)}, u32[]{:S(2)}, u32[]{:S(2)}) collective-permute-start(f32[3,768]{1,0:T(4,128)S(1)} %pad_maximum_fusion.8), channel_id=1, source_target_pairs={{0,4},{4,0},{8,12},{12,8},{16,20},{20,16},{24,28},{28,24},{1,5},{5... | collective-permute-start | bytes 27656 | tf_op jit(solution)/shard_map/ppermute | solution.py:88
  466.0 12.4 %collective-permute-start.26 = (f32[3,768]{1,0:T(4,128)S(1)}, f32[3,768]{1,0:T(4,128)S(1)}, u32[]{:S(2)}, u32[]{:S(2)}) collective-permute-start(f32[3,768]{1,0:T(4,128)S(1)} %fusion.170), channel_id=1, source_target_pairs={{0,8},{4,12},{8,0},{12,4},{16,24},{20,28},{24,16},{28,20},{1,9},{5... | collective-permute-start | bytes 27656 | tf_op jit(solution)/shard_map/ppermute | solution.py:88
  471.2 11.9 %collective-permute-start.21 = (f32[3,768]{1,0:T(4,128)S(1)}, f32[3,768]{1,0:T(4,128)S(1)}, u32[]{:S(2)}, u32[]{:S(2)}) collective-permute-start(f32[3,768]{1,0:T(4,128)S(1)} %fusion.171), channel_id=1, source_target_pairs={{0,8},{4,12},{8,0},{12,4},{16,24},{20,28},{24,16},{28,20},{1,9},{5... | collective-permute-start | bytes 27656 | tf_op jit(solution)/shard_map/ppermute | solution.py:88
  478.4 15.5 %collective-permute-start.27 = (f32[3,768]{1,0:T(4,128)S(1)}, f32[3,768]{1,0:T(4,128)S(1)}, u32[]{:S(2)}, u32[]{:S(2)}) collective-permute-start(f32[3,768]{1,0:T(4,128)S(1)} %fusion.249), channel_id=1, source_target_pairs={{0,16},{4,20},{8,24},{12,28},{16,0},{20,4},{24,8},{28,12},{1,17},{... | collective-permute-start | bytes 27656 | tf_op jit(solution)/shard_map/ppermute | solution.py:88
  483.1 11.2 %collective-permute-start.22 = (f32[3,768]{1,0:T(4,128)S(1)}, f32[3,768]{1,0:T(4,128)S(1)}, u32[]{:S(2)}, u32[]{:S(2)}) collective-permute-start(f32[3,768]{1,0:T(4,128)S(1)} %fusion.250), channel_id=1, source_target_pairs={{0,16},{4,20},{8,24},{12,28},{16,0},{20,4},{24,8},{28,12},{1,17},{... | collective-permute-start | bytes 27656 | tf_op jit(solution)/shard_map/ppermute | solution.py:88
  494.9 4.7 collective-permute-start.23
  495.6 4.7 collective-permute-start.29
  777.5 4.6 collective-permute-start.17
  (147 other events, 4288.4 us)
Sparse Core Ops, SparseCore 0:
  12.2 121.4 all-gather.5
  137.1 78.7 all-gather.7
  219.4 79.9 all-gather.9
  435.5 106.7 reduce-scatter.3
  548.3 106.4 reduce-scatter.5
  660.1 106.3 reduce-scatter.7

commit v2 on v1

--- a/solution.py
+++ b/solution.py
@@ -60,34 +60,42 @@
     return (grad_in, jnp.sum(grad_out * normed, axis=0), jnp.sum(grad_out, axis=0))
 
 
-def partners(axis):
-    size = lax.axis_size(axis)
-    bit = 1
-    while bit < size:
-        yield bit, [(index, index ^ bit) for index in range(size)]
-        bit *= 2
-
-
-def spread(block):
-    for axis in reversed(ALL):
-        here = lax.axis_index(axis)
-        for bit, pairs in partners(axis):
-            other = lax.ppermute(block, axis, pairs)
-            block = jnp.where(
-                (here & bit) > 0,
-                jnp.concatenate([other, block]),
-                jnp.concatenate([block, other]),
-            )
-    return block
-
-
-def total(values, combine=jnp.add):
-    for axis in reversed(ALL):
-        for _, pairs in partners(axis):
-            values = jax.tree.map(
-                lambda part: combine(part, lax.ppermute(part, axis, pairs)), values
-            )
-    return values
+def everyone(block):
+    count = lax.axis_size(ALL[0]) * lax.axis_size(ALL[1])
+    return lax.all_to_all(
+        jnp.broadcast_to(block, (count, block.shape[1])), ALL, 0, 0, tiled=True
+    )
+
+
+def bits_of(axis):
+    return [(axis, bit) for bit in reversed(range(lax.axis_size(axis).bit_length() - 1))]
+
+
+def owned(parts):
+    layout = [bit for axis in ALL for bit in bits_of(axis)]
+    first = (ALL[0], 0)
+    last = [bit for bit in layout if bit[0] == ALL[1] and bit[1] >= 2]
+    middle = [bit for bit in layout if bit != first and bit not in last]
+    results = []
+    for turn, part in enumerate(parts):
+        turn %= len(middle)
+        order = [first] + middle[turn:] + middle[:turn] + last[::-1]
+        left = list(layout)
+        block = part.reshape((2,) * len(layout) + (-1, part.shape[-1]))
+        for step in order:
+            axis, bit = step
+            place = left.index(step)
+            mine = (lax.axis_index(axis) >> bit) & 1
+            send = lax.dynamic_index_in_dim(block, 1 - mine, place, keepdims=False)
+            keep = lax.dynamic_index_in_dim(block, mine, place, keepdims=False)
+            size = lax.axis_size(axis)
+            came = lax.ppermute(send, axis, [(index, index ^ (1 << bit)) for index in range(size)])
+            block = keep.astype(jnp.float32) + came.astype(jnp.float32)
+            left.pop(place)
+            if left:
+                block = block.astype(LOW)
+        results.append(block)
+    return results
 
 
 def solve_kernel(stats_ref, feat_ref, targets_ref, coef_ref, norm_ref, loss_ref):
@@ -237,8 +245,10 @@
         return full.reshape(n_heads, D, block.shape[1])
 
     attn_all = gathered(side_by_side(qkv_anchor, out_anchor), side_by_side(qkv_delta, out_delta))
-    up_all = gathered(up_anchor, up_delta)
-    down_all = gathered(down_anchor.T, down_delta.T)
+    ffn_all = gathered(
+        jnp.concatenate([up_anchor, down_anchor.T], axis=1),
+        jnp.concatenate([up_delta, down_delta.T], axis=1),
+    )
 
     room = 8 * -(-(2 * SEQ // count + 8) // 8)
     slots = count * room
@@ -255,19 +265,24 @@
         dtype=jnp.int32,
     )
     longest = jnp.max(rank) + 1
-    rounds = -(-total(longest.reshape(1, 1), jnp.maximum)[0, 0] // room)
+    own_labels = lax.dynamic_index_in_dim(label_ids, head_index, 0, keepdims=False)
+    own_targets = lax.dynamic_index_in_dim(targets, head_index, 0, keepdims=False)
+    notes = jnp.concatenate(
+        [longest[None].astype(jnp.float32), own_labels.astype(jnp.float32), own_targets]
+    )
     both = jnp.concatenate([table_anchor, table_delta.astype(LOW)], axis=1)
 
     def slot_of(turn):
         within = rank - turn * room
         return jnp.where((within >= 0) & (within < room), owner * room + within, -1)
 
-    def asked(turn):
+    def wanted_of(turn):
         taken = jnp.where(leads, slot_of(turn), -1)
         hit = lax.iota(jnp.int32, slots)[:, None] == taken[None, :]
-        wanted = jnp.sum(jnp.where(hit, local[None, :] + 1, 0), axis=1) - 1
-        wanted = lax.all_to_all(wanted.reshape(count, room), ALL, 0, 0, tiled=True)
-        return wanted.reshape(slots)
+        return (jnp.sum(jnp.where(hit, local[None, :] + 1, 0), axis=1) - 1).reshape(count, room)
+
+    def asked(turn):
+        return lax.all_to_all(wanted_of(turn), ALL, 0, 0, tiled=True).reshape(slots)
 
     def chosen(wanted):
         return (wanted[:, None] == lax.broadcasted_iota(jnp.int32, (slots, vocab), 1)).astype(LOW)
@@ -293,7 +308,18 @@
 
         return lax.cond(rounds > 1, rest, lambda value: value, start)
 
-    wanted_first = asked(0)
+    message = jnp.concatenate(
+        [
+            wanted_of(0).astype(jnp.float32),
+            jnp.broadcast_to(notes[None], (count, notes.shape[0])),
+        ],
+        axis=1,
+    )
+    message = lax.all_to_all(message, ALL, 0, 0, tiled=True)
+    wanted_first = message[:, :room].astype(jnp.int32).reshape(slots)
+    rounds = -(-jnp.max(message[:, room]).astype(jnp.int32) // room)
+    labels = message[:, room + 1 : room + 1 + NLW].astype(jnp.int32) - me * vocab
+    targets_all = message[:, room + 1 + NLW :].T
     embedded_both = more(fetch(0, wanted_first), lambda turn: fetch(turn, asked(turn)))
     start_x, start_dot, normed_zero, inverse_zero = norm_pair(
         embedded_both[:, :D],
@@ -307,11 +333,6 @@
     own_length = lax.dynamic_index_in_dim(lengths, head_index, 0, keepdims=False)
     live = lax.iota(jnp.int32, SEQ) < own_length
     length_float = own_length.astype(jnp.float32)
-
-    notes = jnp.concatenate([label_ids.astype(jnp.float32), targets], axis=1)
-    notes = jnp.swapaxes(lax.all_gather(notes, "rows"), 0, 1).reshape(count, 2 * NLW)
-    labels = notes[:, :NLW].astype(jnp.int32) - me * vocab
-    targets_all = notes[:, NLW:].T
 
     attn_in = start_x.astype(LOW)
     attn_dot_in = start_dot.astype(LOW)
@@ -360,18 +381,17 @@
         bias_delta[1],
     )
     ffn_input = hidden.astype(LOW)
-    half = up_all.shape[2] // 2
-    up_full = up_all[:, :, :half]
-    down_full = down_all[:, :, :half]
-    through = einsum("td,hde->the", ffn_input, up_all)
-    pre_gelu = through[:, :, :half]
-    pre_dot = through[:, :, half:] + einsum("td,hde->the", hidden_dot.astype(LOW), up_full)
+    up_full, down_full, up_step, down_step = jnp.split(ffn_all, 4, axis=2)
+    pre_gelu = einsum("td,hde->the", ffn_input, up_full)
+    pre_dot = einsum("td,hde->the", hidden_dot.astype(LOW), up_full) + einsum(
+        "td,hde->the", ffn_input, up_step
+    )
     activated = jax.nn.gelu(pre_gelu, approximate=False).astype(LOW)
     slope = gelu_slope(pre_gelu)
     act_dot = (slope * pre_dot).astype(LOW)
     ffn_out = einsum("the,hde->td", activated, down_full)
     ffn_dot = einsum("the,hde->td", act_dot, down_full) + einsum(
-        "the,hde->td", activated, down_all[:, :, half:]
+        "the,hde->td", activated, down_step
     )
     final_out, final_dot, normed_two, inverse_two = norm_pair(
         hidden + ffn_out,
@@ -385,7 +405,7 @@
     def pooled(values):
         return (jnp.sum(jnp.where(live[:, None], values, 0.0), axis=0) / length_float).astype(LOW)
 
-    feats = spread(jnp.concatenate([pooled(final_dot), pooled(final_out)])[None])
+    feats = everyone(jnp.concatenate([pooled(final_dot), pooled(final_out)])[None])
     feat_all = feats[:, D:]
     logits = einsum("gd,vd->gv", feat_all, table_anchor)
     logit_dot = einsum("gd,vd->gv", feats, both)
@@ -397,7 +417,7 @@
     stats += [jnp.sum(jnp.where(mark, logits, 0.0), axis=1) for mark in marks]
     stats += [jnp.sum(jnp.where(mark, logit_dot, 0.0), axis=1) for mark in marks]
     stats += [jnp.zeros_like(peak_local)] * (STATS - len(stats))
-    stats = spread(jnp.stack(stats).reshape(1, STATS * count))
+    stats = everyone(jnp.stack(stats).reshape(1, STATS * count))
     coefficient, log_norm, loss_value = solve(stats, feat_all, targets_all)
     coefficient = coefficient.T
     grad_logits = -jnp.sum(coefficient, axis=1, keepdims=True) * jnp.exp(logits - log_norm.T)
@@ -412,15 +432,11 @@
         grad_final, normed_two, inverse_two, gain_anchor[2]
     )
 
-    def owned(gradient):
-        low = gradient.astype(LOW).reshape(n_heads * D, -1)
-        return lax.psum_scatter(low, ALL, scatter_dimension=0, tiled=True).astype(jnp.float32)
-
     grad_ffn = grad_two.astype(LOW)
-    grad_down = owned(einsum("td,the->hde", grad_ffn, activated))
+    grad_down = einsum("td,the->hde", grad_ffn, activated).astype(LOW)
     grad_act = einsum("td,hde->the", grad_ffn, down_full)
     grad_pre = (slope * grad_act).astype(LOW)
-    grad_up = owned(einsum("td,the->hde", ffn_input, grad_pre))
+    grad_up = einsum("td,the->hde", ffn_input, grad_pre).astype(LOW)
     grad_hidden = grad_two + einsum("the,hde->td", grad_pre, up_full)
     grad_one, gain_one, bias_one_grad = norm_backward(
         grad_hidden, normed_one, inverse_one, gain_anchor[1]
@@ -443,7 +459,8 @@
         axis=2,
     )
     grad_qkv = einsum("td,the->hde", attn_in, grad_rows).astype(LOW)
-    grad_attn_all = owned(jnp.concatenate([grad_qkv, grad_out], axis=2))
+    grad_attn_all = jnp.concatenate([grad_qkv, grad_out], axis=2)
+    grad_down, grad_up, grad_attn_all = owned([grad_down, grad_up, grad_attn_all])
     grad_start = grad_one + einsum("the,hde->td", grad_rows, attn_all[:, :, :three])
     grad_embed, gain_zero, bias_zero = norm_backward(
         grad_start, normed_zero, inverse_zero, gain_anchor[0]
@@ -452,15 +469,16 @@
     table_term = einsum("gv,gd->vd", grad_logits, feat_all) + give(0, wanted_first, grad_embed)
     table_grad = more(table_term, lambda turn: give(turn, asked(turn), grad_embed))
 
-    gain_grad, bias_grad = total(
-        (
-            jnp.stack([gain_zero, gain_one, gain_two]),
-            jnp.stack([bias_zero, bias_one_grad, bias_two_grad]),
-        )
-    )
-    squares = sum(jnp.sum(part * part) for part in (table_grad, grad_attn_all, grad_up, grad_down))
-    squares = total(squares.reshape(1, 1))[0, 0]
-    squares = squares + jnp.sum(gain_grad * gain_grad) + jnp.sum(bias_grad * bias_grad)
+    norm_grads = jnp.stack(
+        [gain_zero, gain_one, gain_two, bias_zero, bias_one_grad, bias_two_grad]
+    )
+    pieces = lax.all_to_all(norm_grads.reshape(count, -1), ALL, 0, 0, tiled=True)
+    piece = jnp.sum(pieces, axis=0, keepdims=True)
+    gain_grad, bias_grad = everyone(piece).reshape(2, 3, D)
+    squares = sum(
+        jnp.sum(part * part) for part in (table_grad, grad_attn_all, grad_up, grad_down, piece)
+    )
+    squares = jnp.sum(everyone(jnp.broadcast_to(squares, (1, 128)))[:, 0])
     clip_scale = jnp.minimum(1.0, CLIP_NORM / jnp.sqrt(squares))
     steps_done = step_count[0].astype(jnp.float32)
     bias_one = 1.0 - jnp.power(BETA_ONE, steps_done)

time: 831 us -> 569 us (0.68)
  waiting for transfers between devices: 433 us -> 242 us
  starting transfers between devices: 115 us -> 45 us
  blocking collectives: 26.1 us -> 0 us
  local copies, waits for them, and re-layouts: 39.8 us -> 65.8 us
  other arithmetic: 64.7 us -> 76.8 us
  matrix products: 107 us -> 98.3 us
    reduce_scatter x3 -> x0, waiting for transfers between devices: 246 us -> none  [owned(): lax.psum_scatter(low, ALL, scatter_dimension=0, tiled=True)]
    all_to_all x1, waiting for transfers between devices: 0.01 us -> 84.5 us  [fetch(): lax.all_to_all(rows.reshape(count, room, 2 * D), ALL, 0, 0, tiled=True)]
    ppermute x30 -> x15, starting transfers between devices: 96.9 us -> 12.6 us  [owned(): lax.ppermute(send, axis, [(index, index ^ 1 << bit) for index in range(si...]
    ppermute x30 -> x15, waiting for transfers between devices: 78.6 us -> 44.8 us  [owned(): lax.ppermute(send, axis, [(index, index ^ 1 << bit) for index in range(si...]
    all_gather x1 -> x0, blocking collectives: 26.1 us -> none  [per_device(): lax.all_gather(notes, 'rows')]
    all_gather x3 -> x2, waiting for transfers between devices: 103 us -> 80.5 us  [gathered(): full = lax.all_gather(block, ALL, axis=0, tiled=True)]
    all_to_all x1 -> x6, waiting for transfers between devices: 1.54 us -> 24.5 us  [the longest x4 19.2 us: everyone(): lax.all_to_all(jnp.broadcast_to(block, (count, block.shape[1])), ALL, 0,...]
    all_to_all x1 -> x6, starting transfers between devices: 7.33 us -> 21.7 us  [the longest x4 11.4 us: everyone(): lax.all_to_all(jnp.broadcast_to(block, (count, block.shape[1])), ALL, 0,...]
  transfers between devices with their start and end apart: 40 -> 26, of which waited for: 31 -> 19; matrix products, arithmetic and copies ran while one was open for 14% -> 23% of each run, Pallas kernels for 0% -> 0%
where the time goes in v2:
time: 569 us; the launch traced here: 559 us
  waiting for transfers between devices  242 us (43%)
  matrix products  98.3 us (17%)
  other arithmetic  76.8 us (13%)
  local copies, waits for them, and re-layouts  65.8 us (12%)
  starting transfers between devices  45 us (8%)
  between operations  23.7 us (4%)
  Pallas kernels  6.8 us (1%)
    dot_general x34, matrix products, einsum(): return jnp.einsum(form, left, right, preferred_element_type=jnp.float32)  93.6 us
    all_to_all x1, waiting for transfers between devices, fetch(): lax.all_to_all(rows.reshape(count, room, 2 * D), ALL, 0, 0, tiled=True)  84.5 us
    all_gather x2, waiting for transfers between devices, gathered(): full = lax.all_gather(block, ALL, axis=0, tiled=True)  80.5 us
    ppermute x15, waiting for transfers between devices, owned(): lax.ppermute(send, axis, [(index, index ^ 1 << bit) for index in range(si...  44.8 us
    all_to_all x4, waiting for transfers between devices, everyone(): lax.all_to_all(jnp.broadcast_to(block, (count, block.shape[1])), ALL, 0,...  19.2 us
    sub x5, other arithmetic, adam_update(): master - LEARN_RATE * (direction + DECAY_RATE * master)  16.9 us
    unnamed x247, local copies, waits for them, and re-layouts  15.3 us
    convert_element_type x12, other arithmetic, owned(): block = block.astype(LOW)  12.8 us
  transfers between devices with their start and end apart: 26, of which 19 were waited for; matrix products, arithmetic and copies ran while one was open for 23% of the time, Pallas kernels for 0%

profile of v2, /device:TPU:0, one launch (start us, length us, event | category | flops | bytes accessed | tf_op | source)
XLA Modules:
  0.0 559.0 jit_solution(10037568801378268718)
XLA Ops:
  19.8 7.3 %all-to-all-start.4 = ((f32[32,1,33]{2,1,0:T(1,128)}), f32[32,1,33]{2,1,0:T(1,128)S(1)}, u32[]{:S(2)}, u32[]{:S(2)}) async-start(f32[32,1,33]{2,1,0:T(1,128)} %bitcast.17), calls=%async_computation.4 | async-start | bytes 32768 | tf_op jit(solution)/shard_map/all_to_all | solution.py:318
  34.5 8.3 %fusion.35 = bf16[768,1536]{1,0:T(8,128)(2,1)} fusion(bf16[1572,1536]{1,0:T(8,128)(2,1)} %pad_maximum_fusion, s32[768]{0:T(1024)S(1)} %eq.255), kind=kOutput, calls=%fused_computation.67 | convolution fusion | flops 3711200256 | bytes 7191552 | tf_op jit(solution)/shard_map/sv,vd->sd/dot_general | solution.py:31
  42.8 4.5 all-to-all-start.5
  50.8 84.5 %all-to-all-done.5 = bf16[32,24,1536]{2,1,0:T(8,128)(2,1)S(1)} async-done(((bf16[32,24,1536]{2,1,0:T(8,128)(2,1)}), bf16[32,24,1536]{2,1,0:T(8,128)(2,1)S(1)}, u32[]{:S(2)}, u32[]{:S(2)}) %all-to-all-start.5) | async-done | bytes 2359328 | tf_op jit(solution)/shard_map/all_to_all | solution.py:297
  141.6 5.8 %fusion.188 = f32[256,4,1536]{2,0,1:T(8,128)S(1)} fusion(bf16[4,768,1536]{2,1,0:T(8,128)(2,1)} %bitcast.407, f32[768]{0:T(1024)S(1)} %get-tuple-element.489, f32[768]{0:T(1024)S(1)} %get-tuple-element.602, f32[256,1536]{1,0:T(8,128)} %get-tuple-element.784, f32[256]{0:T(256)S(1)} %add_rsqrt_fusion.2, f32[256]{0:T(256)S(1)} %broadcast_multiply_fusion.14), kind=kOutput, calls=%fused_computation.332 | convolution fusion | flops 2416902144 | bytes 16523264 | tf_op jit(solution)/shard_map/td,hde->the/dot_general | solution.py:31
  177.0 80.4 %all-gather.5.cloned.1.call-done = bf16[3072,3072]{1,0:T(8,128)(2,1)} async-done(((bf16[96,3072]{1,0:T(8,128)(2,1)}), bf16[3072,3072]{1,0:T(8,128)(2,1)}) %all-gather.5.cloned.1.call-update) | async-done | bytes 18874384 | tf_op jit(solution)/shard_map/all_gather | solution.py:244
  257.4 4.5 fusion.133
  262.0 7.6 %fusion.38 = bf16[256,4,768]{2,0,1:T(8,128)(2,1)S(1)} fusion(f32[256,4,768]{2,0,1:T(8,128)S(1)} %get-tuple-element.587, u8[256,768]{1,0:T(8,128)(4,1)S(1)} %get-tuple-element.447, u8[256,768]{1,0:T(8,128)(4,1)S(1)} %get-tuple-element.446), kind=kLoop, calls=%fused_computation.70 | loop fusion | flops 55050240 | bytes 5111808 | tf_op jit(solution)/shard_map/convert_element_type | solution.py:389
  276.8 10.3 %fusion.213 = (f32[256]{0:T(256)S(1)}, f32[256]{0:T(256)S(1)}, f32[256,768]{1,0:T(8,128)}) fusion(f32[256]{0:T(256)S(1)} %add_rsqrt_fusion, f32[256,768]{1,0:T(8,128)S(1)} %get-tuple-element.589, f32[256]{0:T(256)S(1)} %broadcast_multiply_fusion.12, f32[256,768]{1,0:T(8,128)} %fusion.86, bf16[4,768,3072]{2,1,0:T(8,128)(2,1)} %bitcast.485, ...), kind=kOutput, calls=%fused_computation.408 | convolution fusion | flops 2430074368 | bytes 21270528 | tf_op jit(solution)/shard_map/the,hde->td/dot_general | solution.py:31
  295.2 7.0 %all-to-all-done.6 = bf16[32,2,768]{2,1,0:T(2,128)(2,1)S(1)} async-done(((bf16[32,2,768]{2,1,0:T(2,128)(2,1)}), bf16[32,2,768]{2,1,0:T(2,128)(2,1)S(1)}, u32[]{:S(2)}, u32[]{:S(2)}) %all-to-all-start.6) | async-done | bytes 98336 | tf_op jit(solution)/shard_map/all_to_all | solution.py:65
  303.8 4.8 select_reduce_fusion.7
  319.7 6.0 %all-to-all-done.7 = f32[32,1,512]{2,1,0:T(1,128)} async-done(((f32[32,1,512]{2,1,0:T(1,128)}), f32[32,1,512]{2,1,0:T(1,128)}, u32[]{:S(2)}, u32[]{:S(2)}) %all-to-all-start.7) | async-done | bytes 65568 | tf_op jit(solution)/shard_map/all_to_all | solution.py:65
  327.2 6.8 %shard_map.498 = (f32[4,32]{1,0:T(4,128)}, f32[1,32]{1,0:T(1,128)}, f32[1,1]{1,0:T(1,128)}) custom-call(f32[32,512]{1,0:T(8,128)} %bitcast.453, bf16[32,768]{1,0:T(8,128)(2,1)} %slice.234.feat_ref, f32[4,32]{1,0:T(4,128)} %slice_bitcast_fusion.9.targets_ref), custom_call_target="tpu_custom_call" | custom-call | tf_op jit(solution)/shard_map/pallas_call | solution.py:155
  351.4 4.8 multiply_convert_fusion.1
  391.7 4.3 constant_dynamic-slice_fusion.1
  406.7 6.6 %copy.313 = bf16[4,768,768]{2,1,0:T(8,128)(2,1)} copy(bf16[4,768,768]{1,2,0:T(8,128)(2,1)} %pad_maximum_fusion.1) | data formatting | bytes 9437184 | tf_op jit(solution)/shard_map/concatenate | solution.py:462
  417.4 4.6 all-to-all-done.9
  440.3 4.4 multiply_reduce_fusion
  444.7 11.3 %collective-permute-done.11 = bf16[2,2,2,96,768]{4,3,0,2,1:T(8,128)(2,1)} collective-permute-done((bf16[2,2,2,96,768]{4,3,0,2,1:T(8,128)(2,1)}, bf16[2,2,2,96,768]{4,3,0,2,1:T(8,128)(2,1)}, u32[]{:S(2)}, u32[]{:S(2)}) %collective-permute-start.11) | collective-permute-done | bytes 1179680 | tf_op jit(solution)/shard_map/ppermute | solution.py:92
  468.6 4.8 collective-permute-done.12
  474.4 4.4 collective-permute-done.7
  494.3 11.8 %collective-permute-done.4 = bf16[96,768]{1,0:T(8,128)(2,1)S(1)} collective-permute-done((bf16[96,768]{1,0:T(8,128)(2,1)S(1)}, bf16[96,768]{1,0:T(8,128)(2,1)S(1)}, u32[]{:S(2)}, u32[]{:S(2)}) %collective-permute-start.4) | collective-permute-done | bytes 147488 | tf_op jit(solution)/shard_map/ppermute | solution.py:92
  516.6 5.1 all-to-all-done.11
  535.1 13.5 %multiply_subtract_fusion = (f32[1572,768]{1,0:T(8,128)}, f32[1572,768]{1,0:T(8,128)}, f32[1572,768]{1,0:T(8,128)}) fusion(f32[1572,768]{1,0:T(8,128)} %param.51, f32[]{:T(128)} %bitcast.139, f32[]{:T(128)} %bitcast.138, f32[1572,768]{1,0:T(8,128)} %get-tuple-element.785, f32[]{:T(128)S(6)} %min.3, f32[1572,768]{1,0:T(8,128)} %param.53, f32[1572,768]{1,0:T(8,128)} %param.52), kind=kLoop, calls=%fused_computation.33 | loop fusion | flops 19316736 | bytes 33804300 | tf_op jit(solution)/shard_map/sub | solution.py:175
  (478 shorter events, 221.9 us)
Async XLA Ops:
  7.2 134.4 %all-gather.3.cloned.1.call-start = ((), (), s32[]{:S(2)}) async-start(), calls=%async_computation.13 | async-start | bytes 9732096 | tf_op jit(solution)/shard_map/all_gather | solution.py:244
  12.1 245.4 %all-gather.5.cloned.1.call-start = ((), (), s32[]{:S(2)}) async-start(), calls=%async_computation.14 | async-start | bytes 19464192 | tf_op jit(solution)/shard_map/all_gather | solution.py:244
  19.8 14.4 %all-to-all-start.4 = ((f32[32,1,33]{2,1,0:T(1,128)}), f32[32,1,33]{2,1,0:T(1,128)S(1)}, u32[]{:S(2)}, u32[]{:S(2)}) async-start(f32[32,1,33]{2,1,0:T(1,128)} %bitcast.17), calls=%async_computation.4 | async-start | bytes 32768 | tf_op jit(solution)/shard_map/all_to_all | solution.py:318
  42.8 92.4 %all-to-all-start.5 = ((bf16[32,24,1536]{2,1,0:T(8,128)(2,1)}), bf16[32,24,1536]{2,1,0:T(8,128)(2,1)S(1)}, u32[]{:S(2)}, u32[]{:S(2)}) async-start(bf16[32,24,1536]{2,1,0:T(8,128)(2,1)} %bitcast.426), calls=%async_computation.5 | async-start | bytes 4718592 | tf_op jit(solution)/shard_map/all_to_all | solution.py:297
  291.8 10.4 %all-to-all-start.6 = ((bf16[32,2,768]{2,1,0:T(2,128)(2,1)}), bf16[32,2,768]{2,1,0:T(2,128)(2,1)S(1)}, u32[]{:S(2)}, u32[]{:S(2)}) async-start(bf16[32,2,768]{2,1,0:T(2,128)(2,1)} %reshape.600), calls=%async_computation.6 | async-start | bytes 196608 | tf_op jit(solution)/shard_map/all_to_all | solution.py:65
  315.0 10.7 %all-to-all-start.7 = ((f32[32,1,512]{2,1,0:T(1,128)}), f32[32,1,512]{2,1,0:T(1,128)}, u32[]{:S(2)}, u32[]{:S(2)}) async-start(f32[32,1,512]{2,1,0:T(1,128)} %broadcast_in_dim.268), calls=%async_computation.7 | async-start | bytes 131072 | tf_op jit(solution)/shard_map/all_to_all | solution.py:65
  338.8 11.0 %all-to-all-start.8 = ((f32[32,1,768]{2,1,0:T(1,128)}), f32[32,1,768]{2,1,0:T(1,128)}, u32[]{:S(2)}, u32[]{:S(2)}) async-start(f32[32,1,768]{2,1,0:T(1,128)} %copy.307), calls=%async_computation.8 | async-start | bytes 196608 | tf_op jit(solution)/shard_map/all_to_all | solution.py:428
  378.8 10.2 %all-to-all-start.10 = ((f32[32,1,144]{2,1,0:T(1,128)}), f32[32,1,144]{2,1,0:T(1,128)S(1)}, u32[]{:S(2)}, u32[]{:S(2)}) async-start(f32[32,1,144]{2,1,0:T(1,128)} %all_to_all.84), calls=%async_computation.10 | async-start | bytes 65536 | tf_op jit(solution)/shard_map/all_to_all | solution.py:475
  389.0 33.0 %all-to-all-start.9 = ((bf16[32,24,768]{2,1,0:T(8,128)(2,1)}), bf16[32,24,768]{2,1,0:T(8,128)(2,1)S(1)}, u32[]{:S(2)}, u32[]{:S(2)}) async-start(bf16[32,24,768]{2,1,0:T(8,128)(2,1)} %bitcast.93), calls=%async_computation.9 | async-start | bytes 2359296 | tf_op jit(solution)/shard_map/all_to_all | solution.py:302
  397.6 26.8 %collective-permute-start.10 = (bf16[2,2,2,2,96,768]{5,4,1,3,2,0:T(8,128)(2,1)}, bf16[2,2,2,2,96,768]{5,4,1,3,2,0:T(8,128)(2,1)}, u32[]{:S(2)}, u32[]{:S(2)}) collective-permute-start(bf16[2,2,2,2,96,768]{5,4,1,3,2,0:T(8,128)(2,1)} %bitcast.372), channel_id=1, source_target_pairs={{0,1},{1,0},{2,3},{3,2},{4,5},{5,4},{6,7},{7,6},{8,9},{9,8},{10,11... | collective-permute-start | bytes 7077896 | tf_op jit(solution)/shard_map/ppermute | solution.py:92
  401.0 27.7 %collective-permute-start.5 = (bf16[2,2,2,2,96,768]{5,4,1,0,3,2:T(8,128)(2,1)}, bf16[2,2,2,2,96,768]{5,4,1,0,3,2:T(8,128)(2,1)}, u32[]{:S(2)}, u32[]{:S(2)}) collective-permute-start(bf16[2,2,2,2,96,768]{5,4,1,0,3,2:T(8,128)(2,1)} %bitcast.373), channel_id=1, source_target_pairs={{0,1},{1,0},{2,3},{3,2},{4,5},{5,4},{6,7},{7,6},{8,9},{9,8},{10,11... | collective-permute-start | bytes 7077896 | tf_op jit(solution)/shard_map/ppermute | solution.py:92
  416.6 16.1 %collective-permute-start = (bf16[2,2,2,2,96,768]{5,4,3,2,1,0:T(8,128)(2,1)}, bf16[2,2,2,2,96,768]{5,4,3,2,1,0:T(8,128)(2,1)}, u32[]{:S(2)}, u32[]{:S(2)}) collective-permute-start(bf16[2,2,2,2,96,768]{5,4,3,2,1,0:T(8,128)(2,1)} %dynamic-slice_bitcast_fusion), channel_id=1, source_target_pairs={{0,1},{1,0},{2,3},{3,2},{4,5},{5,4},{6,7},{7,6},{8,9},{9,8},{10,11... | collective-permute-start | bytes 7077896 | tf_op jit(solution)/shard_map/ppermute | solution.py:92
  428.1 27.9 %collective-permute-start.11 = (bf16[2,2,2,96,768]{4,3,0,2,1:T(8,128)(2,1)}, bf16[2,2,2,96,768]{4,3,0,2,1:T(8,128)(2,1)}, u32[]{:S(2)}, u32[]{:S(2)}) collective-permute-start(bf16[2,2,2,96,768]{4,3,0,2,1:T(8,128)(2,1)} %dynamic-slice_bitcast_fusion.1), channel_id=1, source_target_pairs={{0,2},{1,3},{2,0},{3,1},{4,6},{5,7},{6,4},{7,5},{8,10},{9,11},{10,... | collective-permute-start | bytes 3538952 | tf_op jit(solution)/shard_map/ppermute | solution.py:92
  432.5 29.2 %collective-permute-start.6 = (bf16[2,2,2,96,768]{4,3,1,0,2:T(8,128)(2,1)}, bf16[2,2,2,96,768]{4,3,1,0,2:T(8,128)(2,1)}, u32[]{:S(2)}, u32[]{:S(2)}) collective-permute-start(bf16[2,2,2,96,768]{4,3,1,0,2:T(8,128)(2,1)} %dynamic-slice_bitcast_fusion.2), channel_id=1, source_target_pairs={{0,8},{4,12},{8,0},{12,4},{16,24},{20,28},{24,16},{28,20},{1,9},{5... | collective-permute-start | bytes 3538952 | tf_op jit(solution)/shard_map/ppermute | solution.py:92
  436.3 28.5 %collective-permute-start.1 = (bf16[2,2,2,96,768]{4,3,2,1,0:T(8,128)(2,1)}, bf16[2,2,2,96,768]{4,3,2,1,0:T(8,128)(2,1)}, u32[]{:S(2)}, u32[]{:S(2)}) collective-permute-start(bf16[2,2,2,96,768]{4,3,2,1,0:T(8,128)(2,1)} %dynamic-slice_bitcast_fusion.3), channel_id=1, source_target_pairs={{0,4},{4,0},{8,12},{12,8},{16,20},{20,16},{24,28},{28,24},{1,5},{5... | collective-permute-start | bytes 3538952 | tf_op jit(solution)/shard_map/ppermute | solution.py:92
  457.7 15.7 %collective-permute-start.12 = (bf16[2,2,96,768]{3,2,0,1:T(8,128)(2,1)S(1)}, bf16[2,2,96,768]{3,2,0,1:T(8,128)(2,1)S(1)}, u32[]{:S(2)}, u32[]{:S(2)}) collective-permute-start(bf16[2,2,96,768]{3,2,0,1:T(8,128)(2,1)S(1)} %dynamic-slice_bitcast_fusion.4), channel_id=1, source_target_pairs={{0,8},{4,12},{8,0},{12,4},{16,24},{20,28},{24,16},{28,20},{1,9},{5... | collective-permute-start | bytes 1769480 | tf_op jit(solution)/shard_map/ppermute | solution.py:92
  463.4 15.5 %collective-permute-start.7 = (bf16[2,2,96,768]{3,2,1,0:T(8,128)(2,1)S(1)}, bf16[2,2,96,768]{3,2,1,0:T(8,128)(2,1)S(1)}, u32[]{:S(2)}, u32[]{:S(2)}) collective-permute-start(bf16[2,2,96,768]{3,2,1,0:T(8,128)(2,1)S(1)} %dynamic-slice_bitcast_fusion.5), channel_id=1, source_target_pairs={{0,4},{4,0},{8,12},{12,8},{16,20},{20,16},{24,28},{28,24},{1,5},{5... | collective-permute-start | bytes 1769480 | tf_op jit(solution)/shard_map/ppermute | solution.py:92
  466.4 16.4 %collective-permute-start.2 = (bf16[2,2,96,768]{3,2,1,0:T(8,128)(2,1)S(1)}, bf16[2,2,96,768]{3,2,1,0:T(8,128)(2,1)S(1)}, u32[]{:S(2)}, u32[]{:S(2)}) collective-permute-start(bf16[2,2,96,768]{3,2,1,0:T(8,128)(2,1)S(1)} %dynamic-slice_bitcast_fusion.6), channel_id=1, source_target_pairs={{0,2},{1,3},{2,0},{3,1},{4,6},{5,7},{6,4},{7,5},{8,10},{9,11},{10,... | collective-permute-start | bytes 1769480 | tf_op jit(solution)/shard_map/ppermute | solution.py:92
  473.6 17.6 %collective-permute-start.13 = (bf16[2,96,768]{2,1,0:T(8,128)(2,1)S(1)}, bf16[2,96,768]{2,1,0:T(8,128)(2,1)S(1)}, u32[]{:S(2)}, u32[]{:S(2)}) collective-permute-start(bf16[2,96,768]{2,1,0:T(8,128)(2,1)S(1)} %dynamic-slice_bitcast_fusion.7), channel_id=1, source_target_pairs={{0,4},{4,0},{8,12},{12,8},{16,20},{20,16},{24,28},{28,24},{1,5},{5... | collective-permute-start | bytes 884744 | tf_op jit(solution)/shard_map/ppermute | solution.py:92
  487.3 20.8 %collective-permute-start.9 = (bf16[96,768]{1,0:T(8,128)(2,1)S(1)}, bf16[96,768]{1,0:T(8,128)(2,1)S(1)}, u32[]{:S(2)}, u32[]{:S(2)}) collective-permute-start(bf16[96,768]{1,0:T(8,128)(2,1)S(1)} %dynamic-slice_bitcast_fusion.11), channel_id=1, source_target_pairs={{0,16},{4,20},{8,24},{12,28},{16,0},{20,4},{24,8},{28,12},{1,17},{... | collective-permute-start | bytes 442376 | tf_op jit(solution)/shard_map/ppermute | solution.py:92
  491.1 15.0 %collective-permute-start.4 = (bf16[96,768]{1,0:T(8,128)(2,1)S(1)}, bf16[96,768]{1,0:T(8,128)(2,1)S(1)}, u32[]{:S(2)}, u32[]{:S(2)}) collective-permute-start(bf16[96,768]{1,0:T(8,128)(2,1)S(1)} %dynamic-slice_bitcast_fusion.12), channel_id=1, source_target_pairs={{0,16},{4,20},{8,24},{12,28},{16,0},{20,4},{24,8},{28,12},{1,17},{... | collective-permute-start | bytes 442376 | tf_op jit(solution)/shard_map/ppermute | solution.py:92
  491.3 18.1 %collective-permute-start.14 = (bf16[96,768]{1,0:T(8,128)(2,1)S(1)}, bf16[96,768]{1,0:T(8,128)(2,1)S(1)}, u32[]{:S(2)}, u32[]{:S(2)}) collective-permute-start(bf16[96,768]{1,0:T(8,128)(2,1)S(1)} %dynamic-slice_bitcast_fusion.10), channel_id=1, source_target_pairs={{0,16},{4,20},{8,24},{12,28},{16,0},{20,4},{24,8},{28,12},{1,17},{... | collective-permute-start | bytes 442376 | tf_op jit(solution)/shard_map/ppermute | solution.py:92
  512.0 9.6 %all-to-all-start.11 = ((f32[32,1,128]{2,1,0:T(1,128)}), f32[32,1,128]{2,1,0:T(1,128)S(1)}, u32[]{:S(2)}, u32[]{:S(2)}) async-start(f32[32,1,128]{2,1,0:T(1,128)} %broadcast_in_dim_broadcast_in_dim.3), calls=%async_computation.11 | async-start | bytes 32768 | tf_op jit(solution)/shard_map/all_to_all | solution.py:65
  522.3 9.8 %all-to-all-start.12 = ((f32[32,1,144]{2,1,0:T(1,128)}), f32[32,1,144]{2,1,0:T(1,128)S(1)}, u32[]{:S(2)}, u32[]{:S(2)}) async-start(f32[32,1,144]{2,1,0:T(1,128)} %broadcast_in_dim.281), calls=%async_computation.12 | async-start | bytes 65536 | tf_op jit(solution)/shard_map/all_to_all | solution.py:65
  (119 other events, 2854.8 us)
Sparse Core Ops, SparseCore 0:
  12.2 121.0 all-gather.2
  136.2 121.1 all-gather.4

commit v3 on v2

--- a/solution.py
+++ b/solution.py
@@ -71,11 +71,43 @@
     return [(axis, bit) for bit in reversed(range(lax.axis_size(axis).bit_length() - 1))]
 
 
-def owned(parts):
+def plan():
     layout = [bit for axis in ALL for bit in bits_of(axis)]
     first = (ALL[0], 0)
     last = [bit for bit in layout if bit[0] == ALL[1] and bit[1] >= 2]
     middle = [bit for bit in layout if bit != first and bit not in last]
+    return layout, first, middle, last
+
+
+def swapped(block, step):
+    axis, bit = step
+    size = lax.axis_size(axis)
+    return lax.ppermute(block, axis, [(index, index ^ (1 << bit)) for index in range(size)])
+
+
+def assembled(blocks):
+    layout, first, middle, last = plan()
+    turns = ((1, 0, 2), (0, 2, 1), (2, 1, 0))
+    results = []
+    for block, turn in zip(blocks, turns):
+        shape = block.shape
+        have = []
+        for step in last + [middle[index] for index in turn] + [first]:
+            axis, bit = step
+            came = swapped(block, step)
+            have = [other for other in layout if other in have or other == step]
+            place = have.index(step)
+            joined = jnp.stack([block, came], axis=place)
+            if axis != ALL[0]:
+                upper = ((lax.axis_index(axis) >> bit) & 1) > 0
+                joined = jnp.where(upper, jnp.stack([came, block], axis=place), joined)
+            block = joined
+        results.append(block.reshape(lax.axis_size(ALL[0]), -1, shape[1]))
+    return results
+
+
+def owned(parts):
+    layout, first, middle, last = plan()
     results = []
     for turn, part in enumerate(parts):
         turn %= len(middle)
@@ -85,12 +117,14 @@
         for step in order:
             axis, bit = step
             place = left.index(step)
-            mine = (lax.axis_index(axis) >> bit) & 1
-            send = lax.dynamic_index_in_dim(block, 1 - mine, place, keepdims=False)
-            keep = lax.dynamic_index_in_dim(block, mine, place, keepdims=False)
-            size = lax.axis_size(axis)
-            came = lax.ppermute(send, axis, [(index, index ^ (1 << bit)) for index in range(size)])
-            block = keep.astype(jnp.float32) + came.astype(jnp.float32)
+            if axis == ALL[0]:
+                keep = lax.index_in_dim(block, 0, place, keepdims=False)
+                send = lax.index_in_dim(block, 1, place, keepdims=False)
+            else:
+                mine = (lax.axis_index(axis) >> bit) & 1
+                keep = lax.dynamic_index_in_dim(block, mine, place, keepdims=False)
+                send = lax.dynamic_index_in_dim(block, 1 - mine, place, keepdims=False)
+            block = keep.astype(jnp.float32) + swapped(send, step).astype(jnp.float32)
             left.pop(place)
             if left:
                 block = block.astype(LOW)
@@ -239,15 +273,15 @@
     def side_by_side(qkv, out):
         return jnp.concatenate([qkv[0], qkv[1], qkv[2], out.T], axis=1)
 
-    def gathered(anchor, delta):
-        block = jnp.concatenate([anchor, delta.astype(LOW)], axis=1)
-        full = lax.all_gather(block, ALL, axis=0, tiled=True)
-        return full.reshape(n_heads, D, block.shape[1])
-
-    attn_all = gathered(side_by_side(qkv_anchor, out_anchor), side_by_side(qkv_delta, out_delta))
-    ffn_all = gathered(
-        jnp.concatenate([up_anchor, down_anchor.T], axis=1),
-        jnp.concatenate([up_delta, down_delta.T], axis=1),
+    def packed(anchor, delta):
+        return jnp.concatenate([anchor, delta.astype(LOW)], axis=1)
+
+    attn_all, up_all, down_all = assembled(
+        [
+            packed(side_by_side(qkv_anchor, out_anchor), side_by_side(qkv_delta, out_delta)),
+            packed(up_anchor, up_delta),
+            packed(down_anchor.T, down_delta.T),
+        ]
     )
 
     room = 8 * -(-(2 * SEQ // count + 8) // 8)
@@ -381,7 +415,8 @@
         bias_delta[1],
     )
     ffn_input = hidden.astype(LOW)
-    up_full, down_full, up_step, down_step = jnp.split(ffn_all, 4, axis=2)
+    up_full, up_step = jnp.split(up_all, 2, axis=2)
+    down_full, down_step = jnp.split(down_all, 2, axis=2)
     pre_gelu = einsum("td,hde->the", ffn_input, up_full)
     pre_dot = einsum("td,hde->the", hidden_dot.astype(LOW), up_full) + einsum(
         "td,hde->the", ffn_input, up_step

time: 569 us -> 655 us (1.15)
  local copies, waits for them, and re-layouts: 65.8 us -> 116 us
  other arithmetic: 76.8 us -> 117 us
  waiting for transfers between devices: 242 us -> 212 us
  starting transfers between devices: 45 us -> 67.2 us
  loops' own time: 0.15 us -> 18.5 us
  between operations: 23.7 us -> 10.6 us
    ppermute x15 -> x30, waiting for transfers between devices: 44.8 us -> 181 us  [swapped(): lax.ppermute(block, axis, [(index, index ^ 1 << bit) for index in range(s...]
    all_to_all x1, waiting for transfers between devices: 84.5 us -> 0.01 us  [fetch(): lax.all_to_all(rows.reshape(count, room, 2 * D), ALL, 0, 0, tiled=True)]
    all_gather x2 -> x0, waiting for transfers between devices: 80.5 us -> none  [gathered(): full = lax.all_gather(block, ALL, axis=0, tiled=True)]
    another operation x3 -> x14, other arithmetic: 2.04 us -> 36.7 us  [the longest x4 27.3 us: assembled(): joined = jnp.stack([block, came], axis=place)]
    another operation x0 -> x5, local copies, waits for them, and re-layouts: none -> 29.4 us  [assembled(): joined = jnp.stack([block, came], axis=place)]
    ppermute x0 -> x8, local copies, waits for them, and re-layouts: none -> 20.2 us  [swapped(): lax.ppermute(block, axis, [(index, index ^ 1 << bit) for index in range(s...]
    another operation x2, loops' own time: 0.15 us -> 18.5 us  [more(): return lax.cond(rounds > 1, rest, lambda value: value, start)]
    ppermute x15 -> x30, starting transfers between devices: 12.6 us -> 30.9 us  [swapped(): lax.ppermute(block, axis, [(index, index ^ 1 << bit) for index in range(s...]
  transfers between devices with their start and end apart: 26 -> 39, of which waited for: 19 -> 22; matrix products, arithmetic and copies ran while one was open for 23% -> 32% of each run, Pallas kernels for 0% -> 0%
where the time goes in v3:
time: 655 us; the launch traced here: 647 us
  waiting for transfers between devices  212 us (32%)
  other arithmetic  117 us (18%)
  local copies, waits for them, and re-layouts  116 us (18%)
  matrix products  99.8 us (15%)
  starting transfers between devices  67.2 us (10%)
  loops' own time  18.5 us (3%)
  between operations  10.6 us (2%)
  Pallas kernels  6.8 us (1%)
    ppermute x30, waiting for transfers between devices, swapped(): lax.ppermute(block, axis, [(index, index ^ 1 << bit) for index in range(s...  181 us
    dot_general x34, matrix products, einsum(): return jnp.einsum(form, left, right, preferred_element_type=jnp.float32)  95.1 us
    ppermute x30, starting transfers between devices, swapped(): lax.ppermute(block, axis, [(index, index ^ 1 << bit) for index in range(s...  30.9 us
    another operation x5, local copies, waits for them, and re-layouts, assembled(): joined = jnp.stack([block, came], axis=place)  29.4 us
    another operation x4, other arithmetic, assembled(): joined = jnp.stack([block, came], axis=place)  27.3 us
    ppermute x8, local copies, waits for them, and re-layouts, swapped(): lax.ppermute(block, axis, [(index, index ^ 1 << bit) for index in range(s...  20.2 us
    unnamed x277, local copies, waits for them, and re-layouts  20.1 us
    all_to_all x4, waiting for transfers between devices, everyone(): lax.all_to_all(jnp.broadcast_to(block, (count, block.shape[1])), ALL, 0,...  19.4 us
  transfers between devices with their start and end apart: 39, of which 22 were waited for; matrix products, arithmetic and copies ran while one was open for 32% of the time, Pallas kernels for 0%

profile of v3, /device:TPU:0, one launch (start us, length us, event | category | flops | bytes accessed | tf_op | source)
XLA Modules:
  0.0 647.2 jit_solution(4874381733592887981)
XLA Ops:
  5.6 7.3 %all-to-all-start.4 = ((f32[32,1,33]{2,1,0:T(1,128)}), f32[32,1,33]{2,1,0:T(1,128)S(1)}, u32[]{:S(2)}, u32[]{:S(2)}) async-start(f32[32,1,33]{2,1,0:T(1,128)} %bitcast.17), calls=%async_computation.4 | async-start | bytes 32768 | tf_op jit(solution)/shard_map/all_to_all | solution.py:352
  34.4 12.4 %collective-permute-done = bf16[96,1536]{1,0:T(8,128)(2,1)S(1)} collective-permute-done((bf16[96,1536]{1,0:T(8,128)(2,1)S(1)}, bf16[96,1536]{1,0:T(8,128)(2,1)S(1)}, u32[]{:S(2)}, u32[]{:S(2)}) %collective-permute-start) | collective-permute-done | bytes 294944 | tf_op jit(solution)/shard_map/ppermute | solution.py:85
  46.9 6.2 collective-permute-done.10
  60.7 10.6 %collective-permute-done.1 = bf16[2,96,1536]{2,1,0:T(8,128)(2,1)S(1)} collective-permute-done((bf16[2,96,1536]{2,1,0:T(8,128)(2,1)S(1)}, bf16[2,96,1536]{2,1,0:T(8,128)(2,1)S(1)}, u32[]{:S(2)}, u32[]{:S(2)}) %collective-permute-start.1) | collective-permute-done | bytes 589856 | tf_op jit(solution)/shard_map/ppermute | solution.py:85
  77.9 21.5 %collective-permute-done.2 = bf16[2,2,96,1536]{3,2,1,0:T(8,128)(2,1)S(1)} collective-permute-done((bf16[2,2,96,1536]{3,2,1,0:T(8,128)(2,1)S(1)}, bf16[2,2,96,1536]{3,2,1,0:T(8,128)(2,1)S(1)}, u32[]{:S(2)}, u32[]{:S(2)}) %collective-permute-start.2) | collective-permute-done | bytes 1179680 | tf_op jit(solution)/shard_map/ppermute | solution.py:85
  105.6 6.0 fusion.35
  126.9 53.5 %collective-permute-done.3 = bf16[2,2,2,96,1536]{4,3,2,1,0:T(8,128)(2,1)} collective-permute-done((bf16[2,2,2,96,1536]{4,3,2,1,0:T(8,128)(2,1)}, bf16[2,2,2,96,1536]{4,3,2,1,0:T(8,128)(2,1)}, u32[]{:S(2)}, u32[]{:S(2)}) %collective-permute-start.3) | collective-permute-done | bytes 2359328 | tf_op jit(solution)/shard_map/ppermute | solution.py:85
  187.8 21.4 %collective-permute-done.8 = bf16[2,2,2,96,1536]{4,3,2,1,0:T(8,128)(2,1)S(1)} collective-permute-done((bf16[2,2,2,96,1536]{4,3,2,1,0:T(8,128)(2,1)S(1)}, bf16[2,2,2,96,1536]{4,3,2,1,0:T(8,128)(2,1)S(1)}, u32[]{:S(2)}, u32[]{:S(2)}) %collective-permute-start.8) | collective-permute-done | bytes 2359328 | tf_op jit(solution)/shard_map/ppermute | solution.py:85
  229.5 12.8 %conditional.2 = (f32[256,1536]{1,0:T(8,128)}) conditional(s32[]{:T(128)} %convert_element_type.368, f32[256,1536]{1,0:T(8,128)} %fusion.125, (s32[]{:T(128)}, s32[256]{0:T(256)S(1)}, s32[256]{0:T(256)S(1)}, pred[256]{0:T(512)(128)(4,1)S(1)}, s32[256]{0:T(256)S(1)}, /*index=5*/bf16[1572,1536]{1,0:T(8,128)(2,1)}, f32[256,1536]{1,0:T(8,128)}) %tuple.54), branch_computations={%region_5.6_spmd, %region_6.10_spmd} | conditional | flops 4316361728 | bytes 19818000 | solution.py:343
  251.5 8.2 %pad_maximum_fusion = bf16[2,2,2,2,2,96,1536]{6,5,2,3,0,4,1:T(8,128)(2,1)} fusion(bf16[2,1,2,2,2,96,1536]{6,5,2,3,0,4,1:T(8,128)(2,1)} %bitcast.505, bf16[2,1,2,2,2,96,1536]{6,5,2,3,0,4,1:T(8,128)(2,1)} %maximum_select_fusion), kind=kLoop, calls=%fused_computation.27 | loop fusion | flops 4718592 | bytes 18874368 | tf_op jit(solution)/shard_map/stack | solution.py:100
  259.7 8.4 %copy.409 = bf16[2,2,2,2,2,96,1536]{6,5,4,3,2,1,0:T(8,128)(2,1)} copy(bf16[2,2,2,2,2,96,1536]{6,5,2,3,0,4,1:T(8,128)(2,1)} %pad_maximum_fusion) | data formatting | bytes 18874368 | tf_op jit(solution)/shard_map/stack | solution.py:100
  281.6 8.2 %pad_maximum_fusion.1 = bf16[2,2,2,2,2,96,1536]{6,5,2,0,4,3,1:T(8,128)(2,1)} fusion(bf16[2,1,2,2,2,96,1536]{6,5,2,0,4,3,1:T(8,128)(2,1)} %bitcast.506, bf16[2,1,2,2,2,96,1536]{6,5,2,0,4,3,1:T(8,128)(2,1)} %maximum_select_fusion.2), kind=kLoop, calls=%fused_computation.28 | loop fusion | flops 4718592 | bytes 18874368 | tf_op jit(solution)/shard_map/stack | solution.py:100
  289.8 8.5 %copy.418 = bf16[2,2,2,2,2,96,1536]{6,5,4,3,2,1,0:T(8,128)(2,1)} copy(bf16[2,2,2,2,2,96,1536]{6,5,2,0,4,3,1:T(8,128)(2,1)} %pad_maximum_fusion.1) | data formatting | bytes 18874368 | tf_op jit(solution)/shard_map/stack | solution.py:100
  337.0 8.3 %pad_maximum_fusion.2 = bf16[2,2,2,2,2,96,1536]{6,5,2,4,3,0,1:T(8,128)(2,1)} fusion(bf16[2,1,2,2,2,96,1536]{6,5,2,4,3,0,1:T(8,128)(2,1)} %bitcast.504, bf16[2,1,2,2,2,96,1536]{6,5,2,4,3,0,1:T(8,128)(2,1)} %get-tuple-element.558), kind=kLoop, calls=%fused_computation.29 | loop fusion | flops 4718592 | bytes 18874368 | tf_op jit(solution)/shard_map/stack | solution.py:100
  345.3 8.3 %copy.425 = bf16[2,2,2,2,2,96,1536]{6,5,4,3,2,1,0:T(8,128)(2,1)} copy(bf16[2,2,2,2,2,96,1536]{6,5,2,4,3,0,1:T(8,128)(2,1)} %pad_maximum_fusion.2) | data formatting | bytes 18874368 | tf_op jit(solution)/shard_map/stack | solution.py:100
  353.6 8.3 %fusion.38 = bf16[256,4,768]{2,0,1:T(8,128)(2,1)S(1)} fusion(f32[256,4,768]{2,0,1:T(8,128)} %get-tuple-element.607, u8[256,768]{1,0:T(8,128)(4,1)S(1)} %get-tuple-element.447, u8[256,768]{1,0:T(8,128)(4,1)S(1)} %get-tuple-element.446), kind=kLoop, calls=%fused_computation.81 | loop fusion | flops 55050240 | bytes 5111808 | tf_op jit(solution)/shard_map/convert_element_type | solution.py:424
  370.3 10.2 %fusion.216 = (f32[256]{0:T(256)S(1)}, f32[256]{0:T(256)S(1)}, f32[256,768]{1,0:T(8,128)}) fusion(f32[256]{0:T(256)S(1)} %add_rsqrt_fusion, f32[256,768]{1,0:T(8,128)S(1)} %get-tuple-element.609, f32[256]{0:T(256)S(1)} %broadcast_multiply_fusion.12, f32[256,768]{1,0:T(8,128)} %fusion.82, bf16[4,768,1536]{2,1,0:T(8,128)(2,1)} %bitcast.520, ...), kind=kOutput, calls=%fused_computation.453 | convolution fusion | flops 2430074368 | bytes 21270528 | tf_op jit(solution)/shard_map/the,hde->td/dot_general | solution.py:31
  390.5 7.1 %all-to-all-done.6 = bf16[32,2,768]{2,1,0:T(2,128)(2,1)S(1)} async-done(((bf16[32,2,768]{2,1,0:T(2,128)(2,1)}), bf16[32,2,768]{2,1,0:T(2,128)(2,1)S(1)}, u32[]{:S(2)}, u32[]{:S(2)}) %all-to-all-start.6) | async-done | bytes 98336 | tf_op jit(solution)/shard_map/all_to_all | solution.py:65
  420.0 6.8 %shard_map.498 = (f32[4,32]{1,0:T(4,128)}, f32[1,32]{1,0:T(1,128)}, f32[1,1]{1,0:T(1,128)}) custom-call(f32[32,512]{1,0:T(8,128)} %bitcast.576, bf16[32,768]{1,0:T(8,128)(2,1)} %slice.282.feat_ref, f32[4,32]{1,0:T(4,128)} %slice_bitcast_fusion.17.targets_ref), custom_call_target="tpu_custom_call" | custom-call | tf_op jit(solution)/shard_map/pallas_call | solution.py:189
  491.4 6.6 %copy.438 = bf16[4,768,768]{2,1,0:T(8,128)(2,1)} copy(bf16[4,768,768]{1,2,0:T(8,128)(2,1)} %pad_maximum_fusion.5) | data formatting | bytes 9437184 | tf_op jit(solution)/shard_map/concatenate | solution.py:497
  535.6 18.7 %collective-permute-done.26 = bf16[2,2,2,96,768]{4,3,0,2,1:T(8,128)(2,1)S(1)} collective-permute-done((bf16[2,2,2,96,768]{4,3,0,2,1:T(8,128)(2,1)S(1)}, bf16[2,2,2,96,768]{4,3,0,2,1:T(8,128)(2,1)S(1)}, u32[]{:S(2)}, u32[]{:S(2)}) %collective-permute-start.26) | collective-permute-done | bytes 1179680 | tf_op jit(solution)/shard_map/ppermute | solution.py:85
  564.0 9.7 %collective-permute-done.27 = bf16[2,2,96,768]{3,2,0,1:T(8,128)(2,1)S(1)} collective-permute-done((bf16[2,2,96,768]{3,2,0,1:T(8,128)(2,1)S(1)}, bf16[2,2,96,768]{3,2,0,1:T(8,128)(2,1)S(1)}, u32[]{:S(2)}, u32[]{:S(2)}) %collective-permute-start.27) | collective-permute-done | bytes 589856 | tf_op jit(solution)/shard_map/ppermute | solution.py:85
  587.2 10.3 %collective-permute-done.19 = bf16[96,768]{1,0:T(8,128)(2,1)S(1)} collective-permute-done((bf16[96,768]{1,0:T(8,128)(2,1)S(1)}, bf16[96,768]{1,0:T(8,128)(2,1)S(1)}, u32[]{:S(2)}, u32[]{:S(2)}) %collective-permute-start.19) | collective-permute-done | bytes 147488 | tf_op jit(solution)/shard_map/ppermute | solution.py:85
  630.1 13.5 %multiply_subtract_fusion = (f32[1572,768]{1,0:T(8,128)}, f32[1572,768]{1,0:T(8,128)}, f32[1572,768]{1,0:T(8,128)}) fusion(f32[1572,768]{1,0:T(8,128)} %param.51, f32[]{:T(128)} %bitcast.179, f32[]{:T(128)} %bitcast.178, f32[1572,768]{1,0:T(8,128)} %get-tuple-element.805, f32[]{:T(128)S(6)} %min.3, f32[1572,768]{1,0:T(8,128)} %param.53, f32[1572,768]{1,0:T(8,128)} %param.52), kind=kLoop, calls=%fused_computation.36 | loop fusion | flops 19316736 | bytes 33804300 | tf_op jit(solution)/shard_map/sub | solution.py:209
  (579 shorter events, 344.1 us)
Async XLA Ops:
  5.6 28.5 %all-to-all-start.4 = ((f32[32,1,33]{2,1,0:T(1,128)}), f32[32,1,33]{2,1,0:T(1,128)S(1)}, u32[]{:S(2)}, u32[]{:S(2)}) async-start(f32[32,1,33]{2,1,0:T(1,128)} %bitcast.17), calls=%async_computation.4 | async-start | bytes 32768 | tf_op jit(solution)/shard_map/all_to_all | solution.py:352
  16.9 29.8 %collective-permute-start = (bf16[96,1536]{1,0:T(8,128)(2,1)S(1)}, bf16[96,1536]{1,0:T(8,128)(2,1)S(1)}, u32[]{:S(2)}, u32[]{:S(2)}) collective-permute-start(bf16[96,1536]{1,0:T(8,128)(2,1)S(1)} %concatenate.240), channel_id=1, source_target_pairs={{0,16},{4,20},{8,24},{12,28},{16,0},{20,4},{24,8},{28,12},{1,17},{... | collective-permute-start | bytes 884744 | tf_op jit(solution)/shard_map/ppermute | solution.py:85
  21.6 31.5 %collective-permute-start.10 = (bf16[96,1536]{1,0:T(8,128)(2,1)S(1)}, bf16[96,1536]{1,0:T(8,128)(2,1)S(1)}, u32[]{:S(2)}, u32[]{:S(2)}) collective-permute-start(bf16[96,1536]{1,0:T(8,128)(2,1)S(1)} %get-tuple-element.581), channel_id=1, source_target_pairs={{0,16},{4,20},{8,24},{12,28},{16,0},{20,4},{24,8},{28,12},{1,17},{... | collective-permute-start | bytes 884744 | tf_op jit(solution)/shard_map/ppermute | solution.py:85
  22.8 36.0 %collective-permute-start.5 = (bf16[96,1536]{1,0:T(8,128)(2,1)}, bf16[96,1536]{1,0:T(8,128)(2,1)S(1)}, u32[]{:S(2)}, u32[]{:S(2)}) collective-permute-start(bf16[96,1536]{1,0:T(8,128)(2,1)} %get-tuple-element.584), channel_id=1, source_target_pairs={{0,16},{4,20},{8,24},{12,28},{16,0},{20,4},{24,8},{28,12},{1,17},{... | collective-permute-start | bytes 884744 | tf_op jit(solution)/shard_map/ppermute | solution.py:85
  46.8 24.5 %collective-permute-start.1 = (bf16[2,96,1536]{2,1,0:T(8,128)(2,1)S(1)}, bf16[2,96,1536]{2,1,0:T(8,128)(2,1)S(1)}, u32[]{:S(2)}, u32[]{:S(2)}) collective-permute-start(bf16[2,96,1536]{2,1,0:T(8,128)(2,1)S(1)} %maximum_select_fusion.12), channel_id=1, source_target_pairs={{0,8},{4,12},{8,0},{12,4},{16,24},{20,28},{24,16},{28,20},{1,9},{5... | collective-permute-start | bytes 1769480 | tf_op jit(solution)/shard_map/ppermute | solution.py:85
  53.2 20.1 %collective-permute-start.11 = (bf16[2,96,1536]{2,1,0:T(8,128)(2,1)S(1)}, bf16[2,96,1536]{2,1,0:T(8,128)(2,1)S(1)}, u32[]{:S(2)}, u32[]{:S(2)}) collective-permute-start(bf16[2,96,1536]{2,1,0:T(8,128)(2,1)S(1)} %maximum_select_fusion.16), channel_id=1, source_target_pairs={{0,4},{4,0},{8,12},{12,8},{16,20},{20,16},{24,28},{28,24},{1,5},{5... | collective-permute-start | bytes 1769480 | tf_op jit(solution)/shard_map/ppermute | solution.py:85
  71.5 28.0 %collective-permute-start.2 = (bf16[2,2,96,1536]{3,2,1,0:T(8,128)(2,1)S(1)}, bf16[2,2,96,1536]{3,2,1,0:T(8,128)(2,1)S(1)}, u32[]{:S(2)}, u32[]{:S(2)}) collective-permute-start(bf16[2,2,96,1536]{3,2,1,0:T(8,128)(2,1)S(1)} %maximum_select_fusion.9), channel_id=1, source_target_pairs={{0,2},{1,3},{2,0},{3,1},{4,6},{5,7},{6,4},{7,5},{8,10},{9,11},{10,... | collective-permute-start | bytes 3538952 | tf_op jit(solution)/shard_map/ppermute | solution.py:85
  74.6 48.6 %collective-permute-start.12 = (bf16[2,2,96,1536]{3,2,1,0:T(8,128)(2,1)}, bf16[2,2,96,1536]{3,2,1,0:T(8,128)(2,1)}, u32[]{:S(2)}, u32[]{:S(2)}) collective-permute-start(bf16[2,2,96,1536]{3,2,1,0:T(8,128)(2,1)} %maximum_select_fusion.10), channel_id=1, source_target_pairs={{0,8},{4,12},{8,0},{12,4},{16,24},{20,28},{24,16},{28,20},{1,9},{5... | collective-permute-start | bytes 3538952 | tf_op jit(solution)/shard_map/ppermute | solution.py:85
  76.2 42.4 %collective-permute-start.7 = (bf16[2,2,96,1536]{3,2,1,0:T(8,128)(2,1)}, bf16[2,2,96,1536]{3,2,1,0:T(8,128)(2,1)S(1)}, u32[]{:S(2)}, u32[]{:S(2)}) collective-permute-start(bf16[2,2,96,1536]{3,2,1,0:T(8,128)(2,1)} %get-tuple-element.574), channel_id=1, source_target_pairs={{0,4},{4,0},{8,12},{12,8},{16,20},{20,16},{24,28},{28,24},{1,5},{5... | collective-permute-start | bytes 3538952 | tf_op jit(solution)/shard_map/ppermute | solution.py:85
  104.0 76.4 %collective-permute-start.3 = (bf16[2,2,2,96,1536]{4,3,2,1,0:T(8,128)(2,1)}, bf16[2,2,2,96,1536]{4,3,2,1,0:T(8,128)(2,1)}, u32[]{:S(2)}, u32[]{:S(2)}) collective-permute-start(bf16[2,2,2,96,1536]{4,3,2,1,0:T(8,128)(2,1)} %copy.404), channel_id=1, source_target_pairs={{0,4},{4,0},{8,12},{12,8},{16,20},{20,16},{24,28},{28,24},{1,5},{5... | collective-permute-start | bytes 7077896 | tf_op jit(solution)/shard_map/ppermute | solution.py:85
  112.9 112.9 %all-to-all-start.5 = ((bf16[32,24,1536]{2,1,0:T(8,128)(2,1)}), bf16[32,24,1536]{2,1,0:T(8,128)(2,1)}, u32[]{:S(2)}, u32[]{:S(2)}) async-start(bf16[32,24,1536]{2,1,0:T(8,128)(2,1)} %bitcast.547), calls=%async_computation.5 | async-start | bytes 4718592 | tf_op jit(solution)/shard_map/all_to_all | solution.py:331
  120.9 88.3 %collective-permute-start.8 = (bf16[2,2,2,96,1536]{4,3,2,1,0:T(8,128)(2,1)S(1)}, bf16[2,2,2,96,1536]{4,3,2,1,0:T(8,128)(2,1)S(1)}, u32[]{:S(2)}, u32[]{:S(2)}) collective-permute-start(bf16[2,2,2,96,1536]{4,3,2,1,0:T(8,128)(2,1)S(1)} %copy.413), channel_id=1, source_target_pairs={{0,8},{4,12},{8,0},{12,4},{16,24},{20,28},{24,16},{28,20},{1,9},{5... | collective-permute-start | bytes 7077896 | tf_op jit(solution)/shard_map/ppermute | solution.py:85
  125.2 87.8 %collective-permute-start.13 = (bf16[2,2,2,96,1536]{4,3,2,1,0:T(8,128)(2,1)S(1)}, bf16[2,2,2,96,1536]{4,3,2,1,0:T(8,128)(2,1)}, u32[]{:S(2)}, u32[]{:S(2)}) collective-permute-start(bf16[2,2,2,96,1536]{4,3,2,1,0:T(8,128)(2,1)S(1)} %copy.421), channel_id=1, source_target_pairs={{0,2},{1,3},{2,0},{3,1},{4,6},{5,7},{6,4},{7,5},{8,10},{9,11},{10,... | collective-permute-start | bytes 7077896 | tf_op jit(solution)/shard_map/ppermute | solution.py:85
  185.6 60.9 %collective-permute-start.4 = (bf16[2,2,2,2,96,1536]{5,4,3,2,1,0:T(8,128)(2,1)}, bf16[2,2,2,2,96,1536]{5,4,3,2,1,0:T(8,128)(2,1)}, u32[]{:S(2)}, u32[]{:S(2)}) collective-permute-start(bf16[2,2,2,2,96,1536]{5,4,3,2,1,0:T(8,128)(2,1)} %copy.407), channel_id=1, source_target_pairs={{0,1},{1,0},{2,3},{3,2},{4,5},{5,4},{6,7},{7,6},{8,9},{9,8},{10,11... | collective-permute-start | bytes 14155784 | tf_op jit(solution)/shard_map/ppermute | solution.py:85
  212.6 64.1 %collective-permute-start.9 = (bf16[2,2,2,2,96,1536]{5,4,3,2,1,0:T(8,128)(2,1)}, bf16[2,2,2,2,96,1536]{5,4,3,2,1,0:T(8,128)(2,1)}, u32[]{:S(2)}, u32[]{:S(2)}) collective-permute-start(bf16[2,2,2,2,96,1536]{5,4,3,2,1,0:T(8,128)(2,1)} %copy.416), channel_id=1, source_target_pairs={{0,1},{1,0},{2,3},{3,2},{4,5},{5,4},{6,7},{7,6},{8,9},{9,8},{10,11... | collective-permute-start | bytes 14155784 | tf_op jit(solution)/shard_map/ppermute | solution.py:85
  220.3 111.8 %collective-permute-start.14 = (bf16[2,2,2,2,96,1536]{5,4,3,2,1,0:T(8,128)(2,1)}, bf16[2,2,2,2,96,1536]{5,4,3,2,1,0:T(8,128)(2,1)}, u32[]{:S(2)}, u32[]{:S(2)}) collective-permute-start(bf16[2,2,2,2,96,1536]{5,4,3,2,1,0:T(8,128)(2,1)} %copy.423), channel_id=1, source_target_pairs={{0,1},{1,0},{2,3},{3,2},{4,5},{5,4},{6,7},{7,6},{8,9},{9,8},{10,11... | collective-permute-start | bytes 14155784 | tf_op jit(solution)/shard_map/ppermute | solution.py:85
  476.4 33.9 %all-to-all-start.9 = ((bf16[32,24,768]{2,1,0:T(8,128)(2,1)}), bf16[32,24,768]{2,1,0:T(8,128)(2,1)}, u32[]{:S(2)}, u32[]{:S(2)}) async-start(bf16[32,24,768]{2,1,0:T(8,128)(2,1)} %bitcast.133), calls=%async_computation.9 | async-start | bytes 2359296 | tf_op jit(solution)/shard_map/all_to_all | solution.py:336
  485.8 37.6 %collective-permute-start.25 = (bf16[2,2,2,2,96,768]{5,4,1,3,2,0:T(8,128)(2,1)}, bf16[2,2,2,2,96,768]{5,4,1,3,2,0:T(8,128)(2,1)}, u32[]{:S(2)}, u32[]{:S(2)}) collective-permute-start(bf16[2,2,2,2,96,768]{5,4,1,3,2,0:T(8,128)(2,1)} %bitcast.449), channel_id=1, source_target_pairs={{0,1},{1,0},{2,3},{3,2},{4,5},{5,4},{6,7},{7,6},{8,9},{9,8},{10,11... | collective-permute-start | bytes 7077896 | tf_op jit(solution)/shard_map/ppermute | solution.py:85
  501.3 25.9 %collective-permute-start.15 = (bf16[2,2,2,2,96,768]{5,4,3,2,1,0:T(8,128)(2,1)}, bf16[2,2,2,2,96,768]{5,4,3,2,1,0:T(8,128)(2,1)}, u32[]{:S(2)}, u32[]{:S(2)}) collective-permute-start(bf16[2,2,2,2,96,768]{5,4,3,2,1,0:T(8,128)(2,1)} %slice_bitcast_fusion), channel_id=1, source_target_pairs={{0,1},{1,0},{2,3},{3,2},{4,5},{5,4},{6,7},{7,6},{8,9},{9,8},{10,11... | collective-permute-start | bytes 7077896 | tf_op jit(solution)/shard_map/ppermute | solution.py:85
  506.4 24.2 %collective-permute-start.20 = (bf16[2,2,2,2,96,768]{5,4,1,0,3,2:T(8,128)(2,1)}, bf16[2,2,2,2,96,768]{5,4,1,0,3,2:T(8,128)(2,1)}, u32[]{:S(2)}, u32[]{:S(2)}) collective-permute-start(bf16[2,2,2,2,96,768]{5,4,1,0,3,2:T(8,128)(2,1)} %bitcast.450), channel_id=1, source_target_pairs={{0,1},{1,0},{2,3},{3,2},{4,5},{5,4},{6,7},{7,6},{8,9},{9,8},{10,11... | collective-permute-start | bytes 7077896 | tf_op jit(solution)/shard_map/ppermute | solution.py:85
  526.7 27.7 %collective-permute-start.26 = (bf16[2,2,2,96,768]{4,3,0,2,1:T(8,128)(2,1)S(1)}, bf16[2,2,2,96,768]{4,3,0,2,1:T(8,128)(2,1)S(1)}, u32[]{:S(2)}, u32[]{:S(2)}) collective-permute-start(bf16[2,2,2,96,768]{4,3,0,2,1:T(8,128)(2,1)S(1)} %slice_bitcast_fusion.2), channel_id=1, source_target_pairs={{0,2},{1,3},{2,0},{3,1},{4,6},{5,7},{6,4},{7,5},{8,10},{9,11},{10,... | collective-permute-start | bytes 3538952 | tf_op jit(solution)/shard_map/ppermute | solution.py:85
  529.9 28.0 %collective-permute-start.16 = (bf16[2,2,2,96,768]{4,3,2,1,0:T(8,128)(2,1)S(1)}, bf16[2,2,2,96,768]{4,3,2,1,0:T(8,128)(2,1)S(1)}, u32[]{:S(2)}, u32[]{:S(2)}) collective-permute-start(bf16[2,2,2,96,768]{4,3,2,1,0:T(8,128)(2,1)S(1)} %dynamic-slice_bitcast_fusion.1), channel_id=1, source_target_pairs={{0,4},{4,0},{8,12},{12,8},{16,20},{20,16},{24,28},{28,24},{1,5},{5... | collective-permute-start | bytes 3538952 | tf_op jit(solution)/shard_map/ppermute | solution.py:85
  533.3 28.9 %collective-permute-start.21 = (bf16[2,2,2,96,768]{4,3,1,0,2:T(8,128)(2,1)S(1)}, bf16[2,2,2,96,768]{4,3,1,0,2:T(8,128)(2,1)S(1)}, u32[]{:S(2)}, u32[]{:S(2)}) collective-permute-start(bf16[2,2,2,96,768]{4,3,1,0,2:T(8,128)(2,1)S(1)} %dynamic-slice_bitcast_fusion), channel_id=1, source_target_pairs={{0,8},{4,12},{8,0},{12,4},{16,24},{20,28},{24,16},{28,20},{1,9},{5... | collective-permute-start | bytes 3538952 | tf_op jit(solution)/shard_map/ppermute | solution.py:85
  554.8 18.9 %collective-permute-start.27 = (bf16[2,2,96,768]{3,2,0,1:T(8,128)(2,1)S(1)}, bf16[2,2,96,768]{3,2,0,1:T(8,128)(2,1)S(1)}, u32[]{:S(2)}, u32[]{:S(2)}) collective-permute-start(bf16[2,2,96,768]{3,2,0,1:T(8,128)(2,1)S(1)} %dynamic-slice_bitcast_fusion.2), channel_id=1, source_target_pairs={{0,8},{4,12},{8,0},{12,4},{16,24},{20,28},{24,16},{28,20},{1,9},{5... | collective-permute-start | bytes 1769480 | tf_op jit(solution)/shard_map/ppermute | solution.py:85
  (147 other events, 3929.3 us)

commit v4 on v3

--- a/solution.py
+++ b/solution.py
@@ -85,36 +85,45 @@
     return lax.ppermute(block, axis, [(index, index ^ (1 << bit)) for index in range(size)])
 
 
-def assembled(blocks):
+def joined(block, have, step):
+    layout = plan()[0]
+    axis, bit = step
+    came = swapped(block, step)
+    have = [other for other in layout if other in have or other == step]
+    place = have.index(step)
+    both = jnp.stack([block, came], axis=place)
+    if axis != ALL[0]:
+        upper = ((lax.axis_index(axis) >> bit) & 1) > 0
+        both = jnp.where(upper, jnp.stack([came, block], axis=place), both)
+    return both, have
+
+
+def assembled(blocks, rows):
     layout, first, middle, last = plan()
-    turns = ((1, 0, 2), (0, 2, 1), (2, 1, 0))
+    orders = [
+        last + [middle[index] for index in turn] for turn in ((1, 0, 2), (0, 2, 1), (2, 1, 0))
+    ]
+    width = blocks[0].shape[1]
+    states = [joined(block, [], order[0]) for block, order in zip(blocks, orders)]
+    started, rows = lax.optimization_barrier(([state[0] for state in states], rows))
     results = []
-    for block, turn in zip(blocks, turns):
-        shape = block.shape
-        have = []
-        for step in last + [middle[index] for index in turn] + [first]:
-            axis, bit = step
-            came = swapped(block, step)
-            have = [other for other in layout if other in have or other == step]
-            place = have.index(step)
-            joined = jnp.stack([block, came], axis=place)
-            if axis != ALL[0]:
-                upper = ((lax.axis_index(axis) >> bit) & 1) > 0
-                joined = jnp.where(upper, jnp.stack([came, block], axis=place), joined)
-            block = joined
-        results.append(block.reshape(lax.axis_size(ALL[0]), -1, shape[1]))
-    return results
+    for block, (_, have), order in zip(started, states, orders):
+        for step in order[1:]:
+            block, have = joined(block, have, step)
+        pair = (block, swapped(block, first))
+        results.append([half.reshape(lax.axis_size(ALL[0]) // 2, -1, width) for half in pair])
+    return results, rows
 
 
 def owned(parts):
     layout, first, middle, last = plan()
     results = []
-    for turn, part in enumerate(parts):
+    for turn, (keep, send) in enumerate(parts):
         turn %= len(middle)
-        order = [first] + middle[turn:] + middle[:turn] + last[::-1]
-        left = list(layout)
-        block = part.reshape((2,) * len(layout) + (-1, part.shape[-1]))
-        for step in order:
+        block = (keep.astype(jnp.float32) + swapped(send, first).astype(jnp.float32)).astype(LOW)
+        left = [step for step in layout if step != first]
+        block = block.reshape((2,) * len(left) + (-1, keep.shape[-1]))
+        for step in middle[turn:] + middle[:turn] + last[::-1]:
             axis, bit = step
             place = left.index(step)
             if axis == ALL[0]:
@@ -276,13 +285,11 @@
     def packed(anchor, delta):
         return jnp.concatenate([anchor, delta.astype(LOW)], axis=1)
 
-    attn_all, up_all, down_all = assembled(
-        [
-            packed(side_by_side(qkv_anchor, out_anchor), side_by_side(qkv_delta, out_delta)),
-            packed(up_anchor, up_delta),
-            packed(down_anchor.T, down_delta.T),
-        ]
-    )
+    blocks = [
+        packed(side_by_side(qkv_anchor, out_anchor), side_by_side(qkv_delta, out_delta)),
+        packed(up_anchor, up_delta),
+        packed(down_anchor.T, down_delta.T),
+    ]
 
     room = 8 * -(-(2 * SEQ // count + 8) // 8)
     slots = count * room
@@ -326,8 +333,10 @@
             slot_of(turn)[:, None] == lax.broadcasted_iota(jnp.int32, (SEQ, slots), 1)
         ).astype(LOW)
 
-    def fetch(turn, wanted):
-        rows = einsum("sv,vd->sd", chosen(wanted), both).astype(LOW)
+    def rows_of(wanted):
+        return einsum("sv,vd->sd", chosen(wanted), both).astype(LOW)
+
+    def fetch(turn, rows):
         rows = lax.all_to_all(rows.reshape(count, room, 2 * D), ALL, 0, 0, tiled=True)
         return einsum("ts,sd->td", token_slots(turn), rows.reshape(slots, 2 * D))
 
@@ -354,7 +363,8 @@
     rounds = -(-jnp.max(message[:, room]).astype(jnp.int32) // room)
     labels = message[:, room + 1 : room + 1 + NLW].astype(jnp.int32) - me * vocab
     targets_all = message[:, room + 1 + NLW :].T
-    embedded_both = more(fetch(0, wanted_first), lambda turn: fetch(turn, asked(turn)))
+    (attn_pair, up_pair, down_pair), rows_first = assembled(blocks, rows_of(wanted_first))
+    embedded_both = more(fetch(0, rows_first), lambda turn: fetch(turn, rows_of(asked(turn))))
     start_x, start_dot, normed_zero, inverse_zero = norm_pair(
         embedded_both[:, :D],
         embedded_both[:, D:],
@@ -371,13 +381,30 @@
     attn_in = start_x.astype(LOW)
     attn_dot_in = start_dot.astype(LOW)
     three = 3 * group_wide
-    wide = attn_all.shape[2] // 2
-    through = einsum("td,hde->the", attn_in, attn_all)
-    projected = through[:, :, :three].astype(LOW)
-    projected_dot = (
-        through[:, :, wide : wide + three]
-        + einsum("td,hde->the", attn_dot_in, attn_all[:, :, :three])
-    ).astype(LOW)
+    wide = attn_pair[0].shape[2] // 2
+    groups = attn_pair[0].shape[0]
+    qkv_full = [half[:, :, :three] for half in attn_pair]
+    out_full = [half[:, :, three:wide] for half in attn_pair]
+    out_step = [half[:, :, wide + three :] for half in attn_pair]
+
+    def into(values, pair):
+        return [einsum("td,hde->the", values, half) for half in pair]
+
+    def out_of(values, pair):
+        return sum(einsum("the,hde->td", part, half) for part, half in zip(values, pair))
+
+    def halves(values):
+        return [values[:, :groups], values[:, groups:]]
+
+    through = into(attn_in, attn_pair)
+    projected = jnp.concatenate([part[:, :, :three].astype(LOW) for part in through], axis=1)
+    projected_dot = jnp.concatenate(
+        [
+            (part[:, :, wide : wide + three] + more_part).astype(LOW)
+            for part, more_part in zip(through, into(attn_dot_in, qkv_full))
+        ],
+        axis=1,
+    )
 
     def split_heads(array):
         array = array.reshape(SEQ, n_heads, 3, local_heads, HDIM)
@@ -398,14 +425,10 @@
     attended_dot = (
         einsum("hqk,khd->qhd", prob_dot, value) + einsum("hqk,khd->qhd", probs_low, value_dot)
     ).astype(LOW)
-    attended = attended.reshape(SEQ, n_heads, group_wide)
-    attended_dot = attended_dot.reshape(SEQ, n_heads, group_wide)
-    out_full = attn_all[:, :, three:wide]
-    out_step = attn_all[:, :, wide + three :]
-    attn_out = einsum("the,hde->td", attended, out_full)
-    attn_dot = einsum("the,hde->td", attended_dot, out_full) + einsum(
-        "the,hde->td", attended, out_step
-    )
+    attended = halves(attended.reshape(SEQ, n_heads, group_wide))
+    attended_dot = halves(attended_dot.reshape(SEQ, n_heads, group_wide))
+    attn_out = out_of(attended, out_full)
+    attn_dot = out_of(attended_dot, out_full) + out_of(attended, out_step)
     hidden, hidden_dot, normed_one, inverse_one = norm_pair(
         start_x + attn_out,
         start_dot + attn_dot,
@@ -415,19 +438,18 @@
         bias_delta[1],
     )
     ffn_input = hidden.astype(LOW)
-    up_full, up_step = jnp.split(up_all, 2, axis=2)
-    down_full, down_step = jnp.split(down_all, 2, axis=2)
-    pre_gelu = einsum("td,hde->the", ffn_input, up_full)
-    pre_dot = einsum("td,hde->the", hidden_dot.astype(LOW), up_full) + einsum(
-        "td,hde->the", ffn_input, up_step
-    )
-    activated = jax.nn.gelu(pre_gelu, approximate=False).astype(LOW)
-    slope = gelu_slope(pre_gelu)
-    act_dot = (slope * pre_dot).astype(LOW)
-    ffn_out = einsum("the,hde->td", activated, down_full)
-    ffn_dot = einsum("the,hde->td", act_dot, down_full) + einsum(
-        "the,hde->td", activated, down_step
-    )
+    up_full, up_step = zip(*(jnp.split(half, 2, axis=2) for half in up_pair))
+    down_full, down_step = zip(*(jnp.split(half, 2, axis=2) for half in down_pair))
+    pre_gelu = into(ffn_input, up_full)
+    pre_dot = [
+        part + more_part
+        for part, more_part in zip(into(hidden_dot.astype(LOW), up_full), into(ffn_input, up_step))
+    ]
+    activated = [jax.nn.gelu(part, approximate=False).astype(LOW) for part in pre_gelu]
+    slope = [gelu_slope(part) for part in pre_gelu]
+    act_dot = [(part * dot).astype(LOW) for part, dot in zip(slope, pre_dot)]
+    ffn_out = out_of(activated, down_full)
+    ffn_dot = out_of(act_dot, down_full) + out_of(activated, down_step)
     final_out, final_dot, normed_two, inverse_two = norm_pair(
         hidden + ffn_out,
         hidden_dot + ffn_dot,
@@ -468,17 +490,20 @@
     )
 
     grad_ffn = grad_two.astype(LOW)
-    grad_down = einsum("td,the->hde", grad_ffn, activated).astype(LOW)
-    grad_act = einsum("td,hde->the", grad_ffn, down_full)
-    grad_pre = (slope * grad_act).astype(LOW)
-    grad_up = einsum("td,the->hde", ffn_input, grad_pre).astype(LOW)
-    grad_hidden = grad_two + einsum("the,hde->td", grad_pre, up_full)
+
+    def outer(left, pair):
+        return [einsum("td,the->hde", left, part).astype(LOW) for part in pair]
+
+    grad_down = outer(grad_ffn, activated)
+    grad_act = into(grad_ffn, down_full)
+    grad_pre = [(part * grad).astype(LOW) for part, grad in zip(slope, grad_act)]
+    grad_up = outer(ffn_input, grad_pre)
+    grad_hidden = grad_two + out_of(grad_pre, up_full)
     grad_one, gain_one, bias_one_grad = norm_backward(
         grad_hidden, normed_one, inverse_one, gain_anchor[1]
     )
     grad_attn = grad_one.astype(LOW)
-    grad_out = einsum("td,the->hde", grad_attn, attended).astype(LOW)
-    grad_att = einsum("td,hde->the", grad_attn, out_full).astype(LOW)
+    grad_att = jnp.concatenate([part.astype(LOW) for part in into(grad_attn, out_full)], axis=1)
     grad_att = grad_att.reshape(SEQ, n_heads * local_heads, HDIM)
     grad_prob = einsum("qhd,khd->hqk", grad_att, value)
     grad_value = einsum("hqk,qhd->khd", probs_low, grad_att)
@@ -493,10 +518,20 @@
         ],
         axis=2,
     )
-    grad_qkv = einsum("td,the->hde", attn_in, grad_rows).astype(LOW)
-    grad_attn_all = jnp.concatenate([grad_qkv, grad_out], axis=2)
+    grad_rows = halves(grad_rows)
+    stacked = [
+        jnp.concatenate(
+            [
+                jnp.pad(rows, ((0, 0), (0, 0), (0, wide - three))),
+                jnp.pad(part, ((0, 0), (0, 0), (three, 0))),
+            ],
+            axis=0,
+        )
+        for rows, part in zip(grad_rows, attended)
+    ]
+    grad_attn_all = outer(jnp.concatenate([attn_in, grad_attn], axis=0), stacked)
     grad_down, grad_up, grad_attn_all = owned([grad_down, grad_up, grad_attn_all])
-    grad_start = grad_one + einsum("the,hde->td", grad_rows, attn_all[:, :, :three])
+    grad_start = grad_one + out_of(grad_rows, qkv_full)
     grad_embed, gain_zero, bias_zero = norm_backward(
         grad_start, normed_zero, inverse_zero, gain_anchor[0]
     )

time: 655 us -> 635 us (0.969)
  waiting for transfers between devices: 212 us -> 271 us
  local copies, waits for them, and re-layouts: 116 us -> 66.2 us
  other arithmetic: 117 us -> 87.2 us
  matrix products: 99.8 us -> 118 us
  loops' own time: 18.5 us -> 3.5 us
  starting transfers between devices: 67.2 us -> 60.6 us
    another operation x5 -> x0, local copies, waits for them, and re-layouts: 29.4 us -> none  [assembled(): joined = jnp.stack([block, came], axis=place)]
    another operation x14 -> x6, other arithmetic: 36.7 us -> 10.5 us  [the longest x2 6.07 us: joined(): both = jnp.stack([block, came], axis=place)]
    ppermute x30, waiting for transfers between devices: 181 us -> 206 us  [swapped(): lax.ppermute(block, axis, [(index, index ^ 1 << bit) for index in range(s...]
    all_to_all x1, waiting for transfers between devices: 0.01 us -> 22.1 us  [per_device(): message = lax.all_to_all(message, ALL, 0, 0, tiled=True)]
    dot_general x34 -> x49, matrix products: 95.1 us -> 113 us  [einsum(): return jnp.einsum(form, left, right, preferred_element_type=jnp.float32)]
    all_to_all x1, waiting for transfers between devices: 2.97 us -> 19.7 us  [give(): sums = lax.all_to_all(sums.reshape(count, room, D), ALL, 0, 0, tiled=True)]
    another operation x2, loops' own time: 18.5 us -> 3.5 us  [more(): return lax.cond(rounds > 1, rest, lambda value: value, start)]
    ppermute x8 -> x3, local copies, waits for them, and re-layouts: 20.2 us -> 7.28 us  [swapped(): lax.ppermute(block, axis, [(index, index ^ 1 << bit) for index in range(s...]
  transfers between devices with their start and end apart: 39 -> 39, of which waited for: 22 -> 22; matrix products, arithmetic and copies ran while one was open for 32% -> 26% of each run, Pallas kernels for 0% -> 0%
where the time goes in v4:
time: 635 us; the launch traced here: 625 us
  waiting for transfers between devices  271 us (43%)
  matrix products  118 us (19%)
  other arithmetic  87.2 us (14%)
  local copies, waits for them, and re-layouts  66.2 us (10%)
  starting transfers between devices  60.6 us (10%)
  between operations  11.1 us (2%)
  Pallas kernels  6.8 us (1%)
    ppermute x30, waiting for transfers between devices, swapped(): lax.ppermute(block, axis, [(index, index ^ 1 << bit) for index in range(s...  206 us
    dot_general x49, matrix products, einsum(): return jnp.einsum(form, left, right, preferred_element_type=jnp.float32)  113 us
    ppermute x30, starting transfers between devices, swapped(): lax.ppermute(block, axis, [(index, index ^ 1 << bit) for index in range(s...  27 us
    unnamed x320, local copies, waits for them, and re-layouts  25.7 us
    all_to_all x1, waiting for transfers between devices, per_device(): message = lax.all_to_all(message, ALL, 0, 0, tiled=True)  22.1 us
    all_to_all x1, waiting for transfers between devices, give(): sums = lax.all_to_all(sums.reshape(count, room, D), ALL, 0, 0, tiled=True)  19.7 us
    select_n x13, other arithmetic, joined(): both = jnp.where(upper, jnp.stack([came, block], axis=place), both)  18.4 us
    all_to_all x4, waiting for transfers between devices, everyone(): lax.all_to_all(jnp.broadcast_to(block, (count, block.shape[1])), ALL, 0,...  17.5 us
  transfers between devices with their start and end apart: 39, of which 22 were waited for; matrix products, arithmetic and copies ran while one was open for 26% of the time, Pallas kernels for 0%

profile of v4, /device:TPU:0, one launch (start us, length us, event | category | flops | bytes accessed | tf_op | source)
XLA Modules:
  0.0 624.7 jit_solution(7593725789441259804)
XLA Ops:
  27.7 22.1 %all-to-all-done.4 = f32[32,1,33]{2,1,0:T(1,128)S(1)} async-done(((f32[32,1,33]{2,1,0:T(1,128)}), f32[32,1,33]{2,1,0:T(1,128)S(1)}, u32[]{:S(2)}, u32[]{:S(2)}) %all-to-all-start.4) | async-done | bytes 4256 | tf_op jit(solution)/shard_map/all_to_all | solution.py:361
  50.1 8.3 %fusion.15 = bf16[768,1536]{1,0:T(8,128)(2,1)} fusion(bf16[1572,1536]{1,0:T(8,128)(2,1)} %pad_maximum_fusion, s32[768]{0:T(1024)S(1)} %eq.255), kind=kOutput, calls=%fused_computation.48 | convolution fusion | flops 3711200256 | bytes 7191552 | tf_op jit(solution)/shard_map/sv,vd->sd/dot_general | solution.py:31
  62.3 14.4 %collective-permute-done.3 = bf16[2,96,1536]{2,1,0:T(8,128)(2,1)S(1)} collective-permute-done((bf16[2,96,1536]{2,1,0:T(8,128)(2,1)S(1)}, bf16[2,96,1536]{2,1,0:T(8,128)(2,1)S(1)}, u32[]{:S(2)}, u32[]{:S(2)}) %collective-permute-start.3) | collective-permute-done | bytes 589856 | tf_op jit(solution)/shard_map/ppermute | solution.py:85
  82.4 24.6 %collective-permute-done.4 = bf16[2,2,96,1536]{3,2,1,0:T(8,128)(2,1)} collective-permute-done((bf16[2,2,96,1536]{3,2,1,0:T(8,128)(2,1)}, bf16[2,2,96,1536]{3,2,1,0:T(8,128)(2,1)}, u32[]{:S(2)}, u32[]{:S(2)}) %collective-permute-start.4) | collective-permute-done | bytes 1179680 | tf_op jit(solution)/shard_map/ppermute | solution.py:85
  111.1 6.6 %collective-permute-done.7 = bf16[2,96,1536]{2,1,0:T(8,128)(2,1)} collective-permute-done((bf16[2,96,1536]{2,1,0:T(8,128)(2,1)S(1)}, bf16[2,96,1536]{2,1,0:T(8,128)(2,1)}, u32[]{:S(2)}, u32[]{:S(2)}) %collective-permute-start.7) | collective-permute-done | bytes 589856 | tf_op jit(solution)/shard_map/ppermute | solution.py:85
  124.0 4.8 all-to-all-start.5
  133.9 75.1 %collective-permute-done.8 = bf16[2,2,96,1536]{3,2,1,0:T(8,128)(2,1)S(1)} collective-permute-done((bf16[2,2,96,1536]{3,2,1,0:T(8,128)(2,1)}, bf16[2,2,96,1536]{3,2,1,0:T(8,128)(2,1)S(1)}, u32[]{:S(2)}, u32[]{:S(2)}) %collective-permute-start.8) | collective-permute-done | bytes 1179680 | tf_op jit(solution)/shard_map/ppermute | solution.py:85
  213.1 5.5 maximum_select_fusion
  223.1 33.1 %collective-permute-done.9 = bf16[2,2,2,96,1536]{4,3,1,0,2:T(8,128)(2,1)S(1)} collective-permute-done((bf16[2,2,2,96,1536]{4,3,1,0,2:T(8,128)(2,1)S(1)}, bf16[2,2,2,96,1536]{4,3,1,0,2:T(8,128)(2,1)S(1)}, u32[]{:S(2)}, u32[]{:S(2)}) %collective-permute-start.9) | collective-permute-done | bytes 2359328 | tf_op jit(solution)/shard_map/ppermute | solution.py:85
  258.8 4.9 copy.352
  348.0 6.4 %fusion.133 = f32[256,768]{1,0:T(8,128)} fusion(bf16[2,768,1536]{2,1,0:T(8,128)(2,1)} %bitcast.545, f32[256,2,768]{2,0,1:T(8,128)} %fusion.30, bf16[2,768,1536]{2,1,0:T(8,128)(2,1)} %bitcast.539, f32[256,768]{1,0:T(8,128)} %copy-done.53, f32[768]{0:T(1024)S(1)} %copy-done.137, f32[768]{0:T(1024)S(1)} %copy-done.138, f32[256]{0:T(256)S(1)} %broadcast_multiply_fusion.8, ...), kind=kOutput, calls=%fused_computation.212 | convolution fusion | flops 1214447616 | bytes 10236928 | tf_op jit(solution)/shard_map/the,hde->td/dot_general | solution.py:31
  354.5 6.9 %fusion.276 = (f32[256]{0:T(256)S(1)}, f32[256]{0:T(256)S(1)}, f32[256,768]{1,0:T(8,128)}) fusion(f32[256]{0:T(256)S(1)} %add_rsqrt_fusion, f32[256,768]{1,0:T(8,128)S(1)} %get-tuple-element.596, f32[256]{0:T(256)S(1)} %broadcast_multiply_fusion.12, f32[256,768]{1,0:T(8,128)S(1)} %fusion.140, f32[256,768]{1,0:T(8,128)} %fusion.133, ...), kind=kOutput, calls=%fused_computation.523 | convolution fusion | flops 1219165696 | bytes 16551936 | tf_op jit(solution)/shard_map/the,hde->td/dot_general | solution.py:31
  366.1 5.3 all-to-all-start.6
  371.9 7.1 %all-to-all-done.6 = bf16[32,2,768]{2,1,0:T(2,128)(2,1)S(1)} async-done(((bf16[32,2,768]{2,1,0:T(2,128)(2,1)}), bf16[32,2,768]{2,1,0:T(2,128)(2,1)S(1)}, u32[]{:S(2)}, u32[]{:S(2)}) %all-to-all-start.6) | async-done | bytes 98336 | tf_op jit(solution)/shard_map/all_to_all | solution.py:65
  380.1 4.8 select_reduce_fusion.7
  394.7 5.3 all-to-all-done.7
  401.6 6.8 %shard_map.498 = (f32[4,32]{1,0:T(4,128)}, f32[1,32]{1,0:T(1,128)}, f32[1,1]{1,0:T(1,128)}) custom-call(f32[32,512]{1,0:T(8,128)} %bitcast.600, bf16[32,768]{1,0:T(8,128)(2,1)} %slice.309.feat_ref, f32[4,32]{1,0:T(4,128)} %slice_bitcast_fusion.13.targets_ref), custom_call_target="tpu_custom_call" | custom-call | tf_op jit(solution)/shard_map/pallas_call | solution.py:198
  473.6 19.7 %all-to-all-done.9 = bf16[32,24,768]{2,1,0:T(8,128)(2,1)} async-done(((bf16[32,24,768]{2,1,0:T(8,128)(2,1)}), bf16[32,24,768]{2,1,0:T(8,128)(2,1)}, u32[]{:S(2)}, u32[]{:S(2)}) %all-to-all-start.9) | async-done | bytes 1179680 | tf_op jit(solution)/shard_map/all_to_all | solution.py:345
  515.8 17.1 %collective-permute-done.16 = bf16[2,2,2,96,768]{4,3,1,2,0:T(8,128)(2,1)S(1)} collective-permute-done((bf16[2,2,2,96,768]{4,3,1,2,0:T(8,128)(2,1)S(1)}, bf16[2,2,2,96,768]{4,3,1,2,0:T(8,128)(2,1)S(1)}, u32[]{:S(2)}, u32[]{:S(2)}) %collective-permute-start.16) | collective-permute-done | bytes 1179680 | tf_op jit(solution)/shard_map/ppermute | solution.py:85
  543.2 10.4 %collective-permute-done.17 = bf16[2,2,96,768]{3,2,0,1:T(8,128)(2,1)S(1)} collective-permute-done((bf16[2,2,96,768]{3,2,0,1:T(8,128)(2,1)S(1)}, bf16[2,2,96,768]{3,2,0,1:T(8,128)(2,1)S(1)}, u32[]{:S(2)}, u32[]{:S(2)}) %collective-permute-start.17) | collective-permute-done | bytes 589856 | tf_op jit(solution)/shard_map/ppermute | solution.py:85
  557.3 4.6 collective-permute-done.18
  566.1 11.2 %collective-permute-done.19 = bf16[96,768]{1,0:T(8,128)(2,1)S(1)} collective-permute-done((bf16[96,768]{1,0:T(8,128)(2,1)S(1)}, bf16[96,768]{1,0:T(8,128)(2,1)S(1)}, u32[]{:S(2)}, u32[]{:S(2)}) %collective-permute-start.19) | collective-permute-done | bytes 147488 | tf_op jit(solution)/shard_map/ppermute | solution.py:85
  590.5 5.1 all-to-all-done.11
  607.3 13.4 %multiply_subtract_fusion = (f32[1572,768]{1,0:T(8,128)}, f32[1572,768]{1,0:T(8,128)}, f32[1572,768]{1,0:T(8,128)}) fusion(f32[1572,768]{1,0:T(8,128)} %param.51, f32[]{:T(128)} %bitcast.180, f32[]{:T(128)} %bitcast.179, f32[1572,768]{1,0:T(8,128)} %get-tuple-element.787, f32[]{:T(128)S(6)} %min.3, f32[1572,768]{1,0:T(8,128)} %param.53, f32[1572,768]{1,0:T(8,128)} %param.52), kind=kLoop, calls=%fused_computation.33 | loop fusion | flops 19316736 | bytes 33804300 | tf_op jit(solution)/shard_map/sub | solution.py:218
  (620 shorter events, 289.7 us)
Async XLA Ops:
  4.8 53.6 %collective-permute-start = (bf16[96,1536]{1,0:T(8,128)(2,1)S(1)}, bf16[96,1536]{1,0:T(8,128)(2,1)S(1)}, u32[]{:S(2)}, u32[]{:S(2)}) collective-permute-start(bf16[96,1536]{1,0:T(8,128)(2,1)S(1)} %concatenate.139), channel_id=1, source_target_pairs={{0,16},{4,20},{8,24},{12,28},{16,0},{20,4},{24,8},{28,12},{1,17},{... | collective-permute-start | bytes 884744 | tf_op jit(solution)/shard_map/ppermute | solution.py:85
  9.1 49.5 %collective-permute-start.1 = (bf16[96,1536]{1,0:T(8,128)(2,1)S(1)}, bf16[96,1536]{1,0:T(8,128)(2,1)S(1)}, u32[]{:S(2)}, u32[]{:S(2)}) collective-permute-start(bf16[96,1536]{1,0:T(8,128)(2,1)S(1)} %get-tuple-element.569), channel_id=1, source_target_pairs={{0,16},{4,20},{8,24},{12,28},{16,0},{20,4},{24,8},{28,12},{1,17},{... | collective-permute-start | bytes 884744 | tf_op jit(solution)/shard_map/ppermute | solution.py:85
  9.2 51.1 %collective-permute-start.2 = (bf16[96,1536]{1,0:T(8,128)(2,1)S(1)}, bf16[96,1536]{1,0:T(8,128)(2,1)}, u32[]{:S(2)}, u32[]{:S(2)}) collective-permute-start(bf16[96,1536]{1,0:T(8,128)(2,1)S(1)} %get-tuple-element.567), channel_id=1, source_target_pairs={{0,16},{4,20},{8,24},{12,28},{16,0},{20,4},{24,8},{28,12},{1,17},{... | collective-permute-start | bytes 884744 | tf_op jit(solution)/shard_map/ppermute | solution.py:85
  18.1 31.7 %all-to-all-start.4 = ((f32[32,1,33]{2,1,0:T(1,128)}), f32[32,1,33]{2,1,0:T(1,128)S(1)}, u32[]{:S(2)}, u32[]{:S(2)}) async-start(f32[32,1,33]{2,1,0:T(1,128)} %bitcast.17), calls=%async_computation.4 | async-start | bytes 32768 | tf_op jit(solution)/shard_map/all_to_all | solution.py:361
  77.9 29.2 %collective-permute-start.4 = (bf16[2,2,96,1536]{3,2,1,0:T(8,128)(2,1)}, bf16[2,2,96,1536]{3,2,1,0:T(8,128)(2,1)}, u32[]{:S(2)}, u32[]{:S(2)}) collective-permute-start(bf16[2,2,96,1536]{3,2,1,0:T(8,128)(2,1)} %maximum_select_fusion.6), channel_id=1, source_target_pairs={{0,2},{1,3},{2,0},{3,1},{4,6},{5,7},{6,4},{7,5},{8,10},{9,11},{10,... | collective-permute-start | bytes 3538952 | tf_op jit(solution)/shard_map/ppermute | solution.py:85
  78.5 39.2 %collective-permute-start.7 = (bf16[2,96,1536]{2,1,0:T(8,128)(2,1)S(1)}, bf16[2,96,1536]{2,1,0:T(8,128)(2,1)}, u32[]{:S(2)}, u32[]{:S(2)}) collective-permute-start(bf16[2,96,1536]{2,1,0:T(8,128)(2,1)S(1)} %maximum_select_fusion.11), channel_id=1, source_target_pairs={{0,2},{1,3},{2,0},{3,1},{4,6},{5,7},{6,4},{7,5},{8,10},{9,11},{10,... | collective-permute-start | bytes 1769480 | tf_op jit(solution)/shard_map/ppermute | solution.py:85
  81.8 47.0 %collective-permute-start.10 = (bf16[2,96,1536]{2,1,0:T(8,128)(2,1)S(1)}, bf16[2,96,1536]{2,1,0:T(8,128)(2,1)S(1)}, u32[]{:S(2)}, u32[]{:S(2)}) collective-permute-start(bf16[2,96,1536]{2,1,0:T(8,128)(2,1)S(1)} %maximum_select_fusion.12), channel_id=1, source_target_pairs={{0,4},{4,0},{8,12},{12,8},{16,20},{20,16},{24,28},{28,24},{1,5},{5... | collective-permute-start | bytes 1769480 | tf_op jit(solution)/shard_map/ppermute | solution.py:85
  110.5 102.6 %collective-permute-start.5 = (bf16[2,2,2,96,1536]{4,3,2,1,0:T(8,128)(2,1)}, bf16[2,2,2,96,1536]{4,3,2,1,0:T(8,128)(2,1)}, u32[]{:S(2)}, u32[]{:S(2)}) collective-permute-start(bf16[2,2,2,96,1536]{4,3,2,1,0:T(8,128)(2,1)} %get-tuple-element.548), channel_id=1, source_target_pairs={{0,4},{4,0},{8,12},{12,8},{16,20},{20,16},{24,28},{28,24},{1,5},{5... | collective-permute-start | bytes 7077896 | tf_op jit(solution)/shard_map/ppermute | solution.py:85
  120.9 88.1 %collective-permute-start.8 = (bf16[2,2,96,1536]{3,2,1,0:T(8,128)(2,1)}, bf16[2,2,96,1536]{3,2,1,0:T(8,128)(2,1)S(1)}, u32[]{:S(2)}, u32[]{:S(2)}) collective-permute-start(bf16[2,2,96,1536]{3,2,1,0:T(8,128)(2,1)} %get-tuple-element.560), channel_id=1, source_target_pairs={{0,4},{4,0},{8,12},{12,8},{16,20},{20,16},{24,28},{28,24},{1,5},{5... | collective-permute-start | bytes 3538952 | tf_op jit(solution)/shard_map/ppermute | solution.py:85
  124.0 144.4 %all-to-all-start.5 = ((bf16[32,24,1536]{2,1,0:T(8,128)(2,1)}), bf16[32,24,1536]{2,1,0:T(8,128)(2,1)}, u32[]{:S(2)}, u32[]{:S(2)}) async-start(bf16[32,24,1536]{2,1,0:T(8,128)(2,1)} %bitcast.561), calls=%async_computation.5 | async-start | bytes 4718592 | tf_op jit(solution)/shard_map/all_to_all | solution.py:340
  130.1 80.2 %collective-permute-start.11 = (bf16[2,2,96,1536]{3,2,0,1:T(8,128)(2,1)}, bf16[2,2,96,1536]{3,2,0,1:T(8,128)(2,1)}, u32[]{:S(2)}, u32[]{:S(2)}) collective-permute-start(bf16[2,2,96,1536]{3,2,0,1:T(8,128)(2,1)} %maximum_select_fusion.7), channel_id=1, source_target_pairs={{0,8},{4,12},{8,0},{12,4},{16,24},{20,28},{24,16},{28,20},{1,9},{5... | collective-permute-start | bytes 3538952 | tf_op jit(solution)/shard_map/ppermute | solution.py:85
  209.4 46.9 %collective-permute-start.9 = (bf16[2,2,2,96,1536]{4,3,1,0,2:T(8,128)(2,1)S(1)}, bf16[2,2,2,96,1536]{4,3,1,0,2:T(8,128)(2,1)S(1)}, u32[]{:S(2)}, u32[]{:S(2)}) collective-permute-start(bf16[2,2,2,96,1536]{4,3,1,0,2:T(8,128)(2,1)S(1)} %maximum_select_fusion.2), channel_id=1, source_target_pairs={{0,8},{4,12},{8,0},{12,4},{16,24},{20,28},{24,16},{28,20},{1,9},{5... | collective-permute-start | bytes 7077896 | tf_op jit(solution)/shard_map/ppermute | solution.py:85
  212.4 51.3 %collective-permute-start.12 = (bf16[2,2,2,96,1536]{4,3,0,2,1:T(8,128)(2,1)S(1)}, bf16[2,2,2,96,1536]{4,3,0,2,1:T(8,128)(2,1)S(1)}, u32[]{:S(2)}, u32[]{:S(2)}) collective-permute-start(bf16[2,2,2,96,1536]{4,3,0,2,1:T(8,128)(2,1)S(1)} %maximum_select_fusion.4), channel_id=1, source_target_pairs={{0,2},{1,3},{2,0},{3,1},{4,6},{5,7},{6,4},{7,5},{8,10},{9,11},{10,... | collective-permute-start | bytes 7077896 | tf_op jit(solution)/shard_map/ppermute | solution.py:85
  218.6 68.2 %collective-permute-start.6 = (bf16[2,2,2,2,96,1536]{5,4,3,2,1,0:T(8,128)(2,1)}, bf16[2,2,2,2,96,1536]{5,4,3,2,1,0:T(8,128)(2,1)}, u32[]{:S(2)}, u32[]{:S(2)}) collective-permute-start(bf16[2,2,2,2,96,1536]{5,4,3,2,1,0:T(8,128)(2,1)} %maximum_select_fusion), channel_id=1, source_target_pairs={{0,1},{1,0},{2,3},{3,2},{4,5},{5,4},{6,7},{7,6},{8,9},{9,8},{10,11... | collective-permute-start | bytes 14155784 | tf_op jit(solution)/shard_map/ppermute | solution.py:85
  258.8 52.2 %collective-permute-start.13 = (bf16[2,2,2,2,96,1536]{5,4,1,0,3,2:T(8,128)(2,1)}, bf16[2,2,2,2,96,1536]{5,4,1,0,3,2:T(8,128)(2,1)}, u32[]{:S(2)}, u32[]{:S(2)}) collective-permute-start(bf16[2,2,2,2,96,1536]{5,4,1,0,3,2:T(8,128)(2,1)} %maximum_select_fusion.1), channel_id=1, source_target_pairs={{0,1},{1,0},{2,3},{3,2},{4,5},{5,4},{6,7},{7,6},{8,9},{9,8},{10,11... | collective-permute-start | bytes 14155784 | tf_op jit(solution)/shard_map/ppermute | solution.py:85
  266.4 64.5 %collective-permute-start.14 = (bf16[2,2,2,2,96,1536]{5,4,1,3,2,0:T(8,128)(2,1)}, bf16[2,2,2,2,96,1536]{5,4,1,3,2,0:T(8,128)(2,1)}, u32[]{:S(2)}, u32[]{:S(2)}) collective-permute-start(bf16[2,2,2,2,96,1536]{5,4,1,3,2,0:T(8,128)(2,1)} %pad_maximum_fusion.1), channel_id=1, source_target_pairs={{0,1},{1,0},{2,3},{3,2},{4,5},{5,4},{6,7},{7,6},{8,9},{9,8},{10,11... | collective-permute-start | bytes 14155784 | tf_op jit(solution)/shard_map/ppermute | solution.py:85
  459.5 33.8 %all-to-all-start.9 = ((bf16[32,24,768]{2,1,0:T(8,128)(2,1)}), bf16[32,24,768]{2,1,0:T(8,128)(2,1)}, u32[]{:S(2)}, u32[]{:S(2)}) async-start(bf16[32,24,768]{2,1,0:T(8,128)(2,1)} %bitcast.140), calls=%async_computation.9 | async-start | bytes 2359296 | tf_op jit(solution)/shard_map/all_to_all | solution.py:345
  467.7 33.0 %collective-permute-start.15 = (bf16[2,768,768]{2,1,0:T(8,128)(2,1)}, bf16[2,768,768]{2,1,0:T(8,128)(2,1)}, u32[]{:S(2)}, u32[]{:S(2)}) collective-permute-start(bf16[2,768,768]{2,1,0:T(8,128)(2,1)} %convert_bitcast_fusion.2), channel_id=1, source_target_pairs={{0,1},{1,0},{2,3},{3,2},{4,5},{5,4},{6,7},{7,6},{8,9},{9,8},{10,11... | collective-permute-start | bytes 7077896 | tf_op jit(solution)/shard_map/ppermute | solution.py:85
  470.2 35.8 %collective-permute-start.20 = (bf16[2,768,768]{2,1,0:T(8,128)(2,1)}, bf16[2,768,768]{2,1,0:T(8,128)(2,1)}, u32[]{:S(2)}, u32[]{:S(2)}) collective-permute-start(bf16[2,768,768]{2,1,0:T(8,128)(2,1)} %convert_bitcast_fusion.1), channel_id=1, source_target_pairs={{0,1},{1,0},{2,3},{3,2},{4,5},{5,4},{6,7},{7,6},{8,9},{9,8},{10,11... | collective-permute-start | bytes 7077896 | tf_op jit(solution)/shard_map/ppermute | solution.py:85
  472.8 36.4 %collective-permute-start.25 = (bf16[2,768,768]{2,1,0:T(8,128)(2,1)}, bf16[2,768,768]{2,1,0:T(8,128)(2,1)}, u32[]{:S(2)}, u32[]{:S(2)}) collective-permute-start(bf16[2,768,768]{2,1,0:T(8,128)(2,1)} %convert_bitcast_fusion), channel_id=1, source_target_pairs={{0,1},{1,0},{2,3},{3,2},{4,5},{5,4},{6,7},{7,6},{8,9},{9,8},{10,11... | collective-permute-start | bytes 7077896 | tf_op jit(solution)/shard_map/ppermute | solution.py:85
  505.2 27.7 %collective-permute-start.16 = (bf16[2,2,2,96,768]{4,3,1,2,0:T(8,128)(2,1)S(1)}, bf16[2,2,2,96,768]{4,3,1,2,0:T(8,128)(2,1)S(1)}, u32[]{:S(2)}, u32[]{:S(2)}) collective-permute-start(bf16[2,2,2,96,768]{4,3,1,2,0:T(8,128)(2,1)S(1)} %bitcast.582), channel_id=1, source_target_pairs={{0,4},{4,0},{8,12},{12,8},{16,20},{20,16},{24,28},{28,24},{1,5},{5... | collective-permute-start | bytes 3538952 | tf_op jit(solution)/shard_map/ppermute | solution.py:85
  509.0 27.7 %collective-permute-start.21 = (bf16[2,2,2,96,768]{4,3,1,0,2:T(8,128)(2,1)S(1)}, bf16[2,2,2,96,768]{4,3,1,0,2:T(8,128)(2,1)S(1)}, u32[]{:S(2)}, u32[]{:S(2)}) collective-permute-start(bf16[2,2,2,96,768]{4,3,1,0,2:T(8,128)(2,1)S(1)} %bitcast.583), channel_id=1, source_target_pairs={{0,8},{4,12},{8,0},{12,4},{16,24},{20,28},{24,16},{28,20},{1,9},{5... | collective-permute-start | bytes 3538952 | tf_op jit(solution)/shard_map/ppermute | solution.py:85
  513.4 28.9 %collective-permute-start.26 = (bf16[2,2,2,96,768]{4,3,0,2,1:T(8,128)(2,1)S(1)}, bf16[2,2,2,96,768]{4,3,0,2,1:T(8,128)(2,1)S(1)}, u32[]{:S(2)}, u32[]{:S(2)}) collective-permute-start(bf16[2,2,2,96,768]{4,3,0,2,1:T(8,128)(2,1)S(1)} %copy.386), channel_id=1, source_target_pairs={{0,2},{1,3},{2,0},{3,1},{4,6},{5,7},{6,4},{7,5},{8,10},{9,11},{10,... | collective-permute-start | bytes 3538952 | tf_op jit(solution)/shard_map/ppermute | solution.py:85
  533.2 20.4 %collective-permute-start.17 = (bf16[2,2,96,768]{3,2,0,1:T(8,128)(2,1)S(1)}, bf16[2,2,96,768]{3,2,0,1:T(8,128)(2,1)S(1)}, u32[]{:S(2)}, u32[]{:S(2)}) collective-permute-start(bf16[2,2,96,768]{3,2,0,1:T(8,128)(2,1)S(1)} %slice_bitcast_fusion), channel_id=1, source_target_pairs={{0,2},{1,3},{2,0},{3,1},{4,6},{5,7},{6,4},{7,5},{8,10},{9,11},{10,... | collective-permute-start | bytes 1769480 | tf_op jit(solution)/shard_map/ppermute | solution.py:85
  (168 other events, 2790.4 us)

commit v5 on v2

--- a/solution.py
+++ b/solution.py
@@ -71,29 +71,40 @@
     return [(axis, bit) for bit in reversed(range(lax.axis_size(axis).bit_length() - 1))]
 
 
-def owned(parts):
+def plan():
     layout = [bit for axis in ALL for bit in bits_of(axis)]
     first = (ALL[0], 0)
     last = [bit for bit in layout if bit[0] == ALL[1] and bit[1] >= 2]
     middle = [bit for bit in layout if bit != first and bit not in last]
+    return layout, first, middle, last
+
+
+def halved(block, left, step):
+    axis, bit = step
+    place = left.index(step)
+    mine = (lax.axis_index(axis) >> bit) & 1
+    send = lax.dynamic_index_in_dim(block, 1 - mine, place, keepdims=False)
+    keep = lax.dynamic_index_in_dim(block, mine, place, keepdims=False)
+    size = lax.axis_size(axis)
+    came = lax.ppermute(send, axis, [(index, index ^ (1 << bit)) for index in range(size)])
+    block = keep.astype(jnp.float32) + came.astype(jnp.float32)
+    left = [other for other in left if other != step]
+    return (block.astype(LOW) if left else block), left
+
+
+def begun(part):
+    layout, first, _, _ = plan()
+    block = part.reshape((2,) * len(layout) + (-1, part.shape[-1]))
+    return halved(block, layout, first)[0]
+
+
+def finished(blocks, turns):
+    layout, first, middle, last = plan()
     results = []
-    for turn, part in enumerate(parts):
-        turn %= len(middle)
-        order = [first] + middle[turn:] + middle[:turn] + last[::-1]
-        left = list(layout)
-        block = part.reshape((2,) * len(layout) + (-1, part.shape[-1]))
-        for step in order:
-            axis, bit = step
-            place = left.index(step)
-            mine = (lax.axis_index(axis) >> bit) & 1
-            send = lax.dynamic_index_in_dim(block, 1 - mine, place, keepdims=False)
-            keep = lax.dynamic_index_in_dim(block, mine, place, keepdims=False)
-            size = lax.axis_size(axis)
-            came = lax.ppermute(send, axis, [(index, index ^ (1 << bit)) for index in range(size)])
-            block = keep.astype(jnp.float32) + came.astype(jnp.float32)
-            left.pop(place)
-            if left:
-                block = block.astype(LOW)
+    for block, turn in zip(blocks, turns):
+        left = [bit for bit in layout if bit != first]
+        for step in middle[turn:] + middle[:turn] + last[::-1]:
+            block, left = halved(block, left, step)
         results.append(block)
     return results
 
@@ -442,8 +453,9 @@
         grad_hidden, normed_one, inverse_one, gain_anchor[1]
     )
     grad_attn = grad_one.astype(LOW)
-    grad_out = einsum("td,the->hde", grad_attn, attended).astype(LOW)
+    begun_ffn = [begun(grad_down), begun(grad_up)]
     grad_att = einsum("td,hde->the", grad_attn, out_full).astype(LOW)
+    grad_att, begun_ffn = lax.optimization_barrier((grad_att, begun_ffn))
     grad_att = grad_att.reshape(SEQ, n_heads * local_heads, HDIM)
     grad_prob = einsum("qhd,khd->hqk", grad_att, value)
     grad_value = einsum("hqk,qhd->khd", probs_low, grad_att)
@@ -458,9 +470,19 @@
         ],
         axis=2,
     )
-    grad_qkv = einsum("td,the->hde", attn_in, grad_rows).astype(LOW)
-    grad_attn_all = jnp.concatenate([grad_qkv, grad_out], axis=2)
-    grad_down, grad_up, grad_attn_all = owned([grad_down, grad_up, grad_attn_all])
+    pair = 2 * group_wide
+    grad_front = einsum("td,the->hde", attn_in, grad_rows[:, :, :pair]).astype(LOW)
+    tail = jnp.concatenate(
+        [
+            jnp.pad(grad_rows[:, :, pair:], ((0, 0), (0, 0), (0, group_wide))),
+            jnp.pad(attended, ((0, 0), (0, 0), (group_wide, 0))),
+        ],
+        axis=0,
+    )
+    grad_tail = einsum("td,the->hde", jnp.concatenate([attn_in, grad_attn], axis=0), tail)
+    begun_attn = [begun(grad_front), begun(grad_tail.astype(LOW))]
+    grad_down, grad_up, grad_front, grad_tail = finished(begun_ffn + begun_attn, (0, 1, 2, 0))
+    grad_attn_all = jnp.concatenate([grad_front, grad_tail], axis=1)
     grad_start = grad_one + einsum("the,hde->td", grad_rows, attn_all[:, :, :three])
     grad_embed, gain_zero, bias_zero = norm_backward(
         grad_start, normed_zero, inverse_zero, gain_anchor[0]

time: 569 us -> 587 us (1.032)
  starting transfers between devices: 45 us -> 64.9 us
  waiting for transfers between devices: 242 us -> 234 us
    ppermute x15 -> x20, starting transfers between devices: 12.6 us -> 28.7 us  [halved(): lax.ppermute(send, axis, [(index, index ^ 1 << bit) for index in range(si...]
    concatenate x1 -> x0, local copies, waits for them, and re-layouts: 6.61 us -> none  [per_device(): grad_attn_all = jnp.concatenate([grad_qkv, grad_out], axis=2)]
    convert_element_type x0 -> x2, local copies, waits for them, and re-layouts: none -> 5.99 us  [the longest x1 2.99 us: per_device(): begun_attn = [begun(grad_front), begun(grad_tail.astype(LOW))]]
    ppermute x15 -> x20, waiting for transfers between devices: 44.8 us -> 41.6 us  [halved(): lax.ppermute(send, axis, [(index, index ^ 1 << bit) for index in range(si...]
    convert_element_type x12 -> x17, other arithmetic: 12.8 us -> 14.9 us  [the longest x16 14.6 us: halved(): return (block.astype(LOW) if left else block, left)]
  transfers between devices with their start and end apart: 26 -> 31, of which waited for: 19 -> 14; matrix products, arithmetic and copies ran while one was open for 23% -> 22% of each run, Pallas kernels for 0% -> 0%
where the time goes in v5:
time: 587 us; the launch traced here: 577 us
  waiting for transfers between devices  234 us (40%)
  matrix products  98.9 us (17%)
  other arithmetic  77 us (13%)
  local copies, waits for them, and re-layouts  65.6 us (11%)
  starting transfers between devices  64.9 us (11%)
  between operations  24.1 us (4%)
  Pallas kernels  6.8 us (1%)
    dot_general x34, matrix products, einsum(): return jnp.einsum(form, left, right, preferred_element_type=jnp.float32)  94.3 us
    all_to_all x1, waiting for transfers between devices, fetch(): lax.all_to_all(rows.reshape(count, room, 2 * D), ALL, 0, 0, tiled=True)  83.9 us
    all_gather x2, waiting for transfers between devices, gathered(): full = lax.all_gather(block, ALL, axis=0, tiled=True)  81.6 us
    ppermute x20, waiting for transfers between devices, halved(): lax.ppermute(send, axis, [(index, index ^ 1 << bit) for index in range(si...  41.6 us
    ppermute x20, starting transfers between devices, halved(): lax.ppermute(send, axis, [(index, index ^ 1 << bit) for index in range(si...  28.7 us
    all_to_all x4, waiting for transfers between devices, everyone(): lax.all_to_all(jnp.broadcast_to(block, (count, block.shape[1])), ALL, 0,...  18.3 us
    sub x5, other arithmetic, adam_update(): master - LEARN_RATE * (direction + DECAY_RATE * master)  16.9 us
    unnamed x247, local copies, waits for them, and re-layouts  15.2 us
  transfers between devices with their start and end apart: 31, of which 14 were waited for; matrix products, arithmetic and copies ran while one was open for 22% of the time, Pallas kernels for 0%

profile of v5, /device:TPU:0, one launch (start us, length us, event | category | flops | bytes accessed | tf_op | source)
XLA Modules:
  0.0 577.2 jit_solution(542986298771739796)
XLA Ops:
  19.8 7.3 %all-to-all-start.4 = ((f32[32,1,33]{2,1,0:T(1,128)}), f32[32,1,33]{2,1,0:T(1,128)S(1)}, u32[]{:S(2)}, u32[]{:S(2)}) async-start(f32[32,1,33]{2,1,0:T(1,128)} %bitcast.17), calls=%async_computation.4 | async-start | bytes 32768 | tf_op jit(solution)/shard_map/all_to_all | solution.py:329
  34.5 8.3 %fusion.34 = bf16[768,1536]{1,0:T(8,128)(2,1)} fusion(bf16[1572,1536]{1,0:T(8,128)(2,1)} %pad_maximum_fusion, s32[768]{0:T(1024)S(1)} %eq.255), kind=kOutput, calls=%fused_computation.63 | convolution fusion | flops 3711200256 | bytes 7191552 | tf_op jit(solution)/shard_map/sv,vd->sd/dot_general | solution.py:31
  51.3 83.9 %all-to-all-done.5 = bf16[32,24,1536]{2,1,0:T(8,128)(2,1)S(1)} async-done(((bf16[32,24,1536]{2,1,0:T(8,128)(2,1)}), bf16[32,24,1536]{2,1,0:T(8,128)(2,1)S(1)}, u32[]{:S(2)}, u32[]{:S(2)}) %all-to-all-start.5) | async-done | bytes 2359328 | tf_op jit(solution)/shard_map/all_to_all | solution.py:308
  141.7 5.5 fusion.172
  175.8 81.6 %all-gather.5.cloned.1.call-done = bf16[3072,3072]{1,0:T(8,128)(2,1)} async-done(((bf16[96,3072]{1,0:T(8,128)(2,1)}), bf16[3072,3072]{1,0:T(8,128)(2,1)}) %all-gather.5.cloned.1.call-update) | async-done | bytes 18874384 | tf_op jit(solution)/shard_map/all_gather | solution.py:255
  257.4 4.5 fusion.152
  262.0 7.4 %fusion.37 = bf16[256,4,768]{2,0,1:T(8,128)(2,1)S(1)} fusion(f32[256,4,768]{2,0,1:T(8,128)S(1)} %get-tuple-element.596, u8[256,768]{1,0:T(8,128)(4,1)S(1)} %get-tuple-element.453, u8[256,768]{1,0:T(8,128)(4,1)S(1)} %get-tuple-element.452), kind=kLoop, calls=%fused_computation.66 | loop fusion | flops 55050240 | bytes 5111808 | tf_op jit(solution)/shard_map/convert_element_type | solution.py:400
  276.6 9.8 %fusion.232 = (f32[256]{0:T(256)S(1)}, f32[256]{0:T(256)S(1)}, f32[256,768]{1,0:T(8,128)}) fusion(f32[256]{0:T(256)S(1)} %add_rsqrt_fusion, f32[256,768]{1,0:T(8,128)S(1)} %get-tuple-element.598, f32[256]{0:T(256)S(1)} %broadcast_multiply_fusion.12, f32[256,768]{1,0:T(8,128)} %fusion.93, bf16[4,768,3072]{2,1,0:T(8,128)(2,1)} %bitcast.508, ...), kind=kOutput, calls=%fused_computation.444 | convolution fusion | flops 2430074368 | bytes 21270528 | tf_op jit(solution)/shard_map/the,hde->td/dot_general | solution.py:31
  295.4 6.2 %all-to-all-done.6 = bf16[32,2,768]{2,1,0:T(2,128)(2,1)S(1)} async-done(((bf16[32,2,768]{2,1,0:T(2,128)(2,1)}), bf16[32,2,768]{2,1,0:T(2,128)(2,1)S(1)}, u32[]{:S(2)}, u32[]{:S(2)}) %all-to-all-start.6) | async-done | bytes 98336 | tf_op jit(solution)/shard_map/all_to_all | solution.py:65
  303.1 4.8 select_reduce_fusion.7
  319.2 6.0 %all-to-all-done.7 = f32[32,1,512]{2,1,0:T(1,128)} async-done(((f32[32,1,512]{2,1,0:T(1,128)}), f32[32,1,512]{2,1,0:T(1,128)}, u32[]{:S(2)}, u32[]{:S(2)}) %all-to-all-start.7) | async-done | bytes 65568 | tf_op jit(solution)/shard_map/all_to_all | solution.py:65
  326.7 6.8 %shard_map.498 = (f32[4,32]{1,0:T(4,128)}, f32[1,32]{1,0:T(1,128)}, f32[1,1]{1,0:T(1,128)}) custom-call(f32[32,512]{1,0:T(8,128)} %bitcast.476, bf16[32,768]{1,0:T(8,128)(2,1)} %slice.236.feat_ref, f32[4,32]{1,0:T(4,128)} %slice_bitcast_fusion.9.targets_ref), custom_call_target="tpu_custom_call" | custom-call | tf_op jit(solution)/shard_map/pallas_call | solution.py:166
  339.7 7.6 %all-to-all-done.8 = f32[32,1,768]{2,1,0:T(1,128)S(1)} async-done(((f32[32,1,768]{2,1,0:T(1,128)}), f32[32,1,768]{2,1,0:T(1,128)S(1)}, u32[]{:S(2)}, u32[]{:S(2)}) %all-to-all-start.8) | async-done | bytes 98336 | tf_op jit(solution)/shard_map/all_to_all | solution.py:439
  349.7 5.0 multiply_convert_fusion.1
  370.4 5.0 multiply_reduce_fusion.3
  391.9 4.9 multiply_reduce_fusion.4
  427.6 7.6 %collective-permute-done.16 = bf16[2,2,2,96,768]{4,3,0,2,1:T(8,128)(2,1)} collective-permute-done((bf16[2,2,2,96,768]{4,3,0,2,1:T(8,128)(2,1)}, bf16[2,2,2,96,768]{4,3,0,2,1:T(8,128)(2,1)}, u32[]{:S(2)}, u32[]{:S(2)}) %collective-permute-start.16) | collective-permute-done | bytes 1179680 | tf_op jit(solution)/shard_map/ppermute | solution.py:89
  450.7 17.3 %collective-permute-done.17 = bf16[2,2,96,768]{3,2,0,1:T(8,128)(2,1)S(1)} collective-permute-done((bf16[2,2,96,768]{3,2,0,1:T(8,128)(2,1)S(1)}, bf16[2,2,96,768]{3,2,0,1:T(8,128)(2,1)S(1)}, u32[]{:S(2)}, u32[]{:S(2)}) %collective-permute-start.17) | collective-permute-done | bytes 589856 | tf_op jit(solution)/shard_map/ppermute | solution.py:89
  470.6 7.5 %collective-permute-done.3 = bf16[2,2,2,96,384]{4,3,2,1,0:T(8,128)(2,1)S(1)} collective-permute-done((bf16[2,2,2,96,384]{4,3,2,1,0:T(8,128)(2,1)S(1)}, bf16[2,2,2,96,384]{4,3,2,1,0:T(8,128)(2,1)S(1)}, u32[]{:S(2)}, u32[]{:S(2)}) %collective-permute-start.3) | collective-permute-done | bytes 589856 | tf_op jit(solution)/shard_map/ppermute | solution.py:89
  493.7 7.5 %collective-permute-start.6 = (bf16[96,384]{1,0:T(8,128)(2,1)S(1)}, bf16[96,384]{1,0:T(8,128)(2,1)S(1)}, u32[]{:S(2)}, u32[]{:S(2)}) collective-permute-start(bf16[96,384]{1,0:T(8,128)(2,1)S(1)} %dynamic-slice_bitcast_fusion.16), channel_id=1, source_target_pairs={{0,16},{4,20},{8,24},{12,28},{16,0},{20,4},{24,8},{28,12},{1,17},{... | collective-permute-start | bytes 221192 | tf_op jit(solution)/shard_map/ppermute | solution.py:89
  511.3 5.6 conditional.3
  525.9 5.2 all-to-all-start.11
  533.0 5.1 all-to-all-done.11
  552.9 13.5 %multiply_subtract_fusion = (f32[1572,768]{1,0:T(8,128)}, f32[1572,768]{1,0:T(8,128)}, f32[1572,768]{1,0:T(8,128)}) fusion(f32[1572,768]{1,0:T(8,128)} %param.51, f32[]{:T(128)} %bitcast.153, f32[]{:T(128)} %bitcast.152, f32[1572,768]{1,0:T(8,128)} %get-tuple-element.791, f32[]{:T(128)S(6)} %min.3, f32[1572,768]{1,0:T(8,128)} %param.53, f32[1572,768]{1,0:T(8,128)} %param.52), kind=kLoop, calls=%fused_computation.33 | loop fusion | flops 19316736 | bytes 33804300 | tf_op jit(solution)/shard_map/sub | solution.py:186
  (499 shorter events, 229.3 us)
Async XLA Ops:
  7.2 134.4 %all-gather.3.cloned.1.call-start = ((), (), s32[]{:S(2)}) async-start(), calls=%async_computation.13 | async-start | bytes 9732096 | tf_op jit(solution)/shard_map/all_gather | solution.py:255
  12.1 245.4 %all-gather.5.cloned.1.call-start = ((), (), s32[]{:S(2)}) async-start(), calls=%async_computation.14 | async-start | bytes 19464192 | tf_op jit(solution)/shard_map/all_gather | solution.py:255
  19.8 14.4 %all-to-all-start.4 = ((f32[32,1,33]{2,1,0:T(1,128)}), f32[32,1,33]{2,1,0:T(1,128)S(1)}, u32[]{:S(2)}, u32[]{:S(2)}) async-start(f32[32,1,33]{2,1,0:T(1,128)} %bitcast.17), calls=%async_computation.4 | async-start | bytes 32768 | tf_op jit(solution)/shard_map/all_to_all | solution.py:329
  42.8 92.4 %all-to-all-start.5 = ((bf16[32,24,1536]{2,1,0:T(8,128)(2,1)}), bf16[32,24,1536]{2,1,0:T(8,128)(2,1)S(1)}, u32[]{:S(2)}, u32[]{:S(2)}) async-start(bf16[32,24,1536]{2,1,0:T(8,128)(2,1)} %bitcast.452), calls=%async_computation.5 | async-start | bytes 4718592 | tf_op jit(solution)/shard_map/all_to_all | solution.py:308
  358.1 20.0 %collective-permute-start.1 = (bf16[2,2,2,2,96,768]{5,4,1,0,3,2:T(8,128)(2,1)}, bf16[2,2,2,2,96,768]{5,4,1,0,3,2:T(8,128)(2,1)}, u32[]{:S(2)}, u32[]{:S(2)}) collective-permute-start(bf16[2,2,2,2,96,768]{5,4,1,0,3,2:T(8,128)(2,1)} %bitcast.400), channel_id=1, source_target_pairs={{0,1},{1,0},{2,3},{3,2},{4,5},{5,4},{6,7},{7,6},{8,9},{9,8},{10,11... | collective-permute-start | bytes 7077896 | tf_op jit(solution)/shard_map/ppermute | solution.py:89
  364.0 18.0 %collective-permute-start = (bf16[2,2,2,2,96,768]{5,4,1,3,2,0:T(8,128)(2,1)}, bf16[2,2,2,2,96,768]{5,4,1,3,2,0:T(8,128)(2,1)}, u32[]{:S(2)}, u32[]{:S(2)}) collective-permute-start(bf16[2,2,2,2,96,768]{5,4,1,3,2,0:T(8,128)(2,1)} %bitcast.401), channel_id=1, source_target_pairs={{0,1},{1,0},{2,3},{3,2},{4,5},{5,4},{6,7},{7,6},{8,9},{9,8},{10,11... | collective-permute-start | bytes 7077896 | tf_op jit(solution)/shard_map/ppermute | solution.py:89
  400.5 22.6 %all-to-all-start.10 = ((f32[32,1,144]{2,1,0:T(1,128)}), f32[32,1,144]{2,1,0:T(1,128)S(1)}, u32[]{:S(2)}, u32[]{:S(2)}) async-start(f32[32,1,144]{2,1,0:T(1,128)} %all_to_all.84), calls=%async_computation.10 | async-start | bytes 65536 | tf_op jit(solution)/shard_map/all_to_all | solution.py:497
  405.6 29.6 %collective-permute-start.16 = (bf16[2,2,2,96,768]{4,3,0,2,1:T(8,128)(2,1)}, bf16[2,2,2,96,768]{4,3,0,2,1:T(8,128)(2,1)}, u32[]{:S(2)}, u32[]{:S(2)}) collective-permute-start(bf16[2,2,2,96,768]{4,3,0,2,1:T(8,128)(2,1)} %dynamic-slice_bitcast_fusion), channel_id=1, source_target_pairs={{0,2},{1,3},{2,0},{3,1},{4,6},{5,7},{6,4},{7,5},{8,10},{9,11},{10,... | collective-permute-start | bytes 3538952 | tf_op jit(solution)/shard_map/ppermute | solution.py:89
  408.5 35.9 %collective-permute-start.12 = (bf16[2,2,2,96,768]{4,3,1,0,2:T(8,128)(2,1)}, bf16[2,2,2,96,768]{4,3,1,0,2:T(8,128)(2,1)}, u32[]{:S(2)}, u32[]{:S(2)}) collective-permute-start(bf16[2,2,2,96,768]{4,3,1,0,2:T(8,128)(2,1)} %dynamic-slice_bitcast_fusion.1), channel_id=1, source_target_pairs={{0,8},{4,12},{8,0},{12,4},{16,24},{20,28},{24,16},{28,20},{1,9},{5... | collective-permute-start | bytes 3538952 | tf_op jit(solution)/shard_map/ppermute | solution.py:89
  414.8 33.1 %collective-permute-start.2 = (bf16[2,2,2,2,96,384]{5,4,3,2,1,0:T(8,128)(2,1)}, bf16[2,2,2,2,96,384]{5,4,3,2,1,0:T(8,128)(2,1)}, u32[]{:S(2)}, u32[]{:S(2)}) collective-permute-start(bf16[2,2,2,2,96,384]{5,4,3,2,1,0:T(8,128)(2,1)} %dynamic-slice_bitcast_fusion.2), channel_id=1, source_target_pairs={{0,1},{1,0},{2,3},{3,2},{4,5},{5,4},{6,7},{7,6},{8,9},{9,8},{10,11... | collective-permute-start | bytes 3538952 | tf_op jit(solution)/shard_map/ppermute | solution.py:89
  419.3 30.9 %collective-permute-start.7 = (bf16[2,2,2,2,96,384]{5,4,1,3,2,0:T(8,128)(2,1)S(1)}, bf16[2,2,2,2,96,384]{5,4,1,3,2,0:T(8,128)(2,1)S(1)}, u32[]{:S(2)}, u32[]{:S(2)}) collective-permute-start(bf16[2,2,2,2,96,384]{5,4,1,3,2,0:T(8,128)(2,1)S(1)} %bitcast.466), channel_id=1, source_target_pairs={{0,1},{1,0},{2,3},{3,2},{4,5},{5,4},{6,7},{7,6},{8,9},{9,8},{10,11... | collective-permute-start | bytes 3538952 | tf_op jit(solution)/shard_map/ppermute | solution.py:89
  423.0 81.0 %all-to-all-start.9 = ((bf16[32,24,768]{2,1,0:T(8,128)(2,1)}), bf16[32,24,768]{2,1,0:T(8,128)(2,1)}, u32[]{:S(2)}, u32[]{:S(2)}) async-start(bf16[32,24,768]{2,1,0:T(8,128)(2,1)} %bitcast.105), calls=%async_computation.9 | async-start | bytes 2359296 | tf_op jit(solution)/shard_map/all_to_all | solution.py:313
  437.2 30.8 %collective-permute-start.17 = (bf16[2,2,96,768]{3,2,0,1:T(8,128)(2,1)S(1)}, bf16[2,2,96,768]{3,2,0,1:T(8,128)(2,1)S(1)}, u32[]{:S(2)}, u32[]{:S(2)}) collective-permute-start(bf16[2,2,96,768]{3,2,0,1:T(8,128)(2,1)S(1)} %dynamic-slice_bitcast_fusion.3), channel_id=1, source_target_pairs={{0,8},{4,12},{8,0},{12,4},{16,24},{20,28},{24,16},{28,20},{1,9},{5... | collective-permute-start | bytes 1769480 | tf_op jit(solution)/shard_map/ppermute | solution.py:89
  446.4 23.4 %collective-permute-start.13 = (bf16[2,2,96,768]{3,2,1,0:T(8,128)(2,1)S(1)}, bf16[2,2,96,768]{3,2,1,0:T(8,128)(2,1)S(1)}, u32[]{:S(2)}, u32[]{:S(2)}) collective-permute-start(bf16[2,2,96,768]{3,2,1,0:T(8,128)(2,1)S(1)} %dynamic-slice_bitcast_fusion.4), channel_id=1, source_target_pairs={{0,4},{4,0},{8,12},{12,8},{16,20},{20,16},{24,28},{28,24},{1,5},{5... | collective-permute-start | bytes 1769480 | tf_op jit(solution)/shard_map/ppermute | solution.py:89
  449.6 28.5 %collective-permute-start.3 = (bf16[2,2,2,96,384]{4,3,2,1,0:T(8,128)(2,1)S(1)}, bf16[2,2,2,96,384]{4,3,2,1,0:T(8,128)(2,1)S(1)}, u32[]{:S(2)}, u32[]{:S(2)}) collective-permute-start(bf16[2,2,2,96,384]{4,3,2,1,0:T(8,128)(2,1)S(1)} %dynamic-slice_bitcast_fusion.6), channel_id=1, source_target_pairs={{0,4},{4,0},{8,12},{12,8},{16,20},{20,16},{24,28},{28,24},{1,5},{5... | collective-permute-start | bytes 1769480 | tf_op jit(solution)/shard_map/ppermute | solution.py:89
  450.6 28.5 %collective-permute-start.8 = (bf16[2,2,2,96,384]{4,3,0,2,1:T(8,128)(2,1)S(1)}, bf16[2,2,2,96,384]{4,3,0,2,1:T(8,128)(2,1)S(1)}, u32[]{:S(2)}, u32[]{:S(2)}) collective-permute-start(bf16[2,2,2,96,384]{4,3,0,2,1:T(8,128)(2,1)S(1)} %dynamic-slice_bitcast_fusion.5), channel_id=1, source_target_pairs={{0,2},{1,3},{2,0},{3,1},{4,6},{5,7},{6,4},{7,5},{8,10},{9,11},{10,... | collective-permute-start | bytes 1769480 | tf_op jit(solution)/shard_map/ppermute | solution.py:89
  468.2 13.8 %collective-permute-start.18 = (bf16[2,96,768]{2,1,0:T(8,128)(2,1)S(1)}, bf16[2,96,768]{2,1,0:T(8,128)(2,1)S(1)}, u32[]{:S(2)}, u32[]{:S(2)}) collective-permute-start(bf16[2,96,768]{2,1,0:T(8,128)(2,1)S(1)} %dynamic-slice_bitcast_fusion.7), channel_id=1, source_target_pairs={{0,4},{4,0},{8,12},{12,8},{16,20},{20,16},{24,28},{28,24},{1,5},{5... | collective-permute-start | bytes 884744 | tf_op jit(solution)/shard_map/ppermute | solution.py:89
  470.0 15.9 %collective-permute-start.14 = (bf16[2,96,768]{2,1,0:T(8,128)(2,1)S(1)}, bf16[2,96,768]{2,1,0:T(8,128)(2,1)S(1)}, u32[]{:S(2)}, u32[]{:S(2)}) collective-permute-start(bf16[2,96,768]{2,1,0:T(8,128)(2,1)S(1)} %dynamic-slice_bitcast_fusion.8), channel_id=1, source_target_pairs={{0,2},{1,3},{2,0},{3,1},{4,6},{5,7},{6,4},{7,5},{8,10},{9,11},{10,... | collective-permute-start | bytes 884744 | tf_op jit(solution)/shard_map/ppermute | solution.py:89
  482.1 19.2 %collective-permute-start.19 = (bf16[96,768]{1,0:T(8,128)(2,1)S(1)}, bf16[96,768]{1,0:T(8,128)(2,1)S(1)}, u32[]{:S(2)}, u32[]{:S(2)}) collective-permute-start(bf16[96,768]{1,0:T(8,128)(2,1)S(1)} %dynamic-slice_bitcast_fusion.11), channel_id=1, source_target_pairs={{0,16},{4,20},{8,24},{12,28},{16,0},{20,4},{24,8},{28,12},{1,17},{... | collective-permute-start | bytes 442376 | tf_op jit(solution)/shard_map/ppermute | solution.py:89
  485.9 16.8 %collective-permute-start.15 = (bf16[96,768]{1,0:T(8,128)(2,1)S(1)}, bf16[96,768]{1,0:T(8,128)(2,1)S(1)}, u32[]{:S(2)}, u32[]{:S(2)}) collective-permute-start(bf16[96,768]{1,0:T(8,128)(2,1)S(1)} %dynamic-slice_bitcast_fusion.12), channel_id=1, source_target_pairs={{0,16},{4,20},{8,24},{12,28},{16,0},{20,4},{24,8},{28,12},{1,17},{... | collective-permute-start | bytes 442376 | tf_op jit(solution)/shard_map/ppermute | solution.py:89
  489.5 11.7 %collective-permute-start.10 = (bf16[2,96,384]{2,1,0:T(8,128)(2,1)S(1)}, bf16[2,96,384]{2,1,0:T(8,128)(2,1)S(1)}, u32[]{:S(2)}, u32[]{:S(2)}) collective-permute-start(bf16[2,96,384]{2,1,0:T(8,128)(2,1)S(1)} %dynamic-slice_bitcast_fusion.13), channel_id=1, source_target_pairs={{0,4},{4,0},{8,12},{12,8},{16,20},{20,16},{24,28},{28,24},{1,5},{5... | collective-permute-start | bytes 442376 | tf_op jit(solution)/shard_map/ppermute | solution.py:89
  493.7 27.6 %collective-permute-start.6 = (bf16[96,384]{1,0:T(8,128)(2,1)S(1)}, bf16[96,384]{1,0:T(8,128)(2,1)S(1)}, u32[]{:S(2)}, u32[]{:S(2)}) collective-permute-start(bf16[96,384]{1,0:T(8,128)(2,1)S(1)} %dynamic-slice_bitcast_fusion.16), channel_id=1, source_target_pairs={{0,16},{4,20},{8,24},{12,28},{16,0},{20,4},{24,8},{28,12},{1,17},{... | collective-permute-start | bytes 221192 | tf_op jit(solution)/shard_map/ppermute | solution.py:89
  501.3 20.0 %collective-permute-start.11 = (bf16[96,384]{1,0:T(8,128)(2,1)S(1)}, bf16[96,384]{1,0:T(8,128)(2,1)S(1)}, u32[]{:S(2)}, u32[]{:S(2)}) collective-permute-start(bf16[96,384]{1,0:T(8,128)(2,1)S(1)} %dynamic-slice_bitcast_fusion.15), channel_id=1, source_target_pairs={{0,16},{4,20},{8,24},{12,28},{16,0},{20,4},{24,8},{28,12},{1,17},{... | collective-permute-start | bytes 221192 | tf_op jit(solution)/shard_map/ppermute | solution.py:89
  525.9 12.2 %all-to-all-start.11 = ((f32[32,1,128]{2,1,0:T(1,128)}), f32[32,1,128]{2,1,0:T(1,128)S(1)}, u32[]{:S(2)}, u32[]{:S(2)}) async-start(f32[32,1,128]{2,1,0:T(1,128)} %broadcast_in_dim_broadcast_in_dim.3), calls=%async_computation.11 | async-start | bytes 32768 | tf_op jit(solution)/shard_map/all_to_all | solution.py:65
  (124 other events, 2692.3 us)
Sparse Core Ops, SparseCore 0:
  12.2 121.0 all-gather.2
  136.2 121.1 all-gather.4

commit v6 on v2

--- a/solution.py
+++ b/solution.py
@@ -474,11 +474,12 @@
     )
     pieces = lax.all_to_all(norm_grads.reshape(count, -1), ALL, 0, 0, tiled=True)
     piece = jnp.sum(pieces, axis=0, keepdims=True)
-    gain_grad, bias_grad = everyone(piece).reshape(2, 3, D)
     squares = sum(
         jnp.sum(part * part) for part in (table_grad, grad_attn_all, grad_up, grad_down, piece)
     )
-    squares = jnp.sum(everyone(jnp.broadcast_to(squares, (1, 128)))[:, 0])
+    shared = everyone(jnp.concatenate([jnp.broadcast_to(squares, (1, 128)), piece], axis=1))
+    gain_grad, bias_grad = shared[:, 128:].reshape(2, 3, D)
+    squares = jnp.sum(shared[:, 0])
     clip_scale = jnp.minimum(1.0, CLIP_NORM / jnp.sqrt(squares))
     steps_done = step_count[0].astype(jnp.float32)
     bias_one = 1.0 - jnp.power(BETA_ONE, steps_done)

time: 569 us -> 565 us (level)
    all_to_all x4 -> x3, starting transfers between devices: 11.4 us -> 8.9 us  [everyone(): lax.all_to_all(jnp.broadcast_to(block, (count, block.shape[1])), ALL, 0,...]
    all_to_all x4 -> x3, waiting for transfers between devices: 19.2 us -> 18.2 us  [everyone(): lax.all_to_all(jnp.broadcast_to(block, (count, block.shape[1])), ALL, 0,...]
    unnamed x247 -> x244, local copies, waits for them, and re-layouts: 15.3 us -> 14.5 us
  transfers between devices with their start and end apart: 26 -> 25, of which waited for: 19 -> 18; matrix products, arithmetic and copies ran while one was open for 23% -> 22% of each run, Pallas kernels for 0% -> 0%
where the time goes in v6:
time: 565 us; the launch traced here: 555 us
  waiting for transfers between devices  242 us (43%)
  matrix products  99.1 us (18%)
  other arithmetic  76.7 us (14%)
  local copies, waits for them, and re-layouts  64.4 us (11%)
  starting transfers between devices  42.5 us (8%)
  between operations  23.7 us (4%)
  Pallas kernels  6.8 us (1%)
    dot_general x34, matrix products, einsum(): return jnp.einsum(form, left, right, preferred_element_type=jnp.float32)  94.4 us
    all_to_all x1, waiting for transfers between devices, fetch(): lax.all_to_all(rows.reshape(count, room, 2 * D), ALL, 0, 0, tiled=True)  84.5 us
    all_gather x2, waiting for transfers between devices, gathered(): full = lax.all_gather(block, ALL, axis=0, tiled=True)  80.6 us
    ppermute x15, waiting for transfers between devices, owned(): lax.ppermute(send, axis, [(index, index ^ 1 << bit) for index in range(si...  44.7 us
    all_to_all x3, waiting for transfers between devices, everyone(): lax.all_to_all(jnp.broadcast_to(block, (count, block.shape[1])), ALL, 0,...  18.2 us
    sub x5, other arithmetic, adam_update(): master - LEARN_RATE * (direction + DECAY_RATE * master)  16.9 us
    unnamed x244, local copies, waits for them, and re-layouts  14.5 us
    convert_element_type x12, other arithmetic, owned(): block = block.astype(LOW)  12.8 us
  transfers between devices with their start and end apart: 25, of which 18 were waited for; matrix products, arithmetic and copies ran while one was open for 22% of the time, Pallas kernels for 0%

profile of v6, /device:TPU:0, one launch (start us, length us, event | category | flops | bytes accessed | tf_op | source)
XLA Modules:
  0.0 554.8 jit_solution(16046820762037863320)
XLA Ops:
  19.8 7.3 %all-to-all-start.4 = ((f32[32,1,33]{2,1,0:T(1,128)}), f32[32,1,33]{2,1,0:T(1,128)S(1)}, u32[]{:S(2)}, u32[]{:S(2)}) async-start(f32[32,1,33]{2,1,0:T(1,128)} %bitcast.17), calls=%async_computation.4 | async-start | bytes 32768 | tf_op jit(solution)/shard_map/all_to_all | solution.py:318
  34.5 8.3 %fusion.35 = bf16[768,1536]{1,0:T(8,128)(2,1)} fusion(bf16[1572,1536]{1,0:T(8,128)(2,1)} %pad_maximum_fusion, s32[768]{0:T(1024)S(1)} %eq.255), kind=kOutput, calls=%fused_computation.67 | convolution fusion | flops 3711200256 | bytes 7191552 | tf_op jit(solution)/shard_map/sv,vd->sd/dot_general | solution.py:31
  42.8 4.5 all-to-all-start.5
  50.8 84.5 %all-to-all-done.5 = bf16[32,24,1536]{2,1,0:T(8,128)(2,1)S(1)} async-done(((bf16[32,24,1536]{2,1,0:T(8,128)(2,1)}), bf16[32,24,1536]{2,1,0:T(8,128)(2,1)S(1)}, u32[]{:S(2)}, u32[]{:S(2)}) %all-to-all-start.5) | async-done | bytes 2359328 | tf_op jit(solution)/shard_map/all_to_all | solution.py:297
  141.6 5.8 %fusion.186 = f32[256,4,1536]{2,0,1:T(8,128)S(1)} fusion(bf16[4,768,1536]{2,1,0:T(8,128)(2,1)} %bitcast.410, f32[768]{0:T(1024)S(1)} %get-tuple-element.465, f32[768]{0:T(1024)S(1)} %get-tuple-element.580, f32[256,1536]{1,0:T(8,128)} %get-tuple-element.762, f32[256]{0:T(256)S(1)} %add_rsqrt_fusion.2, f32[256]{0:T(256)S(1)} %broadcast_multiply_fusion.14), kind=kOutput, calls=%fused_computation.331 | convolution fusion | flops 2416902144 | bytes 16523264 | tf_op jit(solution)/shard_map/td,hde->the/dot_general | solution.py:31
  176.9 80.6 %all-gather.5.cloned.1.call-done = bf16[3072,3072]{1,0:T(8,128)(2,1)} async-done(((bf16[96,3072]{1,0:T(8,128)(2,1)}), bf16[3072,3072]{1,0:T(8,128)(2,1)}) %all-gather.5.cloned.1.call-update) | async-done | bytes 18874384 | tf_op jit(solution)/shard_map/all_gather | solution.py:244
  257.5 4.5 fusion.133
  262.0 7.6 %fusion.38 = bf16[256,4,768]{2,0,1:T(8,128)(2,1)S(1)} fusion(f32[256,4,768]{2,0,1:T(8,128)S(1)} %get-tuple-element.565, u8[256,768]{1,0:T(8,128)(4,1)S(1)} %get-tuple-element.425, u8[256,768]{1,0:T(8,128)(4,1)S(1)} %get-tuple-element.424), kind=kLoop, calls=%fused_computation.70 | loop fusion | flops 55050240 | bytes 5111808 | tf_op jit(solution)/shard_map/convert_element_type | solution.py:389
  276.8 10.3 %fusion.211 = (f32[256]{0:T(256)S(1)}, f32[256]{0:T(256)S(1)}, f32[256,768]{1,0:T(8,128)}) fusion(f32[256]{0:T(256)S(1)} %add_rsqrt_fusion, f32[256,768]{1,0:T(8,128)S(1)} %get-tuple-element.567, f32[256]{0:T(256)S(1)} %broadcast_multiply_fusion.12, f32[256,768]{1,0:T(8,128)} %fusion.86, bf16[4,768,3072]{2,1,0:T(8,128)(2,1)} %bitcast.490, ...), kind=kOutput, calls=%fused_computation.408 | convolution fusion | flops 2430074368 | bytes 21270528 | tf_op jit(solution)/shard_map/the,hde->td/dot_general | solution.py:31
  295.2 7.0 %all-to-all-done.6 = bf16[32,2,768]{2,1,0:T(2,128)(2,1)S(1)} async-done(((bf16[32,2,768]{2,1,0:T(2,128)(2,1)}), bf16[32,2,768]{2,1,0:T(2,128)(2,1)S(1)}, u32[]{:S(2)}, u32[]{:S(2)}) %all-to-all-start.6) | async-done | bytes 98336 | tf_op jit(solution)/shard_map/all_to_all | solution.py:65
  303.7 4.8 select_reduce_fusion.7
  319.7 5.9 %all-to-all-done.7 = f32[32,1,512]{2,1,0:T(1,128)} async-done(((f32[32,1,512]{2,1,0:T(1,128)}), f32[32,1,512]{2,1,0:T(1,128)}, u32[]{:S(2)}, u32[]{:S(2)}) %all-to-all-start.7) | async-done | bytes 65568 | tf_op jit(solution)/shard_map/all_to_all | solution.py:65
  327.0 6.8 %shard_map.498 = (f32[4,32]{1,0:T(4,128)}, f32[1,32]{1,0:T(1,128)}, f32[1,1]{1,0:T(1,128)}) custom-call(f32[32,512]{1,0:T(8,128)} %bitcast.456, bf16[32,768]{1,0:T(8,128)(2,1)} %slice.235.feat_ref, f32[4,32]{1,0:T(4,128)} %slice_bitcast_fusion.9.targets_ref), custom_call_target="tpu_custom_call" | custom-call | tf_op jit(solution)/shard_map/pallas_call | solution.py:155
  351.1 5.4 convolution_convert_fusion.1
  391.5 4.3 constant_dynamic-slice_fusion.1
  406.5 6.6 %copy.273 = bf16[4,768,768]{2,1,0:T(8,128)(2,1)} copy(bf16[4,768,768]{1,2,0:T(8,128)(2,1)} %pad_maximum_fusion.1) | data formatting | bytes 9437184 | tf_op jit(solution)/shard_map/concatenate | solution.py:462
  417.2 4.7 all-to-all-done.10
  440.3 4.4 multiply_reduce_fusion
  444.7 11.2 %collective-permute-done.11 = bf16[2,2,2,96,768]{4,3,0,2,1:T(8,128)(2,1)} collective-permute-done((bf16[2,2,2,96,768]{4,3,0,2,1:T(8,128)(2,1)}, bf16[2,2,2,96,768]{4,3,0,2,1:T(8,128)(2,1)}, u32[]{:S(2)}, u32[]{:S(2)}) %collective-permute-start.11) | collective-permute-done | bytes 1179680 | tf_op jit(solution)/shard_map/ppermute | solution.py:92
  468.5 4.8 collective-permute-done.12
  474.4 4.5 collective-permute-done.7
  494.1 11.8 %collective-permute-done.4 = bf16[96,768]{1,0:T(8,128)(2,1)S(1)} collective-permute-done((bf16[96,768]{1,0:T(8,128)(2,1)S(1)}, bf16[96,768]{1,0:T(8,128)(2,1)S(1)}, u32[]{:S(2)}, u32[]{:S(2)}) %collective-permute-start.4) | collective-permute-done | bytes 147488 | tf_op jit(solution)/shard_map/ppermute | solution.py:92
  516.5 5.3 all-to-all-done.11
  530.8 13.5 %multiply_subtract_fusion = (f32[1572,768]{1,0:T(8,128)}, f32[1572,768]{1,0:T(8,128)}, f32[1572,768]{1,0:T(8,128)}) fusion(f32[1572,768]{1,0:T(8,128)} %param.51, f32[]{:T(128)} %bitcast.139, f32[]{:T(128)} %bitcast.138, f32[1572,768]{1,0:T(8,128)} %get-tuple-element.763, f32[]{:T(128)S(6)} %min.3, f32[1572,768]{1,0:T(8,128)} %param.53, f32[1572,768]{1,0:T(8,128)} %param.52), kind=kLoop, calls=%fused_computation.33 | loop fusion | flops 19316736 | bytes 33804300 | tf_op jit(solution)/shard_map/sub | solution.py:175
  (473 shorter events, 216.9 us)
Async XLA Ops:
  7.2 134.4 %all-gather.3.cloned.1.call-start = ((), (), s32[]{:S(2)}) async-start(), calls=%async_computation.12 | async-start | bytes 9732096 | tf_op jit(solution)/shard_map/all_gather | solution.py:244
  12.1 245.4 %all-gather.5.cloned.1.call-start = ((), (), s32[]{:S(2)}) async-start(), calls=%async_computation.13 | async-start | bytes 19464192 | tf_op jit(solution)/shard_map/all_gather | solution.py:244
  19.8 14.4 %all-to-all-start.4 = ((f32[32,1,33]{2,1,0:T(1,128)}), f32[32,1,33]{2,1,0:T(1,128)S(1)}, u32[]{:S(2)}, u32[]{:S(2)}) async-start(f32[32,1,33]{2,1,0:T(1,128)} %bitcast.17), calls=%async_computation.4 | async-start | bytes 32768 | tf_op jit(solution)/shard_map/all_to_all | solution.py:318
  42.8 92.4 %all-to-all-start.5 = ((bf16[32,24,1536]{2,1,0:T(8,128)(2,1)}), bf16[32,24,1536]{2,1,0:T(8,128)(2,1)S(1)}, u32[]{:S(2)}, u32[]{:S(2)}) async-start(bf16[32,24,1536]{2,1,0:T(8,128)(2,1)} %bitcast.429), calls=%async_computation.5 | async-start | bytes 4718592 | tf_op jit(solution)/shard_map/all_to_all | solution.py:297
  291.7 10.5 %all-to-all-start.6 = ((bf16[32,2,768]{2,1,0:T(2,128)(2,1)}), bf16[32,2,768]{2,1,0:T(2,128)(2,1)S(1)}, u32[]{:S(2)}, u32[]{:S(2)}) async-start(bf16[32,2,768]{2,1,0:T(2,128)(2,1)} %reshape.593), calls=%async_computation.6 | async-start | bytes 196608 | tf_op jit(solution)/shard_map/all_to_all | solution.py:65
  315.0 10.6 %all-to-all-start.7 = ((f32[32,1,512]{2,1,0:T(1,128)}), f32[32,1,512]{2,1,0:T(1,128)}, u32[]{:S(2)}, u32[]{:S(2)}) async-start(f32[32,1,512]{2,1,0:T(1,128)} %broadcast_in_dim.271), calls=%async_computation.7 | async-start | bytes 131072 | tf_op jit(solution)/shard_map/all_to_all | solution.py:65
  338.6 11.0 %all-to-all-start.8 = ((f32[32,1,768]{2,1,0:T(1,128)}), f32[32,1,768]{2,1,0:T(1,128)}, u32[]{:S(2)}, u32[]{:S(2)}) async-start(f32[32,1,768]{2,1,0:T(1,128)} %copy.267), calls=%async_computation.8 | async-start | bytes 196608 | tf_op jit(solution)/shard_map/all_to_all | solution.py:428
  378.7 10.2 %all-to-all-start.9 = ((f32[32,1,144]{2,1,0:T(1,128)}), f32[32,1,144]{2,1,0:T(1,128)S(1)}, u32[]{:S(2)}, u32[]{:S(2)}) async-start(f32[32,1,144]{2,1,0:T(1,128)} %all_to_all.79), calls=%async_computation.9 | async-start | bytes 65536 | tf_op jit(solution)/shard_map/all_to_all | solution.py:475
  388.9 33.0 %all-to-all-start.10 = ((bf16[32,24,768]{2,1,0:T(8,128)(2,1)}), bf16[32,24,768]{2,1,0:T(8,128)(2,1)S(1)}, u32[]{:S(2)}, u32[]{:S(2)}) async-start(bf16[32,24,768]{2,1,0:T(8,128)(2,1)} %bitcast.94), calls=%async_computation.10 | async-start | bytes 2359296 | tf_op jit(solution)/shard_map/all_to_all | solution.py:302
  397.3 26.9 %collective-permute-start.10 = (bf16[2,2,2,2,96,768]{5,4,1,3,2,0:T(8,128)(2,1)}, bf16[2,2,2,2,96,768]{5,4,1,3,2,0:T(8,128)(2,1)}, u32[]{:S(2)}, u32[]{:S(2)}) collective-permute-start(bf16[2,2,2,2,96,768]{5,4,1,3,2,0:T(8,128)(2,1)} %bitcast.374), channel_id=1, source_target_pairs={{0,1},{1,0},{2,3},{3,2},{4,5},{5,4},{6,7},{7,6},{8,9},{9,8},{10,11... | collective-permute-start | bytes 7077896 | tf_op jit(solution)/shard_map/ppermute | solution.py:92
  400.8 27.8 %collective-permute-start.5 = (bf16[2,2,2,2,96,768]{5,4,1,0,3,2:T(8,128)(2,1)}, bf16[2,2,2,2,96,768]{5,4,1,0,3,2:T(8,128)(2,1)}, u32[]{:S(2)}, u32[]{:S(2)}) collective-permute-start(bf16[2,2,2,2,96,768]{5,4,1,0,3,2:T(8,128)(2,1)} %bitcast.375), channel_id=1, source_target_pairs={{0,1},{1,0},{2,3},{3,2},{4,5},{5,4},{6,7},{7,6},{8,9},{9,8},{10,11... | collective-permute-start | bytes 7077896 | tf_op jit(solution)/shard_map/ppermute | solution.py:92
  416.4 16.2 %collective-permute-start = (bf16[2,2,2,2,96,768]{5,4,3,2,1,0:T(8,128)(2,1)}, bf16[2,2,2,2,96,768]{5,4,3,2,1,0:T(8,128)(2,1)}, u32[]{:S(2)}, u32[]{:S(2)}) collective-permute-start(bf16[2,2,2,2,96,768]{5,4,3,2,1,0:T(8,128)(2,1)} %dynamic-slice_bitcast_fusion), channel_id=1, source_target_pairs={{0,1},{1,0},{2,3},{3,2},{4,5},{5,4},{6,7},{7,6},{8,9},{9,8},{10,11... | collective-permute-start | bytes 7077896 | tf_op jit(solution)/shard_map/ppermute | solution.py:92
  428.0 27.9 %collective-permute-start.11 = (bf16[2,2,2,96,768]{4,3,0,2,1:T(8,128)(2,1)}, bf16[2,2,2,96,768]{4,3,0,2,1:T(8,128)(2,1)}, u32[]{:S(2)}, u32[]{:S(2)}) collective-permute-start(bf16[2,2,2,96,768]{4,3,0,2,1:T(8,128)(2,1)} %dynamic-slice_bitcast_fusion.1), channel_id=1, source_target_pairs={{0,2},{1,3},{2,0},{3,1},{4,6},{5,7},{6,4},{7,5},{8,10},{9,11},{10,... | collective-permute-start | bytes 3538952 | tf_op jit(solution)/shard_map/ppermute | solution.py:92
  432.4 29.2 %collective-permute-start.6 = (bf16[2,2,2,96,768]{4,3,1,0,2:T(8,128)(2,1)}, bf16[2,2,2,96,768]{4,3,1,0,2:T(8,128)(2,1)}, u32[]{:S(2)}, u32[]{:S(2)}) collective-permute-start(bf16[2,2,2,96,768]{4,3,1,0,2:T(8,128)(2,1)} %dynamic-slice_bitcast_fusion.2), channel_id=1, source_target_pairs={{0,8},{4,12},{8,0},{12,4},{16,24},{20,28},{24,16},{28,20},{1,9},{5... | collective-permute-start | bytes 3538952 | tf_op jit(solution)/shard_map/ppermute | solution.py:92
  436.2 28.6 %collective-permute-start.1 = (bf16[2,2,2,96,768]{4,3,2,1,0:T(8,128)(2,1)}, bf16[2,2,2,96,768]{4,3,2,1,0:T(8,128)(2,1)}, u32[]{:S(2)}, u32[]{:S(2)}) collective-permute-start(bf16[2,2,2,96,768]{4,3,2,1,0:T(8,128)(2,1)} %dynamic-slice_bitcast_fusion.3), channel_id=1, source_target_pairs={{0,4},{4,0},{8,12},{12,8},{16,20},{20,16},{24,28},{28,24},{1,5},{5... | collective-permute-start | bytes 3538952 | tf_op jit(solution)/shard_map/ppermute | solution.py:92
  457.5 15.8 %collective-permute-start.12 = (bf16[2,2,96,768]{3,2,0,1:T(8,128)(2,1)S(1)}, bf16[2,2,96,768]{3,2,0,1:T(8,128)(2,1)S(1)}, u32[]{:S(2)}, u32[]{:S(2)}) collective-permute-start(bf16[2,2,96,768]{3,2,0,1:T(8,128)(2,1)S(1)} %dynamic-slice_bitcast_fusion.4), channel_id=1, source_target_pairs={{0,8},{4,12},{8,0},{12,4},{16,24},{20,28},{24,16},{28,20},{1,9},{5... | collective-permute-start | bytes 1769480 | tf_op jit(solution)/shard_map/ppermute | solution.py:92
  463.3 15.6 %collective-permute-start.7 = (bf16[2,2,96,768]{3,2,1,0:T(8,128)(2,1)S(1)}, bf16[2,2,96,768]{3,2,1,0:T(8,128)(2,1)S(1)}, u32[]{:S(2)}, u32[]{:S(2)}) collective-permute-start(bf16[2,2,96,768]{3,2,1,0:T(8,128)(2,1)S(1)} %dynamic-slice_bitcast_fusion.5), channel_id=1, source_target_pairs={{0,4},{4,0},{8,12},{12,8},{16,20},{20,16},{24,28},{28,24},{1,5},{5... | collective-permute-start | bytes 1769480 | tf_op jit(solution)/shard_map/ppermute | solution.py:92
  466.4 16.3 %collective-permute-start.2 = (bf16[2,2,96,768]{3,2,1,0:T(8,128)(2,1)S(1)}, bf16[2,2,96,768]{3,2,1,0:T(8,128)(2,1)S(1)}, u32[]{:S(2)}, u32[]{:S(2)}) collective-permute-start(bf16[2,2,96,768]{3,2,1,0:T(8,128)(2,1)S(1)} %dynamic-slice_bitcast_fusion.6), channel_id=1, source_target_pairs={{0,2},{1,3},{2,0},{3,1},{4,6},{5,7},{6,4},{7,5},{8,10},{9,11},{10,... | collective-permute-start | bytes 1769480 | tf_op jit(solution)/shard_map/ppermute | solution.py:92
  473.5 17.6 %collective-permute-start.13 = (bf16[2,96,768]{2,1,0:T(8,128)(2,1)S(1)}, bf16[2,96,768]{2,1,0:T(8,128)(2,1)S(1)}, u32[]{:S(2)}, u32[]{:S(2)}) collective-permute-start(bf16[2,96,768]{2,1,0:T(8,128)(2,1)S(1)} %dynamic-slice_bitcast_fusion.7), channel_id=1, source_target_pairs={{0,4},{4,0},{8,12},{12,8},{16,20},{20,16},{24,28},{28,24},{1,5},{5... | collective-permute-start | bytes 884744 | tf_op jit(solution)/shard_map/ppermute | solution.py:92
  479.1 8.0 %collective-permute-start.8 = (bf16[2,96,768]{2,1,0:T(8,128)(2,1)S(1)}, bf16[2,96,768]{2,1,0:T(8,128)(2,1)S(1)}, u32[]{:S(2)}, u32[]{:S(2)}) collective-permute-start(bf16[2,96,768]{2,1,0:T(8,128)(2,1)S(1)} %dynamic-slice_bitcast_fusion.8), channel_id=1, source_target_pairs={{0,2},{1,3},{2,0},{3,1},{4,6},{5,7},{6,4},{7,5},{8,10},{9,11},{10,... | collective-permute-start | bytes 884744 | tf_op jit(solution)/shard_map/ppermute | solution.py:92
  487.2 20.7 %collective-permute-start.9 = (bf16[96,768]{1,0:T(8,128)(2,1)S(1)}, bf16[96,768]{1,0:T(8,128)(2,1)S(1)}, u32[]{:S(2)}, u32[]{:S(2)}) collective-permute-start(bf16[96,768]{1,0:T(8,128)(2,1)S(1)} %dynamic-slice_bitcast_fusion.11), channel_id=1, source_target_pairs={{0,16},{4,20},{8,24},{12,28},{16,0},{20,4},{24,8},{28,12},{1,17},{... | collective-permute-start | bytes 442376 | tf_op jit(solution)/shard_map/ppermute | solution.py:92
  490.9 15.0 %collective-permute-start.4 = (bf16[96,768]{1,0:T(8,128)(2,1)S(1)}, bf16[96,768]{1,0:T(8,128)(2,1)S(1)}, u32[]{:S(2)}, u32[]{:S(2)}) collective-permute-start(bf16[96,768]{1,0:T(8,128)(2,1)S(1)} %dynamic-slice_bitcast_fusion.12), channel_id=1, source_target_pairs={{0,16},{4,20},{8,24},{12,28},{16,0},{20,4},{24,8},{28,12},{1,17},{... | collective-permute-start | bytes 442376 | tf_op jit(solution)/shard_map/ppermute | solution.py:92
  491.2 18.1 %collective-permute-start.14 = (bf16[96,768]{1,0:T(8,128)(2,1)S(1)}, bf16[96,768]{1,0:T(8,128)(2,1)S(1)}, u32[]{:S(2)}, u32[]{:S(2)}) collective-permute-start(bf16[96,768]{1,0:T(8,128)(2,1)S(1)} %dynamic-slice_bitcast_fusion.10), channel_id=1, source_target_pairs={{0,16},{4,20},{8,24},{12,28},{16,0},{20,4},{24,8},{28,12},{1,17},{... | collective-permute-start | bytes 442376 | tf_op jit(solution)/shard_map/ppermute | solution.py:92
  511.9 9.8 %all-to-all-start.11 = ((f32[32,1,272]{2,1,0:T(1,128)}), f32[32,1,272]{2,1,0:T(1,128)S(1)}, u32[]{:S(2)}, u32[]{:S(2)}) async-start(f32[32,1,272]{2,1,0:T(1,128)} %broadcast_in_dim.282), calls=%async_computation.11 | async-start | bytes 98304 | tf_op jit(solution)/shard_map/all_to_all | solution.py:65
  (116 other events, 2807.6 us)
Sparse Core Ops, SparseCore 0:
  12.2 121.0 all-gather.2
  136.2 121.2 all-gather.4
